TPU v7x, 256 devices: a whole 4x4x8 slice. The times are simulated.
256 devices in a mesh: dir: 4 (over x_lo, core), tb: 64 (over z, y, x_hi).
Axes of the slice: x: 4 (x_hi: 2, x_lo: 2; x = x_hi * 2 + x_lo), y: 4, z: 8, core: 2. Of those that a mesh axis runs over, the one named last changes fastest.
Arguments:
- visibilities: bfloat16 [65536, 128], P('tb'), may hold values from -6 to 6
- uv_coords: bfloat16 [2, 65536], P(None, 'tb'), may hold values from -32 to 32
- comp_lm: float32 [2, 12288], P(None, 'dir'), may hold values from -0.25 to 0.25
- spectra: bfloat16 [2, 12288, 128], P(None, 'dir'), may hold values from -0.1875 to 0.1875
- ridge_weight: float32 [128], replicated, may hold values from 32 to 512
- assignment: int32 [12288], P('dir'), may hold values from 0 to 3071, as said below
- peel_order: int32 [12], P('dir'), may hold values from 0 to 2, as said below
- block_tile: int32 [2048, 1], P('tb'), may hold values from 0 to 63; in each aligned block of 32 rows (0 to 31, 32 to 63, ...) at most 2 rows name the same one
Outputs:
- residual: bfloat16 [65536, 128], P('tb')
- subgrids: float32 [64, 2, 1024, 128], P('tb', None, 'dir')
Inputs may be any that keep to these rules, and one draw needn't show every extreme that they name: `assignment`: each owner's 3 * 1024 entries are a permutation of its local component numbers. `peel_order`: each owner's 3 entries are a permutation of its directions. `block_tile`: among the 32 blocks of one index of tb no tile is named more than 2 times; every tile is named by some block of the whole array.
All inputs are finite; a program needn't handle non-finite values.
Results may differ from a plain program's by a relative error of at most 0.0064.
Values may be sent and summed in bfloat16 or wider, within the bound.
No kernel may reach another device: no remote copies, remote signals or barrier semaphores. Data moves between devices by JAX's collectives and lax.ppermute only.
A program may use at most 64 MiB of HBM per device.

v0:
```python
import jax
import jax.numpy as jnp
from jax import lax
from jax.experimental import pallas as pl
from jax.experimental.pallas import tpu as pltpu
from jax.sharding import PartitionSpec as P

NCOMP = 1024
GRID = 32
DIR_DEV = 3
ITERS = 4
BB = 32
GB = 128
ROWS_DEV = 1024
PIX = 1024
COLS = 128
N_DIR = 4
N_TB = 64
NB = 32
SLOTS = 2
QROWS = ROWS_DEV // N_DIR
HALF = BB // 2
POOL = DIR_DEV * NCOMP
WIDE = DIR_DEV * COLS
CHUNK = 256
NCHUNK = POOL // CHUNK
SEND_ROWS = SLOTS * HALF + 8

F32 = jnp.float32
BF16 = jnp.bfloat16

SIN_C = (2.6417407853784525, -1.0859537956447276, 0.1306204657138272)
COS_C = (1.681792784129167, -2.074822793580374, 0.42650038149094444, -0.03432262097868313)
ROOT2 = 1.4142135623730951


def vmem():
    return pl.BlockSpec(memory_space=pltpu.VMEM)


def smem():
    return pl.BlockSpec(memory_space=pltpu.SMEM)


def params(mib):
    return pltpu.CompilerParams(vmem_limit_bytes=mib << 20)


def cos_sin_turns(turns):
    r = turns - jnp.round(turns)
    z = r * r
    s = ((SIN_C[2] * z + SIN_C[1]) * z + SIN_C[0]) * r
    c = ((COS_C[3] * z + COS_C[2]) * z + COS_C[1]) * z + COS_C[0]
    s1 = s * c
    c1 = ROOT2 - s * s
    return 1.0 - s1 * s1, s1 * c1


def three_parts(value):
    high = value.astype(BF16)
    left = value - high.astype(F32)
    mid = left.astype(BF16)
    low = (left - mid.astype(F32)).astype(BF16)
    return high, mid, low


def prepare_kernel(order_ref, assign_ref, lm_ref, uv_ref, spec_ref, lm8_ref, uv8_ref, wide_ref, pos_ref):
    lh, lmid, ll = three_parts(lm_ref[...])
    zero = jnp.zeros((2, POOL), BF16)
    lm8_ref[...] = jnp.concatenate(
        [lh[0:1], lmid[0:1], ll[0:1], lh[1:2], lmid[1:2], ll[1:2], zero], axis=0
    )
    for q in range(N_DIR):
        u = uv_ref[0:1, q * QROWS : (q + 1) * QROWS]
        v = uv_ref[1:2, q * QROWS : (q + 1) * QROWS]
        uv8_ref[q] = jnp.concatenate([u, u, u, v, v, v, jnp.zeros((2, QROWS), BF16)], axis=0)
    assign = assign_ref[...]
    low = assign & 127
    high = assign >> 7
    segment = lax.broadcasted_iota(jnp.int32, (1, POOL), 1) // NCOMP
    place = jnp.zeros((1, POOL), F32)
    for p in range(DIR_DEV):
        place = jnp.where(segment == order_ref[p], float(p), place)
    low_hot = (lax.broadcasted_iota(jnp.int32, (128, POOL), 0) == low).astype(F32).astype(BF16)
    high_hot = jnp.where(lax.broadcasted_iota(jnp.int32, (32, POOL), 0) == high, place, 0.0).astype(BF16)
    pos_ref[...] = lax.dot_general(
        low_hot, high_hot, (((1,), (1,)), ((), ())), preferred_element_type=F32
    )

    def mask_chunk(j, carry):
        for h in range(CHUNK // 128):
            column = 2 * j + h
            pick = (lax.broadcasted_iota(jnp.int32, (32, 128), 0) == column).astype(F32).astype(BF16)
            place_here = jnp.dot(pos_ref[...].astype(BF16), pick, preferred_element_type=F32)
            for part in range(2):
                rows = spec_ref[part, pl.ds(pl.multiple_of(column * 128, 128), 128), :].astype(F32)
                for p in range(DIR_DEV):
                    kept = jnp.where(place_here == float(p), rows, 0.0).astype(BF16)
                    first = part * CHUNK + h * 128
                    wide_ref[j, first : first + 128, p * COLS : (p + 1) * COLS] = kept
        return carry

    lax.fori_loop(0, NCHUNK, mask_chunk, 0)


def prepare(peel_order, assignment, comp_lm, uv_coords, spectra):
    return pl.pallas_call(
        prepare_kernel,
        out_shape=(
            jax.ShapeDtypeStruct((8, POOL), BF16),
            jax.ShapeDtypeStruct((N_DIR, 8, QROWS), BF16),
            jax.ShapeDtypeStruct((NCHUNK, 2 * CHUNK, WIDE), BF16),
        ),
        in_specs=[smem(), vmem(), vmem(), vmem(), vmem()],
        out_specs=(vmem(), vmem(), vmem()),
        scratch_shapes=[pltpu.VMEM((128, 32), F32)],
        compiler_params=params(16),
        name="prepare",
    )(peel_order, assignment.reshape(1, POOL), comp_lm, uv_coords, spectra)


def predict_kernel(flips, ids_ref, uv8_ref, lm8_ref, wide_ref, *rest):
    out_refs = rest[: len(flips)]
    tab_a, tab_b, acc_ref = rest[len(flips) :]
    me = ids_ref[0]
    uv_rows = jnp.concatenate([uv8_ref[me ^ x].astype(F32).T for x in flips], axis=0).astype(BF16)

    def table(j, tab_ref):
        lm = lm8_ref[:, pl.ds(pl.multiple_of(j * CHUNK, CHUNK), CHUNK)]
        turns = jnp.dot(uv_rows, lm, preferred_element_type=F32)
        cos, sin = cos_sin_turns(turns)
        tab_ref[:, :CHUNK] = cos.astype(BF16)
        tab_ref[:, CHUNK:] = sin.astype(BF16)

    def gather(j, tab_ref):
        acc_ref[...] += jnp.dot(tab_ref[...], wide_ref[j], preferred_element_type=F32)

    acc_ref[...] = jnp.zeros(acc_ref.shape, F32)
    table(0, tab_a)

    def step(i, carry):
        gather(2 * i, tab_a)
        table(2 * i + 1, tab_b)
        gather(2 * i + 1, tab_b)
        table(jnp.minimum(2 * i + 2, NCHUNK - 1), tab_a)
        return carry

    lax.fori_loop(0, NCHUNK // 2 - 1, step, 0)
    table(NCHUNK - 1, tab_b)
    gather(NCHUNK - 2, tab_a)
    gather(NCHUNK - 1, tab_b)
    for n in range(len(flips)):
        for p in range(DIR_DEV):
            out_refs[n][p] = acc_ref[n * QROWS : (n + 1) * QROWS, p * COLS : (p + 1) * COLS].astype(BF16)


def predict(flips, ids, uv8, lm8, wide):
    rows = QROWS * len(flips)

    def kernel(*refs):
        predict_kernel(flips, *refs)

    return pl.pallas_call(
        kernel,
        out_shape=tuple(jax.ShapeDtypeStruct((DIR_DEV, QROWS, COLS), BF16) for _ in flips),
        in_specs=[smem(), vmem(), vmem(), vmem()],
        out_specs=tuple(vmem() for _ in flips),
        scratch_shapes=[
            pltpu.VMEM((rows, 2 * CHUNK), BF16),
            pltpu.VMEM((rows, 2 * CHUNK), BF16),
            pltpu.VMEM((rows, WIDE), F32),
        ],
        compiler_params=params(16),
        name="predict",
    )(ids, uv8, lm8, wide)


def per_block_sum(value):
    return jnp.sum(value.reshape(QROWS // GB, GB, COLS), axis=1)


def peel_kernel(ids_ref, vis_ref, ridge_ref, m0_ref, m1_ref, m2_ref, m3_ref, out_ref, model_ref, inv_ref):
    me = ids_ref[0]
    ridge = ridge_ref[...]
    for x, ref in enumerate((m0_ref, m1_ref, m2_ref, m3_ref)):
        owner = me ^ x
        for p in range(DIR_DEV):
            model = ref[p].astype(F32)
            model_ref[owner * DIR_DEV + p] = model
            inv_ref[owner * DIR_DEV + p] = 1.0 / (per_block_sum(model * model) + ridge)
    lane = lax.broadcasted_iota(jnp.int32, (QROWS // GB, COLS), 1)

    def neighbours(gain):
        lower = jnp.where(lane < 2, gain, pltpu.roll(gain, 2, 1))
        upper = jnp.where(lane >= COLS - 2, gain, pltpu.roll(gain, COLS - 2, 1))
        return 0.5 * (lower + upper)

    remains = vis_ref[pl.ds(pl.multiple_of(me * QROWS, QROWS), QROWS), :].astype(F32)
    for j in range(N_DIR * DIR_DEV):
        model = model_ref[j]
        inv = inv_ref[j]
        cross = per_block_sum(remains * model) * inv
        pull = ridge * inv
        gain = cross + pull
        for _ in range(ITERS - 1):
            gain = cross + pull * neighbours(gain)
        spread = jnp.concatenate(
            [jnp.broadcast_to(gain[b : b + 1], (GB, COLS)) for b in range(QROWS // GB)], axis=0
        )
        remains = remains - spread * model
        if (j + 1) % DIR_DEV == 0:
            remains = remains.astype(BF16).astype(F32)
    out_ref[...] = remains.astype(BF16)


def peel(ids, visibilities, ridge_weight, models):
    return pl.pallas_call(
        peel_kernel,
        out_shape=jax.ShapeDtypeStruct((QROWS, COLS), BF16),
        in_specs=[smem()] + [vmem()] * 6,
        out_specs=vmem(),
        scratch_shapes=[
            pltpu.VMEM((N_DIR * DIR_DEV, QROWS, COLS), F32),
            pltpu.VMEM((N_DIR * DIR_DEV, QROWS // GB, COLS), F32),
        ],
        compiler_params=params(16),
        name="peel",
    )(ids, visibilities, ridge_weight.reshape(1, COLS), *models)


def label_kernel(ids_ref, tile_ref, uv_ref, out_ref):
    half = ids_ref[1]
    offset = ids_ref[2]
    tiles = tile_ref[...].astype(F32)
    block_of_lane = lax.broadcasted_iota(jnp.int32, (NB, ROWS_DEV), 1) // BB
    expand = (block_of_lane == lax.broadcasted_iota(jnp.int32, (NB, ROWS_DEV), 0)).astype(F32)
    tile_of_lane = jnp.sum(expand * tiles, axis=0, keepdims=True)
    sub = lax.broadcasted_iota(jnp.int32, (NB, NB), 0)
    col = lax.broadcasted_iota(jnp.int32, (NB, NB), 1)
    tile_row = jnp.sum(jnp.where(sub == col, tiles, 0.0), axis=0, keepdims=True)
    slot = jnp.sum(jnp.where((tiles == tile_row) & (col < sub), 1.0, 0.0), axis=1, keepdims=True)
    slot_of_row = lax.dot_general(
        expand.astype(BF16),
        jnp.broadcast_to(slot, (NB, COLS)).astype(BF16),
        (((0,), (0,)), ((), ())),
        preferred_element_type=F32,
    )
    within = lax.broadcasted_iota(jnp.int32, (ROWS_DEV, COLS), 0) % BB - half * HALF
    lane = lax.broadcasted_iota(jnp.int32, (ROWS_DEV, COLS), 1)
    goal = slot_of_row.astype(jnp.int32) * HALF + within + offset
    spot = jnp.where((goal == lane) & (within >= 0) & (within < HALF), 1.0, 0.0).astype(BF16)
    row = lax.broadcasted_iota(jnp.int32, (N_TB * 8, ROWS_DEV), 0)
    u = uv_ref[0:1, :].astype(F32)
    v = uv_ref[1:2, :].astype(F32)
    value = jnp.where(row % 8 == 0, u, jnp.where(row % 8 == 1, v, 0.0))
    value = jnp.where((row // 8).astype(F32) == tile_of_lane, value, 0.0).astype(BF16)
    out = jnp.dot(value, spot, preferred_element_type=F32)
    out_ref[...] = out.reshape(N_TB, 8, COLS).astype(BF16)


def label(ids, block_tile, uv_coords):
    return pl.pallas_call(
        label_kernel,
        out_shape=jax.ShapeDtypeStruct((N_TB, 8, COLS), BF16),
        in_specs=[smem(), vmem(), vmem()],
        out_specs=vmem(),
        compiler_params=params(16),
        name="label",
    )(ids, block_tile, uv_coords)


def pack_kernel(ids_ref, tile_ref, r0_ref, r1_ref, r2_ref, r3_ref, coords_ref, out_ref, all_ref, stage_ref, seen_ref):
    me = ids_ref[0]
    half = ids_ref[1]
    for x, ref in enumerate((r0_ref, r1_ref, r2_ref, r3_ref)):
        rows = ref[...]
        all_ref[pl.ds(pl.multiple_of((me ^ x) * QROWS, QROWS), QROWS), :] = rows
        stage_ref[pl.ds((me ^ x) * (2 * QROWS // BB), 2 * QROWS // BB)] = rows.reshape(
            2 * QROWS // BB, HALF, COLS
        )
    out_ref[:, : SLOTS * HALF, :] = jnp.zeros((N_TB, SLOTS * HALF, COLS), BF16)
    out_ref[:, SLOTS * HALF :, :] = coords_ref[...]

    def clear(t, carry):
        seen_ref[t] = 0
        return carry

    lax.fori_loop(0, N_TB, clear, 0)

    def place(b, carry):
        tile = tile_ref[b]
        slot = seen_ref[tile]
        seen_ref[tile] = slot + 1
        out_ref[tile, pl.ds(pl.multiple_of(slot * HALF, HALF), HALF), :] = stage_ref[2 * b + half]
        return carry

    lax.fori_loop(0, NB, place, 0)


def pack(ids, tile_ids, rows, coords):
    return pl.pallas_call(
        pack_kernel,
        out_shape=(
            jax.ShapeDtypeStruct((N_TB, SEND_ROWS, COLS), BF16),
            jax.ShapeDtypeStruct((ROWS_DEV, COLS), BF16),
        ),
        in_specs=[smem(), smem()] + [vmem()] * 5,
        out_specs=(vmem(), vmem()),
        scratch_shapes=[
            pltpu.VMEM((2 * NB, HALF, COLS), BF16),
            pltpu.SMEM((N_TB,), jnp.int32),
        ],
        compiler_params=params(16),
        name="pack",
    )(ids, tile_ids, *rows, coords)


def grid_kernel(ids_ref, got_ref, keep_ref, give_ref, tab_ref):
    chip = ids_ref[0] // 2
    half = ids_ref[1]
    tiles = N_TB * SLOTS * HALF // 128
    groups = N_TB // tiles
    coords = got_ref[:, SLOTS * HALF :, :].astype(F32).reshape(tiles, groups, 8, COLS)
    coords = jnp.sum(coords, axis=1)
    y_pixel = (lax.broadcasted_iota(jnp.int32, (GRID, 1), 0) - GRID // 2).astype(F32)
    order = lax.broadcasted_iota(jnp.int32, (16, 1), 0)
    x_pixel = (16 * chip + 8 * ((order // 8) ^ half) + order % 8 - GRID // 2).astype(F32)
    scale = 1.0 / (2.0 * GRID)
    for tile in range(tiles):
        u = coords[tile, 0:1, :] * scale
        v = coords[tile, 1:2, :] * scale
        cx, sx = cos_sin_turns(x_pixel * u)
        cy, sy = cos_sin_turns(y_pixel * v)
        lanes = slice(tile * 128, (tile + 1) * 128)
        for x in range(16):
            a, b = cx[x : x + 1], sx[x : x + 1]
            tab_ref[x * GRID : (x + 1) * GRID, lanes] = (a * cy - b * sy).astype(BF16)
            tab_ref[512 + x * GRID : 512 + (x + 1) * GRID, lanes] = (b * cy + a * sy).astype(BF16)
    rows = got_ref[:, : SLOTS * HALF, :].reshape(N_TB * SLOTS * HALF, COLS)
    total = jnp.dot(tab_ref[...], rows, preferred_element_type=F32) * float(ROWS_DEV) ** (-0.5)
    for part in range(2):
        keep_ref[part] = total[part * 512 : part * 512 + 256]
        give_ref[part] = total[part * 512 + 256 : part * 512 + 512]


def grid_rows(ids, got):
    return pl.pallas_call(
        grid_kernel,
        out_shape=(
            jax.ShapeDtypeStruct((2, PIX // N_DIR, COLS), F32),
            jax.ShapeDtypeStruct((2, PIX // N_DIR, COLS), F32),
        ),
        in_specs=[smem(), vmem()],
        out_specs=(vmem(), vmem()),
        scratch_shapes=[pltpu.VMEM((1024, N_TB * SLOTS * HALF), BF16)],
        compiler_params=params(24),
        name="grid",
    )(ids, got)


def swap(value, flip):
    return lax.ppermute(value, "dir", [(i, i ^ flip) for i in range(N_DIR)])


def local(
    visibilities, uv_coords, comp_lm, spectra, ridge_weight, assignment, peel_order, block_tile
):
    me = lax.axis_index("dir")
    station = lax.axis_index("tb")
    ids = jnp.stack([me, me % 2, (station % 4) * BB]).astype(jnp.int32)
    lm8, uv8, wide = prepare(peel_order, assignment, comp_lm, uv_coords, spectra)
    (far_a,) = predict((2,), ids, uv8, lm8, wide)
    got_a = swap(far_a, 2)
    (far_b,) = predict((3,), ids, uv8, lm8, wide)
    got_b = swap(far_b, 3)
    near, own = predict((1, 0), ids, uv8, lm8, wide)
    got_near = swap(near, 1)
    rows = peel(ids, visibilities, ridge_weight, (own, got_near, got_a, got_b))
    coords = label(ids, block_tile, uv_coords)
    gathered = (rows, swap(rows, 1), swap(rows, 2), swap(rows, 3))
    send, residual = pack(ids, block_tile[:, 0], gathered, coords)
    got = lax.all_to_all(send, "tb", split_axis=0, concat_axis=0, tiled=True)
    keep, give = grid_rows(ids, got)
    subgrids = (keep + swap(give, 1))[None]
    return residual, subgrids


def solution(mesh):
    return jax.shard_map(
        local,
        mesh=mesh,
        in_specs=(
            P("tb", None),
            P(None, "tb"),
            P(None, "dir"),
            P(None, "dir", None),
            P(),
            P("dir"),
            P("dir"),
            P("tb", None),
        ),
        out_specs=(P("tb", None), P("tb", None, "dir", None)),
        check_vma=False,
    )
```

profile of v0, /device:TPU:1, one launch (start us, length us, event | category | flops | bytes accessed | tf_op | source)
XLA Modules:
  0.0 87.5 jit_solution(2707682439448640469)
XLA Ops:
  0.7 1.4 %copy-done = bf16[2,3072,128]{2,1,0:T(8,128)(2,1)S(1)} copy-done((bf16[2,3072,128]{2,1,0:T(8,128)(2,1)S(1)}, bf16[2,3072,128]{2,1,0:T(8,128)(2,1)}, u32[]{:S(2)}) %copy-start) | copy-done | bytes 1572888
  2.1 0.7 copy-done.2
  2.9 0.7 copy-done.3
  3.6 0.7 copy-done.5
  4.3 0.7 copy-done.8
  4.9 3.4 %prepare.1 = (bf16[8,3072]{1,0:T(8,128)(2,1)S(1)}, bf16[4,8,256]{2,1,0:T(8,128)(2,1)S(1)}, bf16[12,512,384]{2,1,0:T(8,128)(2,1)S(1)}) custom-call(s32[3]{0:T(128)S(1)} %copy-done.8, s32[1,3072]{1,0:T(1,128)S(1)} %bitcast.8, f32[2,3072]{1,0:T(2,128)S(1)} %copy-done.2, bf16[2,1024]{1,0:T(2,128)(2,1)S(1)} %copy-done.3, bf16[2,3072,128]{2,1,0:T(8,128)(2,1)S(1)} %copy-done), custom_call_target="tpu_custom_call" | custom-call | tf_op jit(solution)/shard_map/prepare/pallas_call | solution.py:107
  8.3 5.9 %predict.5 = bf16[3,256,128]{2,1,0:T(8,128)(2,1)S(1)} custom-call(s32[3]{0:T(128)S(1)} %pad_add_fusion.refs_0_.ids_ref, bf16[4,8,256]{2,1,0:T(8,128)(2,1)S(1)} %get-tuple-element.11.refs_1_, bf16[8,3072]{1,0:T(8,128)(2,1)S(1)} %get-tuple-element.12.refs_2_, bf16[12,512,384]{2,1,0:T(8,128)(2,1)S(1)} %get-tuple-element.13.refs_3_), custom_call_target="tpu_custom_call" | custom-call | tf_op jit(solution)/shard_map/predict/pallas_call | solution.py:163
  14.3 2.7 %collective-permute-start.2 = (bf16[3,256,128]{2,1,0:T(8,128)(2,1)S(1)}, bf16[3,256,128]{2,1,0:T(8,128)(2,1)S(1)}, u32[]{:S(2)}, u32[]{:S(2)}) collective-permute-start(bf16[3,256,128]{2,1,0:T(8,128)(2,1)S(1)} %predict.5), channel_id=1, source_target_pairs={{0,192},{64,128},{128,64},{192,0},{1,193},{65,129},{129,65},{193,1... | collective-permute-start | bytes 589832 | tf_op jit(solution)/shard_map/ppermute | solution.py:362
  16.9 5.9 %predict.4 = bf16[3,256,128]{2,1,0:T(8,128)(2,1)S(1)} custom-call(s32[3]{0:T(128)S(1)} %pad_add_fusion.refs_0_.ids_ref, bf16[4,8,256]{2,1,0:T(8,128)(2,1)S(1)} %get-tuple-element.11.refs_1_, bf16[8,3072]{1,0:T(8,128)(2,1)S(1)} %get-tuple-element.12.refs_2_, bf16[12,512,384]{2,1,0:T(8,128)(2,1)S(1)} %get-tuple-element.13.refs_3_), custom_call_target="tpu_custom_call" | custom-call | tf_op jit(solution)/shard_map/predict/pallas_call | solution.py:163
  22.8 2.1 %collective-permute-start.1 = (bf16[3,256,128]{2,1,0:T(8,128)(2,1)S(1)}, bf16[3,256,128]{2,1,0:T(8,128)(2,1)S(1)}, u32[]{:S(2)}, u32[]{:S(2)}) collective-permute-start(bf16[3,256,128]{2,1,0:T(8,128)(2,1)S(1)} %predict.4), channel_id=1, source_target_pairs={{0,128},{64,192},{128,0},{192,64},{1,129},{65,193},{129,1},{193,65... | collective-permute-start | bytes 589832 | tf_op jit(solution)/shard_map/ppermute | solution.py:362
  24.9 9.4 %predict.3 = (bf16[3,256,128]{2,1,0:T(8,128)(2,1)S(1)}, bf16[3,256,128]{2,1,0:T(8,128)(2,1)S(1)}) custom-call(s32[3]{0:T(128)S(1)} %pad_add_fusion.refs_0_.ids_ref, bf16[4,8,256]{2,1,0:T(8,128)(2,1)S(1)} %get-tuple-element.11.refs_1_, bf16[8,3072]{1,0:T(8,128)(2,1)S(1)} %get-tuple-element.12.refs_2_, bf16[12,512,384]{2,1,0:T(8,128)(2,1)S(1)} %get-tuple-element.13.refs_3_), custom_call_target="tpu_custom_call" | custom-call | tf_op jit(solution)/shard_map/predict/pallas_call | solution.py:163
  34.4 1.4 %collective-permute-done.m1_ref = bf16[3,256,128]{2,1,0:T(8,128)(2,1)S(1)} collective-permute-done((bf16[3,256,128]{2,1,0:T(8,128)(2,1)S(1)}, bf16[3,256,128]{2,1,0:T(8,128)(2,1)S(1)}, u32[]{:S(2)}, u32[]{:S(2)}) %collective-permute-start) | collective-permute-done | bytes 196640 | tf_op jit(solution)/shard_map/ppermute | solution.py:362
  35.8 3.7 %peel.1.r0_ref = bf16[256,128]{1,0:T(8,128)(2,1)S(1)} custom-call(s32[3]{0:T(128)S(1)} %pad_add_fusion.refs_0_.ids_ref, bf16[1024,128]{1,0:T(8,128)(2,1)S(1)} %copy-done.1, f32[1,128]{1,0:T(1,128)S(1)} %bitcast.10, bf16[3,256,128]{2,1,0:T(8,128)(2,1)S(1)} %get-tuple-element.14.m0_ref, bf16[3,256,128]{2,1,0:T(8,128)(2,1)S(1)} %collective-permute-done.m1_ref, ...), custom_call_target="tpu_custom_call" | custom-call | tf_op jit(solution)/shard_map/peel/pallas_call | solution.py:217
  39.5 0.2 collective-permute-start.3
  39.7 0.3 collective-permute-start.4
  40.0 1.7 %collective-permute-start.5 = (bf16[256,128]{1,0:T(8,128)(2,1)S(1)}, bf16[256,128]{1,0:T(8,128)(2,1)S(1)}, u32[]{:S(2)}, u32[]{:S(2)}) collective-permute-start(bf16[256,128]{1,0:T(8,128)(2,1)S(1)} %peel.1.r0_ref), channel_id=1, source_target_pairs={{0,192},{64,128},{128,64},{192,0},{1,193},{65,129},{129,65},{193,1... | collective-permute-start | bytes 196616 | tf_op jit(solution)/shard_map/ppermute | solution.py:362
  41.8 1.6 %label.1.coords_ref = bf16[64,8,128]{2,1,0:T(8,128)(2,1)S(1)} custom-call(s32[3]{0:T(128)S(1)} %pad_add_fusion.refs_0_.ids_ref, s32[32,1]{1,0:T(8,128)S(1)} %copy.10.tile_ref, bf16[2,1024]{1,0:T(2,128)(2,1)S(1)} %copy-done.4), custom_call_target="tpu_custom_call" | custom-call | tf_op jit(solution)/shard_map/label/pallas_call | solution.py:262
  43.4 1.5 %collective-permute-done.5.r3_ref = bf16[256,128]{1,0:T(8,128)(2,1)S(1)} collective-permute-done((bf16[256,128]{1,0:T(8,128)(2,1)S(1)}, bf16[256,128]{1,0:T(8,128)(2,1)S(1)}, u32[]{:S(2)}, u32[]{:S(2)}) %collective-permute-start.5) | collective-permute-done | bytes 65568 | tf_op jit(solution)/shard_map/ppermute | solution.py:362
  45.0 2.1 %pack.1 = (bf16[64,40,128]{2,1,0:T(8,128)(2,1)S(1)}, bf16[1024,128]{1,0:T(8,128)(2,1)}) custom-call(s32[3]{0:T(128)S(1)} %pad_add_fusion.refs_0_.ids_ref, s32[32]{0:T(128)S(1)} %bitcast.9, bf16[256,128]{1,0:T(8,128)(2,1)S(1)} %peel.1.r0_ref, bf16[256,128]{1,0:T(8,128)(2,1)S(1)} %collective-permute-done.3.r1_ref, ...), custom_call_target="tpu_custom_call" | custom-call | tf_op jit(solution)/shard_map/pack/pallas_call | solution.py:301
  47.1 32.4 %all_to_all.5.got_ref = bf16[64,40,128]{2,1,0:T(8,128)(2,1)S(1)} all-to-all(bf16[64,40,128]{2,1,0:T(8,128)(2,1)S(1)} %get-tuple-element.17), channel_id=1, replica_groups=mesh['dir'=4,'tb'=64] {'tb'}, dimensions={0} | all-to-all | bytes 1310720 | tf_op jit(solution)/shard_map/all_to_all | solution.py:382
  79.5 2.9 %grid.1 = (f32[2,256,128]{2,1,0:T(8,128)S(1)}, f32[2,256,128]{2,1,0:T(8,128)S(1)}) custom-call(s32[3]{0:T(128)S(1)} %pad_add_fusion.refs_0_.ids_ref, bf16[64,40,128]{2,1,0:T(8,128)(2,1)S(1)} %all_to_all.5.got_ref), custom_call_target="tpu_custom_call" | custom-call | tf_op jit(solution)/shard_map/grid/pallas_call | solution.py:347
  82.5 3.2 %collective-permute-start.6 = (f32[2,256,128]{2,1,0:T(8,128)S(1)}, f32[2,256,128]{2,1,0:T(8,128)S(1)}, u32[]{:S(2)}, u32[]{:S(2)}) collective-permute-start(f32[2,256,128]{2,1,0:T(8,128)S(1)} %get-tuple-element.19), channel_id=1, source_target_pairs={{0,64},{64,0},{128,192},{192,128},{1,65},{65,1},{129,193},{193,129... | collective-permute-start | bytes 786440 | tf_op jit(solution)/shard_map/ppermute | solution.py:362
  85.6 1.2 %collective-permute-done.6 = f32[2,256,128]{2,1,0:T(8,128)S(1)} collective-permute-done((f32[2,256,128]{2,1,0:T(8,128)S(1)}, f32[2,256,128]{2,1,0:T(8,128)S(1)}, u32[]{:S(2)}, u32[]{:S(2)}) %collective-permute-start.6) | collective-permute-done | bytes 262176 | tf_op jit(solution)/shard_map/ppermute | solution.py:362
  86.8 0.7 add_bitcast_fusion
  (20 shorter events, 0.3 us)
Async XLA Ops:
  0.7 1.4 %copy-start = (bf16[2,3072,128]{2,1,0:T(8,128)(2,1)S(1)}, bf16[2,3072,128]{2,1,0:T(8,128)(2,1)}, u32[]{:S(2)}) copy-start(bf16[2,3072,128]{2,1,0:T(8,128)(2,1)} %spec_ref.1) | copy-start | bytes 4718596
  2.1 0.7 copy-start.2
  2.9 0.7 copy-start.3
  3.6 0.7 copy-start.5
  4.3 0.7 copy-start.8
  14.2 21.6 %copy-start.1 = (bf16[1024,128]{1,0:T(8,128)(2,1)S(1)}, bf16[1024,128]{1,0:T(8,128)(2,1)}, u32[]{:S(2)}) copy-start(bf16[1024,128]{1,0:T(8,128)(2,1)} %vis_ref.1) | copy-start | bytes 786436
  14.2 21.6 %copy-start.7 = (f32[128]{0:T(128)S(1)}, f32[128]{0:T(128)}, u32[]{:S(2)}) copy-start(f32[128]{0:T(128)} %param.12) | copy-start | bytes 1540
  14.2 27.5 %copy-start.6 = (s32[32,1]{0,1:T(1,128)S(1)}, s32[32,1]{0,1:T(1,128)}, u32[]{:S(2)}) copy-start(s32[32,1]{0,1:T(1,128)} %param.15) | copy-start | bytes 388
  14.2 27.6 %copy-start.4 = (bf16[2,1024]{1,0:T(2,128)(2,1)S(1)}, bf16[2,1024]{1,0:T(2,128)(2,1)}, u32[]{:S(2)}) copy-start(bf16[2,1024]{1,0:T(2,128)(2,1)} %uv_ref.3) | copy-start | bytes 12292
  14.3 20.1 %collective-permute-start.2 = (bf16[3,256,128]{2,1,0:T(8,128)(2,1)S(1)}, bf16[3,256,128]{2,1,0:T(8,128)(2,1)S(1)}, u32[]{:S(2)}, u32[]{:S(2)}) collective-permute-start(bf16[3,256,128]{2,1,0:T(8,128)(2,1)S(1)} %predict.5), channel_id=1, source_target_pairs={{0,192},{64,128},{128,64},{192,0},{1,193},{65,129},{129,65},{193,1... | collective-permute-start | bytes 589832 | tf_op jit(solution)/shard_map/ppermute | solution.py:362
  22.8 11.6 %collective-permute-start.1 = (bf16[3,256,128]{2,1,0:T(8,128)(2,1)S(1)}, bf16[3,256,128]{2,1,0:T(8,128)(2,1)S(1)}, u32[]{:S(2)}, u32[]{:S(2)}) collective-permute-start(bf16[3,256,128]{2,1,0:T(8,128)(2,1)S(1)} %predict.4), channel_id=1, source_target_pairs={{0,128},{64,192},{128,0},{192,64},{1,129},{65,193},{129,1},{193,65... | collective-permute-start | bytes 589832 | tf_op jit(solution)/shard_map/ppermute | solution.py:362
  34.3 1.5 %collective-permute-start = (bf16[3,256,128]{2,1,0:T(8,128)(2,1)S(1)}, bf16[3,256,128]{2,1,0:T(8,128)(2,1)S(1)}, u32[]{:S(2)}, u32[]{:S(2)}) collective-permute-start(bf16[3,256,128]{2,1,0:T(8,128)(2,1)S(1)} %get-tuple-element.15), channel_id=1, source_target_pairs={{0,64},{64,0},{128,192},{192,128},{1,65},{65,1},{129,193},{193,129... | collective-permute-start | bytes 589832 | tf_op jit(solution)/shard_map/ppermute | solution.py:362
  39.5 3.9 %collective-permute-start.3 = (bf16[256,128]{1,0:T(8,128)(2,1)S(1)}, bf16[256,128]{1,0:T(8,128)(2,1)S(1)}, u32[]{:S(2)}, u32[]{:S(2)}) collective-permute-start(bf16[256,128]{1,0:T(8,128)(2,1)S(1)} %peel.1.r0_ref), channel_id=1, source_target_pairs={{0,64},{64,0},{128,192},{192,128},{1,65},{65,1},{129,193},{193,129... | collective-permute-start | bytes 196616 | tf_op jit(solution)/shard_map/ppermute | solution.py:362
  39.7 3.7 %collective-permute-start.4 = (bf16[256,128]{1,0:T(8,128)(2,1)S(1)}, bf16[256,128]{1,0:T(8,128)(2,1)S(1)}, u32[]{:S(2)}, u32[]{:S(2)}) collective-permute-start(bf16[256,128]{1,0:T(8,128)(2,1)S(1)} %peel.1.r0_ref), channel_id=1, source_target_pairs={{0,128},{64,192},{128,0},{192,64},{1,129},{65,193},{129,1},{193,65... | collective-permute-start | bytes 196616 | tf_op jit(solution)/shard_map/ppermute | solution.py:362
  40.0 5.0 %collective-permute-start.5 = (bf16[256,128]{1,0:T(8,128)(2,1)S(1)}, bf16[256,128]{1,0:T(8,128)(2,1)S(1)}, u32[]{:S(2)}, u32[]{:S(2)}) collective-permute-start(bf16[256,128]{1,0:T(8,128)(2,1)S(1)} %peel.1.r0_ref), channel_id=1, source_target_pairs={{0,192},{64,128},{128,64},{192,0},{1,193},{65,129},{129,65},{193,1... | collective-permute-start | bytes 196616 | tf_op jit(solution)/shard_map/ppermute | solution.py:362
  82.5 4.3 %collective-permute-start.6 = (f32[2,256,128]{2,1,0:T(8,128)S(1)}, f32[2,256,128]{2,1,0:T(8,128)S(1)}, u32[]{:S(2)}, u32[]{:S(2)}) collective-permute-start(f32[2,256,128]{2,1,0:T(8,128)S(1)} %get-tuple-element.19), channel_id=1, source_target_pairs={{0,64},{64,0},{128,192},{192,128},{1,65},{65,1},{129,193},{193,129... | collective-permute-start | bytes 786440 | tf_op jit(solution)/shard_map/ppermute | solution.py:362
where the time goes:
time: 87.8 us; the launch traced here: 87.5 us
  Pallas kernels  34.8 us (40%)
  blocking collectives  32.4 us (37%)
  starting transfers between devices  10.3 us (12%)
  local copies, waits for them, and re-layouts  4.31 us (5%)
  waiting for transfers between devices  4.13 us (5%)
    all_to_all x1, blocking collectives, local(): got = lax.all_to_all(send, 'tb', split_axis=0, concat_axis=0, tiled=True)  32.4 us
    pallas_call x3, Pallas kernels, predict(): pl.pallas_call(kernel, out_shape=tuple((jax.ShapeDtypeStruct((DIR_DEV, QR...  21.1 us
    ppermute x7, starting transfers between devices, swap(): return lax.ppermute(value, 'dir', [(i, i ^ flip) for i in range(N_DIR)])  10.3 us
    unnamed x19, local copies, waits for them, and re-layouts  4.31 us
    ppermute x7, waiting for transfers between devices, swap(): return lax.ppermute(value, 'dir', [(i, i ^ flip) for i in range(N_DIR)])  4.13 us
    pallas_call x1, Pallas kernels, peel(): pl.pallas_call(peel_kernel, out_shape=jax.ShapeDtypeStruct((QROWS, COLS),...  3.71 us
    pallas_call x1, Pallas kernels, prepare(): pl.pallas_call(prepare_kernel, out_shape=(jax.ShapeDtypeStruct((8, POOL),...  3.4 us
    pallas_call x1, Pallas kernels, grid_rows(): pl.pallas_call(grid_kernel, out_shape=(jax.ShapeDtypeStruct((2, PIX // N_...  2.94 us
  transfers between devices with their start and end apart: 7, of which 3 were waited for; matrix products, arithmetic and copies ran while one was open for 0% of the time, Pallas kernels for 19%

commit v1 on v0

--- a/solution.py
+++ b/solution.py
@@ -17,14 +17,13 @@
 N_DIR = 4
 N_TB = 64
 NB = 32
-SLOTS = 2
 QROWS = ROWS_DEV // N_DIR
 HALF = BB // 2
 POOL = DIR_DEV * NCOMP
 WIDE = DIR_DEV * COLS
 CHUNK = 256
 NCHUNK = POOL // CHUNK
-SEND_ROWS = SLOTS * HALF + 8
+MESSAGE = 8 * HALF + 8
 
 F32 = jnp.float32
 BF16 = jnp.bfloat16
@@ -64,7 +63,18 @@
     return high, mid, low
 
 
-def prepare_kernel(order_ref, assign_ref, lm_ref, uv_ref, spec_ref, lm8_ref, uv8_ref, wide_ref, pos_ref):
+def prepare_kernel(
+    order_hbm, assign_hbm, lm_hbm, uv_hbm, spec_hbm, lm8_ref, uv8_ref, wide_ref,
+    order_ref, assign_ref, lm_ref, uv_ref, spec_ref, pos_ref, sems
+):
+    pairs = (
+        (assign_hbm, assign_ref), (order_hbm, order_ref), (lm_hbm, lm_ref), (uv_hbm, uv_ref), (spec_hbm, spec_ref)
+    )
+    copies = [pltpu.make_async_copy(src, dst, sems.at[n]) for n, (src, dst) in enumerate(pairs)]
+    for copy in copies:
+        copy.start()
+    for copy in copies[:4]:
+        copy.wait()
     lh, lmid, ll = three_parts(lm_ref[...])
     zero = jnp.zeros((2, POOL), BF16)
     lm8_ref[...] = jnp.concatenate(
@@ -86,6 +96,7 @@
     pos_ref[...] = lax.dot_general(
         low_hot, high_hot, (((1,), (1,)), ((), ())), preferred_element_type=F32
     )
+    copies[4].wait()
 
     def mask_chunk(j, carry):
         for h in range(CHUNK // 128):
@@ -111,9 +122,17 @@
             jax.ShapeDtypeStruct((N_DIR, 8, QROWS), BF16),
             jax.ShapeDtypeStruct((NCHUNK, 2 * CHUNK, WIDE), BF16),
         ),
-        in_specs=[smem(), vmem(), vmem(), vmem(), vmem()],
+        in_specs=[pl.BlockSpec(memory_space=pl.ANY)] * 5,
         out_specs=(vmem(), vmem(), vmem()),
-        scratch_shapes=[pltpu.VMEM((128, 32), F32)],
+        scratch_shapes=[
+            pltpu.SMEM((DIR_DEV,), jnp.int32),
+            pltpu.VMEM((1, POOL), jnp.int32),
+            pltpu.VMEM((2, POOL), F32),
+            pltpu.VMEM((2, ROWS_DEV), BF16),
+            pltpu.VMEM((2, POOL, COLS), BF16),
+            pltpu.VMEM((128, 32), F32),
+            pltpu.SemaphoreType.DMA((5,)),
+        ],
         compiler_params=params(16),
         name="prepare",
     )(peel_order, assignment.reshape(1, POOL), comp_lm, uv_coords, spectra)
@@ -228,40 +247,46 @@
     )(ids, visibilities, ridge_weight.reshape(1, COLS), *models)
 
 
+def plane_offset(target, station):
+    return (((target >> 1) - (station >> 1)) & 3) * 2 + ((target ^ station) & 1)
+
+
+def plane_target(station, step):
+    return ((((station >> 1) + (step >> 1)) & 3) << 1) | ((station ^ step) & 1)
+
+
 def label_kernel(ids_ref, tile_ref, uv_ref, out_ref):
-    half = ids_ref[1]
-    offset = ids_ref[2]
-    tiles = tile_ref[...].astype(F32)
+    half, z, xy = ids_ref[1], ids_ref[2], ids_ref[3]
+    tiles = tile_ref[...]
     block_of_lane = lax.broadcasted_iota(jnp.int32, (NB, ROWS_DEV), 1) // BB
-    expand = (block_of_lane == lax.broadcasted_iota(jnp.int32, (NB, ROWS_DEV), 0)).astype(F32)
-    tile_of_lane = jnp.sum(expand * tiles, axis=0, keepdims=True)
+    expand = block_of_lane == lax.broadcasted_iota(jnp.int32, (NB, ROWS_DEV), 0)
     sub = lax.broadcasted_iota(jnp.int32, (NB, NB), 0)
     col = lax.broadcasted_iota(jnp.int32, (NB, NB), 1)
-    tile_row = jnp.sum(jnp.where(sub == col, tiles, 0.0), axis=0, keepdims=True)
-    slot = jnp.sum(jnp.where((tiles == tile_row) & (col < sub), 1.0, 0.0), axis=1, keepdims=True)
-    slot_of_row = lax.dot_general(
-        expand.astype(BF16),
-        jnp.broadcast_to(slot, (NB, COLS)).astype(BF16),
-        (((0,), (0,)), ((), ())),
-        preferred_element_type=F32,
-    )
+    tile_row = jnp.sum(jnp.where(sub == col, tiles.astype(F32), 0.0), axis=0, keepdims=True)
+    slot = jnp.sum(jnp.where((tiles.astype(F32) == tile_row) & (col < sub), 1.0, 0.0), axis=1, keepdims=True)
+    up = ((tiles >> 3) - z) & 7
+    across = plane_offset(tiles & 7, xy)
+    code = jnp.where(slot < 0.5, up * 8 + (tiles & 7), 64 + across * 8 + (tiles >> 3)).astype(F32)
+    code_of_lane = jnp.sum(jnp.where(expand, code, 0.0), axis=0, keepdims=True)
     within = lax.broadcasted_iota(jnp.int32, (ROWS_DEV, COLS), 0) % BB - half * HALF
     lane = lax.broadcasted_iota(jnp.int32, (ROWS_DEV, COLS), 1)
-    goal = slot_of_row.astype(jnp.int32) * HALF + within + offset
-    spot = jnp.where((goal == lane) & (within >= 0) & (within < HALF), 1.0, 0.0).astype(BF16)
-    row = lax.broadcasted_iota(jnp.int32, (N_TB * 8, ROWS_DEV), 0)
-    u = uv_ref[0:1, :].astype(F32)
-    v = uv_ref[1:2, :].astype(F32)
-    value = jnp.where(row % 8 == 0, u, jnp.where(row % 8 == 1, v, 0.0))
-    value = jnp.where((row // 8).astype(F32) == tile_of_lane, value, 0.0).astype(BF16)
-    out = jnp.dot(value, spot, preferred_element_type=F32)
-    out_ref[...] = out.reshape(N_TB, 8, COLS).astype(BF16)
+    spot = jnp.where(lane % HALF == within, 1.0, 0.0).astype(BF16)
+    row = lax.broadcasted_iota(jnp.int32, (128, ROWS_DEV), 0).astype(F32)
+    mine = row == code_of_lane
+    u = jnp.where(mine, uv_ref[0:1, :].astype(F32), 0.0).astype(BF16)
+    v = jnp.where(mine, uv_ref[1:2, :].astype(F32), 0.0).astype(BF16)
+    u = jnp.dot(u, spot, preferred_element_type=F32)
+    v = jnp.dot(v, spot, preferred_element_type=F32)
+    step = (lax.broadcasted_iota(jnp.int32, (128, COLS), 0) // 8) % 8
+    group = lax.broadcasted_iota(jnp.int32, (128, COLS), 1) // HALF
+    out = jnp.where(group == step, u, jnp.where(group == (step + 4) % 8, v, 0.0))
+    out_ref[...] = out.reshape(16, 8, COLS).astype(BF16)
 
 
 def label(ids, block_tile, uv_coords):
     return pl.pallas_call(
         label_kernel,
-        out_shape=jax.ShapeDtypeStruct((N_TB, 8, COLS), BF16),
+        out_shape=jax.ShapeDtypeStruct((16, 8, COLS), BF16),
         in_specs=[smem(), vmem(), vmem()],
         out_specs=vmem(),
         compiler_params=params(16),
@@ -269,17 +294,17 @@
     )(ids, block_tile, uv_coords)
 
 
-def pack_kernel(ids_ref, tile_ref, r0_ref, r1_ref, r2_ref, r3_ref, coords_ref, out_ref, all_ref, stage_ref, seen_ref):
-    me = ids_ref[0]
-    half = ids_ref[1]
+def pack_kernel(ids_ref, tile_ref, r0_ref, r1_ref, r2_ref, r3_ref, coords_ref, *rest):
+    out_refs = rest[:16]
+    all_ref, stage_ref, work_ref, seen_ref = rest[16:]
+    me, half, z, xy = ids_ref[0], ids_ref[1], ids_ref[2], ids_ref[3]
     for x, ref in enumerate((r0_ref, r1_ref, r2_ref, r3_ref)):
         rows = ref[...]
         all_ref[pl.ds(pl.multiple_of((me ^ x) * QROWS, QROWS), QROWS), :] = rows
         stage_ref[pl.ds((me ^ x) * (2 * QROWS // BB), 2 * QROWS // BB)] = rows.reshape(
             2 * QROWS // BB, HALF, COLS
         )
-    out_ref[:, : SLOTS * HALF, :] = jnp.zeros((N_TB, SLOTS * HALF, COLS), BF16)
-    out_ref[:, SLOTS * HALF :, :] = coords_ref[...]
+    work_ref[...] = jnp.zeros((16, 128, COLS), BF16)
 
     def clear(t, carry):
         seen_ref[t] = 0
@@ -289,46 +314,85 @@
 
     def place(b, carry):
         tile = tile_ref[b]
-        slot = seen_ref[tile]
-        seen_ref[tile] = slot + 1
-        out_ref[tile, pl.ds(pl.multiple_of(slot * HALF, HALF), HALF), :] = stage_ref[2 * b + half]
+        second = seen_ref[tile]
+        seen_ref[tile] = 1
+        up = ((tile >> 3) - z) & 7
+        across = 8 + plane_offset(tile & 7, xy)
+        message = jnp.where(second == 0, up, across)
+        piece = jnp.where(second == 0, tile & 7, tile >> 3)
+        work_ref[message, pl.ds(pl.multiple_of(piece * HALF, HALF), HALF), :] = stage_ref[2 * b + half]
         return carry
 
     lax.fori_loop(0, NB, place, 0)
+    for n in range(16):
+        out_refs[n][:128, :] = work_ref[n]
+        out_refs[n][128:, :] = coords_ref[n]
 
 
 def pack(ids, tile_ids, rows, coords):
-    return pl.pallas_call(
+    message = jax.ShapeDtypeStruct((MESSAGE, COLS), BF16)
+    out = pl.pallas_call(
         pack_kernel,
-        out_shape=(
-            jax.ShapeDtypeStruct((N_TB, SEND_ROWS, COLS), BF16),
-            jax.ShapeDtypeStruct((ROWS_DEV, COLS), BF16),
-        ),
+        out_shape=(message,) * 16 + (jax.ShapeDtypeStruct((ROWS_DEV, COLS), BF16),),
         in_specs=[smem(), smem()] + [vmem()] * 5,
-        out_specs=(vmem(), vmem()),
+        out_specs=(vmem(),) * 17,
         scratch_shapes=[
             pltpu.VMEM((2 * NB, HALF, COLS), BF16),
+            pltpu.VMEM((16, 128, COLS), BF16),
             pltpu.SMEM((N_TB,), jnp.int32),
         ],
         compiler_params=params(16),
         name="pack",
     )(ids, tile_ids, *rows, coords)
-
-
-def grid_kernel(ids_ref, got_ref, keep_ref, give_ref, tab_ref):
+    return out[:8], out[8:16], out[16]
+
+
+def regroup_kernel(second_is_plane, ids_ref, *refs):
+    in_refs, out_refs, (coords_ref,) = refs[:8], refs[8:16], refs[16:]
+    z, xy = ids_ref[2], ids_ref[3]
+    for d in range(8):
+        coords_ref[d * 8 : d * 8 + 8, :] = in_refs[d][128:, :].astype(F32)
+    for e in range(8):
+        piece = plane_target(xy, e) if second_is_plane else (z + e) & 7
+        for d in range(8):
+            out_refs[e][d * HALF : (d + 1) * HALF, :] = in_refs[d][
+                pl.ds(pl.multiple_of(piece * HALF, HALF), HALF), :
+            ]
+        out_refs[e][128:, :] = coords_ref[pl.ds(piece, 8, stride=8), :].astype(BF16)
+
+
+def regroup(ids, messages, second_is_plane):
+    message = jax.ShapeDtypeStruct((MESSAGE, COLS), BF16)
+
+    def kernel(*refs):
+        regroup_kernel(second_is_plane, *refs)
+
+    return pl.pallas_call(
+        kernel,
+        out_shape=(message,) * 8,
+        in_specs=[smem()] + [vmem()] * 8,
+        out_specs=(vmem(),) * 8,
+        scratch_shapes=[pltpu.VMEM((64, COLS), F32)],
+        compiler_params=params(16),
+        name="regroup",
+    )(ids, *messages)
+
+
+def grid_kernel(ids_ref, *refs):
+    in_refs, (keep_ref, give_ref, tab_ref, row_ref) = refs[:16], refs[16:]
     chip = ids_ref[0] // 2
     half = ids_ref[1]
-    tiles = N_TB * SLOTS * HALF // 128
-    groups = N_TB // tiles
-    coords = got_ref[:, SLOTS * HALF :, :].astype(F32).reshape(tiles, groups, 8, COLS)
-    coords = jnp.sum(coords, axis=1)
     y_pixel = (lax.broadcasted_iota(jnp.int32, (GRID, 1), 0) - GRID // 2).astype(F32)
     order = lax.broadcasted_iota(jnp.int32, (16, 1), 0)
     x_pixel = (16 * chip + 8 * ((order // 8) ^ half) + order % 8 - GRID // 2).astype(F32)
     scale = 1.0 / (2.0 * GRID)
-    for tile in range(tiles):
-        u = coords[tile, 0:1, :] * scale
-        v = coords[tile, 1:2, :] * scale
+    sub = lax.broadcasted_iota(jnp.int32, (8, COLS), 0)
+    group = lax.broadcasted_iota(jnp.int32, (8, COLS), 1) // HALF
+    for tile in range(16):
+        coords = in_refs[tile][128:, :].astype(F32)
+        u = jnp.sum(jnp.where(group == sub, coords, 0.0), axis=0, keepdims=True) * scale
+        v = jnp.sum(jnp.where(group == (sub + 4) % 8, coords, 0.0), axis=0, keepdims=True) * scale
+        v = pltpu.roll(v, 64, 1)
         cx, sx = cos_sin_turns(x_pixel * u)
         cy, sy = cos_sin_turns(y_pixel * v)
         lanes = slice(tile * 128, (tile + 1) * 128)
@@ -336,26 +400,36 @@
             a, b = cx[x : x + 1], sx[x : x + 1]
             tab_ref[x * GRID : (x + 1) * GRID, lanes] = (a * cy - b * sy).astype(BF16)
             tab_ref[512 + x * GRID : 512 + (x + 1) * GRID, lanes] = (b * cy + a * sy).astype(BF16)
-    rows = got_ref[:, : SLOTS * HALF, :].reshape(N_TB * SLOTS * HALF, COLS)
-    total = jnp.dot(tab_ref[...], rows, preferred_element_type=F32) * float(ROWS_DEV) ** (-0.5)
+        row_ref[lanes, :] = in_refs[tile][:128, :]
+    total = jnp.dot(tab_ref[...], row_ref[...], preferred_element_type=F32) * float(ROWS_DEV) ** (-0.5)
     for part in range(2):
         keep_ref[part] = total[part * 512 : part * 512 + 256]
         give_ref[part] = total[part * 512 + 256 : part * 512 + 512]
 
 
-def grid_rows(ids, got):
+def grid_rows(ids, messages):
     return pl.pallas_call(
         grid_kernel,
         out_shape=(
             jax.ShapeDtypeStruct((2, PIX // N_DIR, COLS), F32),
             jax.ShapeDtypeStruct((2, PIX // N_DIR, COLS), F32),
         ),
-        in_specs=[smem(), vmem()],
+        in_specs=[smem()] + [vmem()] * 16,
         out_specs=(vmem(), vmem()),
-        scratch_shapes=[pltpu.VMEM((1024, N_TB * SLOTS * HALF), BF16)],
+        scratch_shapes=[pltpu.VMEM((1024, 2048), BF16), pltpu.VMEM((2048, COLS), BF16)],
         compiler_params=params(24),
         name="grid",
-    )(ids, got)
+    )(ids, *messages)
+
+
+def up_z(messages):
+    pairs = [[(i, (i + 8 * d) % N_TB) for i in range(N_TB)] for d in range(8)]
+    return [messages[0]] + [lax.ppermute(messages[d], "tb", pairs[d]) for d in range(1, 8)]
+
+
+def over_plane(messages):
+    pairs = [[(i, (i & ~7) + plane_target(i & 7, d)) for i in range(N_TB)] for d in range(8)]
+    return [messages[0]] + [lax.ppermute(messages[d], "tb", pairs[d]) for d in range(1, 8)]
 
 
 def swap(value, flip):
@@ -367,7 +441,7 @@
 ):
     me = lax.axis_index("dir")
     station = lax.axis_index("tb")
-    ids = jnp.stack([me, me % 2, (station % 4) * BB]).astype(jnp.int32)
+    ids = jnp.stack([me, me & 1, station >> 3, station & 7]).astype(jnp.int32)
     lm8, uv8, wide = prepare(peel_order, assignment, comp_lm, uv_coords, spectra)
     (far_a,) = predict((2,), ids, uv8, lm8, wide)
     got_a = swap(far_a, 2)
@@ -378,9 +452,10 @@
     rows = peel(ids, visibilities, ridge_weight, (own, got_near, got_a, got_b))
     coords = label(ids, block_tile, uv_coords)
     gathered = (rows, swap(rows, 1), swap(rows, 2), swap(rows, 3))
-    send, residual = pack(ids, block_tile[:, 0], gathered, coords)
-    got = lax.all_to_all(send, "tb", split_axis=0, concat_axis=0, tiled=True)
-    keep, give = grid_rows(ids, got)
+    first_up, first_over, residual = pack(ids, block_tile[:, 0], gathered, coords)
+    second_over = regroup(ids, up_z(first_up), True)
+    second_up = regroup(ids, over_plane(first_over), False)
+    keep, give = grid_rows(ids, over_plane(second_over) + up_z(second_up))
     subgrids = (keep + swap(give, 1))[None]
     return residual, subgrids
 

time: 87.8 us -> 123 us (1.40)
  starting transfers between devices: 10.3 us -> 67.5 us
  blocking collectives: 32.4 us -> 0 us
  waiting for transfers between devices: 4.13 us -> 13.8 us
    ppermute x0 -> x28, starting transfers between devices: none -> 51.4 us  [the longest x14 27 us: up_z(): lax.ppermute(messages[d], 'tb', pairs[d])]
    all_to_all x1 -> x0, blocking collectives: 32.4 us -> none  [local(): got = lax.all_to_all(send, 'tb', split_axis=0, concat_axis=0, tiled=True)]
    ppermute x7, starting transfers between devices: 10.3 us -> 16 us  [swap(): return lax.ppermute(value, 'dir', [(i, i ^ flip) for i in range(N_DIR)])]
    ppermute x0 -> x28, waiting for transfers between devices: none -> 5.06 us  [the longest x14 5.02 us: over_plane(): lax.ppermute(messages[d], 'tb', pairs[d])]
    ppermute x7, waiting for transfers between devices: 4.13 us -> 8.74 us  [swap(): return lax.ppermute(value, 'dir', [(i, i ^ flip) for i in range(N_DIR)])]
    pallas_call x2 -> x4, Pallas kernels: 3.67 us -> 4.48 us  [the longest x1 2.22 us: pack(): pl.pallas_call(pack_kernel, out_shape=(message,) * 16 + (jax.ShapeDtypeSt...]
  transfers between devices with their start and end apart: 7 -> 35, of which waited for: 3 -> 6; matrix products, arithmetic and copies ran while one was open for 0% -> 0% of each run, Pallas kernels for 19% -> 11%
where the time goes in v1:
time: 123 us
  starting transfers between devices  67.5 us (55%)
  Pallas kernels  35.7 us (29%)
  waiting for transfers between devices  13.8 us (11%)
  local copies, waits for them, and re-layouts  4.31 us (4%)
    ppermute x14, starting transfers between devices, up_z(): lax.ppermute(messages[d], 'tb', pairs[d])  27 us
    ppermute x14, starting transfers between devices, over_plane(): lax.ppermute(messages[d], 'tb', pairs[d])  24.4 us
    pallas_call x3, Pallas kernels, predict(): pl.pallas_call(kernel, out_shape=tuple((jax.ShapeDtypeStruct((DIR_DEV, QR...  21.1 us
    ppermute x7, starting transfers between devices, swap(): return lax.ppermute(value, 'dir', [(i, i ^ flip) for i in range(N_DIR)])  16 us
    ppermute x7, waiting for transfers between devices, swap(): return lax.ppermute(value, 'dir', [(i, i ^ flip) for i in range(N_DIR)])  8.74 us
    ppermute x14, waiting for transfers between devices, over_plane(): lax.ppermute(messages[d], 'tb', pairs[d])  5.02 us
    unnamed x19, local copies, waits for them, and re-layouts  4.31 us
    pallas_call x1, Pallas kernels, peel(): pl.pallas_call(peel_kernel, out_shape=jax.ShapeDtypeStruct((QROWS, COLS),...  3.71 us
  transfers between devices with their start and end apart: 35, of which 6 were waited for; matrix products, arithmetic and copies ran while one was open for 0% of the time, Pallas kernels for 11%

profile of v1, /device:TPU:1, one launch (start us, length us, event | category | flops | bytes accessed | tf_op | source)
XLA Modules:
  0.0 122.9 jit_solution(15231445807705012890)
XLA Ops:
  4.9 3.4 %prepare.1 = (bf16[8,3072]{1,0:T(8,128)(2,1)S(1)}, bf16[4,8,256]{2,1,0:T(8,128)(2,1)S(1)}, bf16[12,512,384]{2,1,0:T(8,128)(2,1)S(1)}) custom-call(s32[3]{0:T(128)S(1)} %copy-done.8, s32[1,3072]{1,0:T(1,128)S(1)} %bitcast.9, f32[2,3072]{1,0:T(2,128)S(1)} %copy-done.2, bf16[2,1024]{1,0:T(2,128)(2,1)S(1)} %copy-done.3, bf16[2,3072,128]{2,1,0:T(8,128)(2,1)S(1)} %copy-done), custom_call_target="tpu_custom_call" | custom-call | tf_op jit(solution)/shard_map/prepare/pallas_call | solution.py:118
  8.3 9.4 %predict.3 = (bf16[3,256,128]{2,1,0:T(8,128)(2,1)S(1)}, bf16[3,256,128]{2,1,0:T(8,128)(2,1)S(1)}) custom-call(s32[4]{0:T(128)S(1)} %pad_add_fusion.refs_0_.ids_ref, bf16[4,8,256]{2,1,0:T(8,128)(2,1)S(1)} %get-tuple-element.42.refs_1_, bf16[8,3072]{1,0:T(8,128)(2,1)S(1)} %get-tuple-element.43.refs_2_, bf16[12,512,384]{2,1,0:T(8,128)(2,1)S(1)} %get-tuple-element.44.refs_3_), custom_call_target="tpu_custom_call" | custom-call | tf_op jit(solution)/shard_map/predict/pallas_call | solution.py:182
  17.8 3.3 %collective-permute-start = (bf16[3,256,128]{2,1,0:T(8,128)(2,1)S(1)}, bf16[3,256,128]{2,1,0:T(8,128)(2,1)S(1)}, u32[]{:S(2)}, u32[]{:S(2)}) collective-permute-start(bf16[3,256,128]{2,1,0:T(8,128)(2,1)S(1)} %get-tuple-element.46), channel_id=1, source_target_pairs={{0,64},{64,0},{128,192},{192,128},{1,65},{65,1},{129,193},{193,129... | collective-permute-start | bytes 589832 | tf_op jit(solution)/shard_map/ppermute | solution.py:436
  21.1 5.9 %predict.5 = bf16[3,256,128]{2,1,0:T(8,128)(2,1)S(1)} custom-call(s32[4]{0:T(128)S(1)} %pad_add_fusion.refs_0_.ids_ref, bf16[4,8,256]{2,1,0:T(8,128)(2,1)S(1)} %get-tuple-element.42.refs_1_, bf16[8,3072]{1,0:T(8,128)(2,1)S(1)} %get-tuple-element.43.refs_2_, bf16[12,512,384]{2,1,0:T(8,128)(2,1)S(1)} %get-tuple-element.44.refs_3_), custom_call_target="tpu_custom_call" | custom-call | tf_op jit(solution)/shard_map/predict/pallas_call | solution.py:182
  27.1 5.9 %predict.4 = bf16[3,256,128]{2,1,0:T(8,128)(2,1)S(1)} custom-call(s32[4]{0:T(128)S(1)} %pad_add_fusion.refs_0_.ids_ref, bf16[4,8,256]{2,1,0:T(8,128)(2,1)S(1)} %get-tuple-element.42.refs_1_, bf16[8,3072]{1,0:T(8,128)(2,1)S(1)} %get-tuple-element.43.refs_2_, bf16[12,512,384]{2,1,0:T(8,128)(2,1)S(1)} %get-tuple-element.44.refs_3_), custom_call_target="tpu_custom_call" | custom-call | tf_op jit(solution)/shard_map/predict/pallas_call | solution.py:182
  34.4 5.1 %collective-permute-done.1.m2_ref = bf16[3,256,128]{2,1,0:T(8,128)(2,1)S(1)} collective-permute-done((bf16[3,256,128]{2,1,0:T(8,128)(2,1)S(1)}, bf16[3,256,128]{2,1,0:T(8,128)(2,1)S(1)}, u32[]{:S(2)}, u32[]{:S(2)}) %collective-permute-start.1) | collective-permute-done | bytes 196640 | tf_op jit(solution)/shard_map/ppermute | solution.py:436
  39.4 3.7 %peel.1.r0_ref = bf16[256,128]{1,0:T(8,128)(2,1)S(1)} custom-call(s32[4]{0:T(128)S(1)} %pad_add_fusion.refs_0_.ids_ref, bf16[1024,128]{1,0:T(8,128)(2,1)S(1)} %copy-done.1, f32[1,128]{1,0:T(1,128)S(1)} %bitcast.11, bf16[3,256,128]{2,1,0:T(8,128)(2,1)S(1)} %get-tuple-element.45.m0_ref, bf16[3,256,128]{2,1,0:T(8,128)(2,1)S(1)} %collective-permute-done.m1_ref, ...), custom_call_target="tpu_custom_call" | custom-call | tf_op jit(solution)/shard_map/peel/pallas_call | solution.py:236
  49.6 2.2 %pack.1 = (bf16[136,128]{1,0:T(8,128)(2,1)S(1)}, bf16[136,128]{1,0:T(8,128)(2,1)S(1)}, bf16[136,128]{1,0:T(8,128)(2,1)S(1)}, bf16[136,128]{1,0:T(8,128)(2,1)S(1)...) custom-call(s32[4]{0:T(128)S(1)} %pad_add_fusion.refs_0_.ids_ref, ...), custom_call_target="tpu_custom_call" | custom-call | tf_op jit(solution)/shard_map/pack/pallas_call | solution.py:334
  56.3 2.1 %collective-permute-start.23 = (bf16[136,128]{1,0:T(8,128)(2,1)S(1)}, bf16[136,128]{1,0:T(8,128)(2,1)S(1)}, u32[]{:S(2)}, u32[]{:S(2)}) collective-permute-start(bf16[136,128]{1,0:T(8,128)(2,1)S(1)} %get-tuple-element.68), channel_id=1, source_target_pairs={{0,4},{1,5},{2,6},{3,7},{4,0},{5,1},{6,2},{7,3},{8,12},{9,13},{10,... | collective-permute-start | bytes 104456 | tf_op jit(solution)/shard_map/ppermute | solution.py:432
  58.4 3.0 %collective-permute-start.24 = (bf16[136,128]{1,0:T(8,128)(2,1)S(1)}, bf16[136,128]{1,0:T(8,128)(2,1)S(1)}, u32[]{:S(2)}, u32[]{:S(2)}) collective-permute-start(bf16[136,128]{1,0:T(8,128)(2,1)S(1)} %get-tuple-element.69), channel_id=1, source_target_pairs={{0,5},{1,4},{2,7},{3,6},{4,1},{5,0},{6,3},{7,2},{8,13},{9,12},{10,... | collective-permute-start | bytes 104456 | tf_op jit(solution)/shard_map/ppermute | solution.py:432
  64.0 5.7 %collective-permute-start.10 = (bf16[136,128]{1,0:T(8,128)(2,1)S(1)}, bf16[136,128]{1,0:T(8,128)(2,1)S(1)}, u32[]{:S(2)}, u32[]{:S(2)}) collective-permute-start(bf16[136,128]{1,0:T(8,128)(2,1)S(1)} %get-tuple-element.53), channel_id=1, source_target_pairs={{0,40},{1,41},{2,42},{3,43},{4,44},{5,45},{6,46},{7,47},{8,48},{9,... | collective-permute-start | bytes 104456 | tf_op jit(solution)/shard_map/ppermute | solution.py:427
  71.7 1.8 %collective-permute-start.7 = (bf16[136,128]{1,0:T(8,128)(2,1)S(1)}, bf16[136,128]{1,0:T(8,128)(2,1)S(1)}, u32[]{:S(2)}, u32[]{:S(2)}) collective-permute-start(bf16[136,128]{1,0:T(8,128)(2,1)S(1)} %get-tuple-element.50), channel_id=1, source_target_pairs={{0,16},{1,17},{2,18},{3,19},{4,20},{5,21},{6,22},{7,23},{8,24},{9,... | collective-permute-start | bytes 104456 | tf_op jit(solution)/shard_map/ppermute | solution.py:427
  73.6 2.2 %collective-permute-start.8 = (bf16[136,128]{1,0:T(8,128)(2,1)S(1)}, bf16[136,128]{1,0:T(8,128)(2,1)S(1)}, u32[]{:S(2)}, u32[]{:S(2)}) collective-permute-start(bf16[136,128]{1,0:T(8,128)(2,1)S(1)} %get-tuple-element.51), channel_id=1, source_target_pairs={{0,24},{1,25},{2,26},{3,27},{4,28},{5,29},{6,30},{7,31},{8,32},{9,... | collective-permute-start | bytes 104456 | tf_op jit(solution)/shard_map/ppermute | solution.py:427
  75.8 2.7 %collective-permute-start.9 = (bf16[136,128]{1,0:T(8,128)(2,1)S(1)}, bf16[136,128]{1,0:T(8,128)(2,1)S(1)}, u32[]{:S(2)}, u32[]{:S(2)}) collective-permute-start(bf16[136,128]{1,0:T(8,128)(2,1)S(1)} %get-tuple-element.52), channel_id=1, source_target_pairs={{0,32},{1,33},{2,34},{3,35},{4,36},{5,37},{6,38},{7,39},{8,40},{9,... | collective-permute-start | bytes 104456 | tf_op jit(solution)/shard_map/ppermute | solution.py:427
  79.9 2.4 %collective-permute-start.28 = (bf16[136,128]{1,0:T(8,128)(2,1)S(1)}, bf16[136,128]{1,0:T(8,128)(2,1)S(1)}, u32[]{:S(2)}, u32[]{:S(2)}) collective-permute-start(bf16[136,128]{1,0:T(8,128)(2,1)S(1)} %get-tuple-element.74), channel_id=1, source_target_pairs={{0,16},{1,17},{2,18},{3,19},{4,20},{5,21},{6,22},{7,23},{8,24},{9,... | collective-permute-start | bytes 104456 | tf_op jit(solution)/shard_map/ppermute | solution.py:427
  83.2 4.1 %collective-permute-start.30 = (bf16[136,128]{1,0:T(8,128)(2,1)S(1)}, bf16[136,128]{1,0:T(8,128)(2,1)S(1)}, u32[]{:S(2)}, u32[]{:S(2)}) collective-permute-start(bf16[136,128]{1,0:T(8,128)(2,1)S(1)} %get-tuple-element.76), channel_id=1, source_target_pairs={{0,32},{1,33},{2,34},{3,35},{4,36},{5,37},{6,38},{7,39},{8,40},{9,... | collective-permute-start | bytes 104456 | tf_op jit(solution)/shard_map/ppermute | solution.py:427
  88.8 2.6 %collective-permute-start.32 = (bf16[136,128]{1,0:T(8,128)(2,1)S(1)}, bf16[136,128]{1,0:T(8,128)(2,1)S(1)}, u32[]{:S(2)}, u32[]{:S(2)}) collective-permute-start(bf16[136,128]{1,0:T(8,128)(2,1)S(1)} %get-tuple-element.78), channel_id=1, source_target_pairs={{0,48},{1,49},{2,50},{3,51},{4,52},{5,53},{6,54},{7,55},{8,56},{9,... | collective-permute-start | bytes 104456 | tf_op jit(solution)/shard_map/ppermute | solution.py:427
  92.3 2.5 %collective-permute-start.13 = (bf16[136,128]{1,0:T(8,128)(2,1)S(1)}, bf16[136,128]{1,0:T(8,128)(2,1)S(1)}, u32[]{:S(2)}, u32[]{:S(2)}) collective-permute-start(bf16[136,128]{1,0:T(8,128)(2,1)S(1)} %get-tuple-element.57), channel_id=1, source_target_pairs={{0,1},{1,0},{2,3},{3,2},{4,5},{5,4},{6,7},{7,6},{8,9},{9,8},{10,11... | collective-permute-start | bytes 104456 | tf_op jit(solution)/shard_map/ppermute | solution.py:432
  96.3 2.5 %collective-permute-start.16 = (bf16[136,128]{1,0:T(8,128)(2,1)S(1)}, bf16[136,128]{1,0:T(8,128)(2,1)S(1)}, u32[]{:S(2)}, u32[]{:S(2)}) collective-permute-start(bf16[136,128]{1,0:T(8,128)(2,1)S(1)} %get-tuple-element.60), channel_id=1, source_target_pairs={{0,4},{1,5},{2,6},{3,7},{4,0},{5,1},{6,2},{7,3},{8,12},{9,13},{10,... | collective-permute-start | bytes 104456 | tf_op jit(solution)/shard_map/ppermute | solution.py:432
  98.8 2.6 %collective-permute-start.17 = (bf16[136,128]{1,0:T(8,128)(2,1)S(1)}, bf16[136,128]{1,0:T(8,128)(2,1)S(1)}, u32[]{:S(2)}, u32[]{:S(2)}) collective-permute-start(bf16[136,128]{1,0:T(8,128)(2,1)S(1)} %get-tuple-element.61), channel_id=1, source_target_pairs={{0,5},{1,4},{2,7},{3,6},{4,1},{5,0},{6,3},{7,2},{8,13},{9,12},{10,... | collective-permute-start | bytes 104456 | tf_op jit(solution)/shard_map/ppermute | solution.py:432
  101.5 2.6 %collective-permute-start.18 = (bf16[136,128]{1,0:T(8,128)(2,1)S(1)}, bf16[136,128]{1,0:T(8,128)(2,1)S(1)}, u32[]{:S(2)}, u32[]{:S(2)}) collective-permute-start(bf16[136,128]{1,0:T(8,128)(2,1)S(1)} %get-tuple-element.62), channel_id=1, source_target_pairs={{0,6},{1,7},{2,0},{3,1},{4,2},{5,3},{6,4},{7,5},{8,14},{9,15},{10,... | collective-permute-start | bytes 104456 | tf_op jit(solution)/shard_map/ppermute | solution.py:432
  105.6 3.9 %collective-permute-done.19.refs_7_ = bf16[136,128]{1,0:T(8,128)(2,1)S(1)} collective-permute-done((bf16[136,128]{1,0:T(8,128)(2,1)S(1)}, bf16[136,128]{1,0:T(8,128)(2,1)S(1)}, u32[]{:S(2)}, u32[]{:S(2)}) %collective-permute-start.19) | collective-permute-done | bytes 34848 | tf_op jit(solution)/shard_map/ppermute | solution.py:432
  109.5 3.0 %grid.1 = (f32[2,256,128]{2,1,0:T(8,128)S(1)}, f32[2,256,128]{2,1,0:T(8,128)S(1)}) custom-call(s32[4]{0:T(128)S(1)} %pad_add_fusion.refs_0_.ids_ref, bf16[136,128]{1,0:T(8,128)(2,1)S(1)} %get-tuple-element.56.refs_0_, bf16[136,128]{1,0:T(8,128)(2,1)S(1)} %collective-permute-done.13.refs_1_, bf16[136,128]{1,0:T(8,128)(2,1)S(1)} %collective-permute-done.14.refs_2_, ...), custom_call_target="tpu_custom_call" | custom-call | tf_op jit(solution)/shard_map/grid/pallas_call | solution.py:411
  112.5 8.5 %collective-permute-start.34 = (f32[2,256,128]{2,1,0:T(8,128)S(1)}, f32[2,256,128]{2,1,0:T(8,128)S(1)}, u32[]{:S(2)}, u32[]{:S(2)}) collective-permute-start(f32[2,256,128]{2,1,0:T(8,128)S(1)} %get-tuple-element.81), channel_id=1, source_target_pairs={{0,64},{64,0},{128,192},{192,128},{1,65},{65,1},{129,193},{193,129... | collective-permute-start | bytes 786440 | tf_op jit(solution)/shard_map/ppermute | solution.py:436
  (77 shorter events, 31.1 us)
Async XLA Ops:
  17.8 16.6 %collective-permute-start = (bf16[3,256,128]{2,1,0:T(8,128)(2,1)S(1)}, bf16[3,256,128]{2,1,0:T(8,128)(2,1)S(1)}, u32[]{:S(2)}, u32[]{:S(2)}) collective-permute-start(bf16[3,256,128]{2,1,0:T(8,128)(2,1)S(1)} %get-tuple-element.46), channel_id=1, source_target_pairs={{0,64},{64,0},{128,192},{192,128},{1,65},{65,1},{129,193},{193,129... | collective-permute-start | bytes 589832 | tf_op jit(solution)/shard_map/ppermute | solution.py:436
  51.8 9.6 %collective-permute-start.20 = (bf16[136,128]{1,0:T(8,128)(2,1)S(1)}, bf16[136,128]{1,0:T(8,128)(2,1)S(1)}, u32[]{:S(2)}, u32[]{:S(2)}) collective-permute-start(bf16[136,128]{1,0:T(8,128)(2,1)S(1)} %get-tuple-element.65), channel_id=1, source_target_pairs={{0,1},{1,0},{2,3},{3,2},{4,5},{5,4},{6,7},{7,6},{8,9},{9,8},{10,11... | collective-permute-start | bytes 104456 | tf_op jit(solution)/shard_map/ppermute | solution.py:432
  53.4 9.4 %collective-permute-start.21 = (bf16[136,128]{1,0:T(8,128)(2,1)S(1)}, bf16[136,128]{1,0:T(8,128)(2,1)S(1)}, u32[]{:S(2)}, u32[]{:S(2)}) collective-permute-start(bf16[136,128]{1,0:T(8,128)(2,1)S(1)} %get-tuple-element.66), channel_id=1, source_target_pairs={{0,2},{1,3},{2,4},{3,5},{4,6},{5,7},{6,0},{7,1},{8,10},{9,11},{10,... | collective-permute-start | bytes 104456 | tf_op jit(solution)/shard_map/ppermute | solution.py:432
  54.7 9.3 %collective-permute-start.22 = (bf16[136,128]{1,0:T(8,128)(2,1)S(1)}, bf16[136,128]{1,0:T(8,128)(2,1)S(1)}, u32[]{:S(2)}, u32[]{:S(2)}) collective-permute-start(bf16[136,128]{1,0:T(8,128)(2,1)S(1)} %get-tuple-element.67), channel_id=1, source_target_pairs={{0,3},{1,2},{2,5},{3,4},{4,7},{5,6},{6,1},{7,0},{8,11},{9,10},{10,... | collective-permute-start | bytes 104456 | tf_op jit(solution)/shard_map/ppermute | solution.py:432
  56.3 13.5 %collective-permute-start.23 = (bf16[136,128]{1,0:T(8,128)(2,1)S(1)}, bf16[136,128]{1,0:T(8,128)(2,1)S(1)}, u32[]{:S(2)}, u32[]{:S(2)}) collective-permute-start(bf16[136,128]{1,0:T(8,128)(2,1)S(1)} %get-tuple-element.68), channel_id=1, source_target_pairs={{0,4},{1,5},{2,6},{3,7},{4,0},{5,1},{6,2},{7,3},{8,12},{9,13},{10,... | collective-permute-start | bytes 104456 | tf_op jit(solution)/shard_map/ppermute | solution.py:432
  58.4 11.6 %collective-permute-start.24 = (bf16[136,128]{1,0:T(8,128)(2,1)S(1)}, bf16[136,128]{1,0:T(8,128)(2,1)S(1)}, u32[]{:S(2)}, u32[]{:S(2)}) collective-permute-start(bf16[136,128]{1,0:T(8,128)(2,1)S(1)} %get-tuple-element.69), channel_id=1, source_target_pairs={{0,5},{1,4},{2,7},{3,6},{4,1},{5,0},{6,3},{7,2},{8,13},{9,12},{10,... | collective-permute-start | bytes 104456 | tf_op jit(solution)/shard_map/ppermute | solution.py:432
  61.4 9.1 %collective-permute-start.25 = (bf16[136,128]{1,0:T(8,128)(2,1)S(1)}, bf16[136,128]{1,0:T(8,128)(2,1)S(1)}, u32[]{:S(2)}, u32[]{:S(2)}) collective-permute-start(bf16[136,128]{1,0:T(8,128)(2,1)S(1)} %get-tuple-element.70), channel_id=1, source_target_pairs={{0,6},{1,7},{2,0},{3,1},{4,2},{5,3},{6,4},{7,5},{8,14},{9,15},{10,... | collective-permute-start | bytes 104456 | tf_op jit(solution)/shard_map/ppermute | solution.py:432
  62.8 8.9 %collective-permute-start.26 = (bf16[136,128]{1,0:T(8,128)(2,1)S(1)}, bf16[136,128]{1,0:T(8,128)(2,1)S(1)}, u32[]{:S(2)}, u32[]{:S(2)}) collective-permute-start(bf16[136,128]{1,0:T(8,128)(2,1)S(1)} %get-tuple-element.71), channel_id=1, source_target_pairs={{0,7},{1,6},{2,1},{3,0},{4,3},{5,2},{6,5},{7,4},{8,15},{9,14},{10,... | collective-permute-start | bytes 104456 | tf_op jit(solution)/shard_map/ppermute | solution.py:432
  64.0 9.5 %collective-permute-start.10 = (bf16[136,128]{1,0:T(8,128)(2,1)S(1)}, bf16[136,128]{1,0:T(8,128)(2,1)S(1)}, u32[]{:S(2)}, u32[]{:S(2)}) collective-permute-start(bf16[136,128]{1,0:T(8,128)(2,1)S(1)} %get-tuple-element.53), channel_id=1, source_target_pairs={{0,40},{1,41},{2,42},{3,43},{4,44},{5,45},{6,46},{7,47},{8,48},{9,... | collective-permute-start | bytes 104456 | tf_op jit(solution)/shard_map/ppermute | solution.py:427
  70.0 9.1 %collective-permute-start.12 = (bf16[136,128]{1,0:T(8,128)(2,1)S(1)}, bf16[136,128]{1,0:T(8,128)(2,1)S(1)}, u32[]{:S(2)}, u32[]{:S(2)}) collective-permute-start(bf16[136,128]{1,0:T(8,128)(2,1)S(1)} %get-tuple-element.55), channel_id=1, source_target_pairs={{0,56},{1,57},{2,58},{3,59},{4,60},{5,61},{6,62},{7,63},{8,0},{9,1... | collective-permute-start | bytes 104456 | tf_op jit(solution)/shard_map/ppermute | solution.py:427
  70.5 9.4 %collective-permute-start.6 = (bf16[136,128]{1,0:T(8,128)(2,1)S(1)}, bf16[136,128]{1,0:T(8,128)(2,1)S(1)}, u32[]{:S(2)}, u32[]{:S(2)}) collective-permute-start(bf16[136,128]{1,0:T(8,128)(2,1)S(1)} %get-tuple-element.49), channel_id=1, source_target_pairs={{0,8},{1,9},{2,10},{3,11},{4,12},{5,13},{6,14},{7,15},{8,16},{9,17... | collective-permute-start | bytes 104456 | tf_op jit(solution)/shard_map/ppermute | solution.py:427
  71.7 10.6 %collective-permute-start.7 = (bf16[136,128]{1,0:T(8,128)(2,1)S(1)}, bf16[136,128]{1,0:T(8,128)(2,1)S(1)}, u32[]{:S(2)}, u32[]{:S(2)}) collective-permute-start(bf16[136,128]{1,0:T(8,128)(2,1)S(1)} %get-tuple-element.50), channel_id=1, source_target_pairs={{0,16},{1,17},{2,18},{3,19},{4,20},{5,21},{6,22},{7,23},{8,24},{9,... | collective-permute-start | bytes 104456 | tf_op jit(solution)/shard_map/ppermute | solution.py:427
  73.6 9.6 %collective-permute-start.8 = (bf16[136,128]{1,0:T(8,128)(2,1)S(1)}, bf16[136,128]{1,0:T(8,128)(2,1)S(1)}, u32[]{:S(2)}, u32[]{:S(2)}) collective-permute-start(bf16[136,128]{1,0:T(8,128)(2,1)S(1)} %get-tuple-element.51), channel_id=1, source_target_pairs={{0,24},{1,25},{2,26},{3,27},{4,28},{5,29},{6,30},{7,31},{8,32},{9,... | collective-permute-start | bytes 104456 | tf_op jit(solution)/shard_map/ppermute | solution.py:427
  75.8 11.5 %collective-permute-start.9 = (bf16[136,128]{1,0:T(8,128)(2,1)S(1)}, bf16[136,128]{1,0:T(8,128)(2,1)S(1)}, u32[]{:S(2)}, u32[]{:S(2)}) collective-permute-start(bf16[136,128]{1,0:T(8,128)(2,1)S(1)} %get-tuple-element.52), channel_id=1, source_target_pairs={{0,32},{1,33},{2,34},{3,35},{4,36},{5,37},{6,38},{7,39},{8,40},{9,... | collective-permute-start | bytes 104456 | tf_op jit(solution)/shard_map/ppermute | solution.py:427
  79.1 9.7 %collective-permute-start.27 = (bf16[136,128]{1,0:T(8,128)(2,1)S(1)}, bf16[136,128]{1,0:T(8,128)(2,1)S(1)}, u32[]{:S(2)}, u32[]{:S(2)}) collective-permute-start(bf16[136,128]{1,0:T(8,128)(2,1)S(1)} %get-tuple-element.73), channel_id=1, source_target_pairs={{0,8},{1,9},{2,10},{3,11},{4,12},{5,13},{6,14},{7,15},{8,16},{9,17... | collective-permute-start | bytes 104456 | tf_op jit(solution)/shard_map/ppermute | solution.py:427
  79.9 11.5 %collective-permute-start.28 = (bf16[136,128]{1,0:T(8,128)(2,1)S(1)}, bf16[136,128]{1,0:T(8,128)(2,1)S(1)}, u32[]{:S(2)}, u32[]{:S(2)}) collective-permute-start(bf16[136,128]{1,0:T(8,128)(2,1)S(1)} %get-tuple-element.74), channel_id=1, source_target_pairs={{0,16},{1,17},{2,18},{3,19},{4,20},{5,21},{6,22},{7,23},{8,24},{9,... | collective-permute-start | bytes 104456 | tf_op jit(solution)/shard_map/ppermute | solution.py:427
  82.3 10.0 %collective-permute-start.29 = (bf16[136,128]{1,0:T(8,128)(2,1)S(1)}, bf16[136,128]{1,0:T(8,128)(2,1)S(1)}, u32[]{:S(2)}, u32[]{:S(2)}) collective-permute-start(bf16[136,128]{1,0:T(8,128)(2,1)S(1)} %get-tuple-element.75), channel_id=1, source_target_pairs={{0,24},{1,25},{2,26},{3,27},{4,28},{5,29},{6,30},{7,31},{8,32},{9,... | collective-permute-start | bytes 104456 | tf_op jit(solution)/shard_map/ppermute | solution.py:427
  83.2 11.6 %collective-permute-start.30 = (bf16[136,128]{1,0:T(8,128)(2,1)S(1)}, bf16[136,128]{1,0:T(8,128)(2,1)S(1)}, u32[]{:S(2)}, u32[]{:S(2)}) collective-permute-start(bf16[136,128]{1,0:T(8,128)(2,1)S(1)} %get-tuple-element.76), channel_id=1, source_target_pairs={{0,32},{1,33},{2,34},{3,35},{4,36},{5,37},{6,38},{7,39},{8,40},{9,... | collective-permute-start | bytes 104456 | tf_op jit(solution)/shard_map/ppermute | solution.py:427
  87.2 8.7 %collective-permute-start.31 = (bf16[136,128]{1,0:T(8,128)(2,1)S(1)}, bf16[136,128]{1,0:T(8,128)(2,1)S(1)}, u32[]{:S(2)}, u32[]{:S(2)}) collective-permute-start(bf16[136,128]{1,0:T(8,128)(2,1)S(1)} %get-tuple-element.77), channel_id=1, source_target_pairs={{0,40},{1,41},{2,42},{3,43},{4,44},{5,45},{6,46},{7,47},{8,48},{9,... | collective-permute-start | bytes 104456 | tf_op jit(solution)/shard_map/ppermute | solution.py:427
  92.3 9.2 %collective-permute-start.13 = (bf16[136,128]{1,0:T(8,128)(2,1)S(1)}, bf16[136,128]{1,0:T(8,128)(2,1)S(1)}, u32[]{:S(2)}, u32[]{:S(2)}) collective-permute-start(bf16[136,128]{1,0:T(8,128)(2,1)S(1)} %get-tuple-element.57), channel_id=1, source_target_pairs={{0,1},{1,0},{2,3},{3,2},{4,5},{5,4},{6,7},{7,6},{8,9},{9,8},{10,11... | collective-permute-start | bytes 104456 | tf_op jit(solution)/shard_map/ppermute | solution.py:432
  94.7 9.3 %collective-permute-start.14 = (bf16[136,128]{1,0:T(8,128)(2,1)S(1)}, bf16[136,128]{1,0:T(8,128)(2,1)S(1)}, u32[]{:S(2)}, u32[]{:S(2)}) collective-permute-start(bf16[136,128]{1,0:T(8,128)(2,1)S(1)} %get-tuple-element.58), channel_id=1, source_target_pairs={{0,2},{1,3},{2,4},{3,5},{4,6},{5,7},{6,0},{7,1},{8,10},{9,11},{10,... | collective-permute-start | bytes 104456 | tf_op jit(solution)/shard_map/ppermute | solution.py:432
  96.0 8.5 %collective-permute-start.15 = (bf16[136,128]{1,0:T(8,128)(2,1)S(1)}, bf16[136,128]{1,0:T(8,128)(2,1)S(1)}, u32[]{:S(2)}, u32[]{:S(2)}) collective-permute-start(bf16[136,128]{1,0:T(8,128)(2,1)S(1)} %get-tuple-element.59), channel_id=1, source_target_pairs={{0,3},{1,2},{2,5},{3,4},{4,7},{5,6},{6,1},{7,0},{8,11},{9,10},{10,... | collective-permute-start | bytes 104456 | tf_op jit(solution)/shard_map/ppermute | solution.py:432
  96.3 8.2 %collective-permute-start.16 = (bf16[136,128]{1,0:T(8,128)(2,1)S(1)}, bf16[136,128]{1,0:T(8,128)(2,1)S(1)}, u32[]{:S(2)}, u32[]{:S(2)}) collective-permute-start(bf16[136,128]{1,0:T(8,128)(2,1)S(1)} %get-tuple-element.60), channel_id=1, source_target_pairs={{0,4},{1,5},{2,6},{3,7},{4,0},{5,1},{6,2},{7,3},{8,12},{9,13},{10,... | collective-permute-start | bytes 104456 | tf_op jit(solution)/shard_map/ppermute | solution.py:432
  112.5 9.6 %collective-permute-start.34 = (f32[2,256,128]{2,1,0:T(8,128)S(1)}, f32[2,256,128]{2,1,0:T(8,128)S(1)}, u32[]{:S(2)}, u32[]{:S(2)}) collective-permute-start(f32[2,256,128]{2,1,0:T(8,128)S(1)} %get-tuple-element.81), channel_id=1, source_target_pairs={{0,64},{64,0},{128,192},{192,128},{1,65},{65,1},{129,193},{193,129... | collective-permute-start | bytes 786440 | tf_op jit(solution)/shard_map/ppermute | solution.py:436
  (20 other events, 166.9 us)

commit v2 on v0

--- a/solution.py
+++ b/solution.py
@@ -64,7 +64,18 @@
     return high, mid, low
 
 
-def prepare_kernel(order_ref, assign_ref, lm_ref, uv_ref, spec_ref, lm8_ref, uv8_ref, wide_ref, pos_ref):
+def prepare_kernel(
+    order_hbm, assign_hbm, lm_hbm, uv_hbm, spec_hbm, lm8_ref, uv8_ref, wide_ref,
+    order_ref, assign_ref, lm_ref, uv_ref, spec_ref, pos_ref, sems
+):
+    pairs = (
+        (assign_hbm, assign_ref), (order_hbm, order_ref), (lm_hbm, lm_ref), (uv_hbm, uv_ref), (spec_hbm, spec_ref)
+    )
+    copies = [pltpu.make_async_copy(src, dst, sems.at[n]) for n, (src, dst) in enumerate(pairs)]
+    for copy in copies:
+        copy.start()
+    for copy in copies[:4]:
+        copy.wait()
     lh, lmid, ll = three_parts(lm_ref[...])
     zero = jnp.zeros((2, POOL), BF16)
     lm8_ref[...] = jnp.concatenate(
@@ -83,24 +94,20 @@
         place = jnp.where(segment == order_ref[p], float(p), place)
     low_hot = (lax.broadcasted_iota(jnp.int32, (128, POOL), 0) == low).astype(F32).astype(BF16)
     high_hot = jnp.where(lax.broadcasted_iota(jnp.int32, (32, POOL), 0) == high, place, 0.0).astype(BF16)
-    pos_ref[...] = lax.dot_general(
-        low_hot, high_hot, (((1,), (1,)), ((), ())), preferred_element_type=F32
-    )
-
-    def mask_chunk(j, carry):
-        for h in range(CHUNK // 128):
-            column = 2 * j + h
-            pick = (lax.broadcasted_iota(jnp.int32, (32, 128), 0) == column).astype(F32).astype(BF16)
-            place_here = jnp.dot(pos_ref[...].astype(BF16), pick, preferred_element_type=F32)
+    pos = lax.dot_general(low_hot, high_hot, (((1,), (1,)), ((), ())), preferred_element_type=F32)
+    column = lax.broadcasted_iota(jnp.int32, (32, POOL), 1) // 128
+    pick = (column == lax.broadcasted_iota(jnp.int32, (32, POOL), 0)).astype(F32).astype(BF16)
+    pos_ref[...] = jnp.dot(pos.astype(BF16), pick, preferred_element_type=F32)
+    copies[4].wait()
+    for column in range(POOL // 128):
+        place_here = pos_ref[:, column * 128 : (column + 1) * 128]
+        for p in range(DIR_DEV):
+            mask = jnp.where(place_here == float(p), 1.0, 0.0).astype(BF16)
             for part in range(2):
-                rows = spec_ref[part, pl.ds(pl.multiple_of(column * 128, 128), 128), :].astype(F32)
-                for p in range(DIR_DEV):
-                    kept = jnp.where(place_here == float(p), rows, 0.0).astype(BF16)
-                    first = part * CHUNK + h * 128
-                    wide_ref[j, first : first + 128, p * COLS : (p + 1) * COLS] = kept
-        return carry
-
-    lax.fori_loop(0, NCHUNK, mask_chunk, 0)
+                first = part * CHUNK + (column % 2) * 128
+                wide_ref[column // 2, first : first + 128, p * COLS : (p + 1) * COLS] = (
+                    spec_ref[part, column * 128 : (column + 1) * 128, :] * mask
+                )
 
 
 def prepare(peel_order, assignment, comp_lm, uv_coords, spectra):
@@ -111,12 +118,23 @@
             jax.ShapeDtypeStruct((N_DIR, 8, QROWS), BF16),
             jax.ShapeDtypeStruct((NCHUNK, 2 * CHUNK, WIDE), BF16),
         ),
-        in_specs=[smem(), vmem(), vmem(), vmem(), vmem()],
+        in_specs=[pl.BlockSpec(memory_space=pltpu.MemorySpace.HBM)] * 5,
         out_specs=(vmem(), vmem(), vmem()),
-        scratch_shapes=[pltpu.VMEM((128, 32), F32)],
+        scratch_shapes=[
+            pltpu.SMEM((DIR_DEV,), jnp.int32),
+            pltpu.VMEM((1, POOL), jnp.int32),
+            pltpu.VMEM((2, POOL), F32),
+            pltpu.VMEM((2, ROWS_DEV), BF16),
+            pltpu.VMEM((2, POOL, COLS), BF16),
+            pltpu.VMEM((128, POOL), F32),
+            pltpu.SemaphoreType.DMA((5,)),
+        ],
         compiler_params=params(16),
         name="prepare",
-    )(peel_order, assignment.reshape(1, POOL), comp_lm, uv_coords, spectra)
+    )(*(
+        pltpu.with_memory_space_constraint(value, pltpu.MemorySpace.HBM)
+        for value in (peel_order, assignment.reshape(1, POOL), comp_lm, uv_coords, spectra)
+    ))
 
 
 def predict_kernel(flips, ids_ref, uv8_ref, lm8_ref, wide_ref, *rest):
@@ -126,29 +144,22 @@
     uv_rows = jnp.concatenate([uv8_ref[me ^ x].astype(F32).T for x in flips], axis=0).astype(BF16)
 
     def table(j, tab_ref):
-        lm = lm8_ref[:, pl.ds(pl.multiple_of(j * CHUNK, CHUNK), CHUNK)]
+        lm = lm8_ref[:, j * CHUNK : (j + 1) * CHUNK]
         turns = jnp.dot(uv_rows, lm, preferred_element_type=F32)
         cos, sin = cos_sin_turns(turns)
         tab_ref[:, :CHUNK] = cos.astype(BF16)
         tab_ref[:, CHUNK:] = sin.astype(BF16)
 
-    def gather(j, tab_ref):
-        acc_ref[...] += jnp.dot(tab_ref[...], wide_ref[j], preferred_element_type=F32)
-
-    acc_ref[...] = jnp.zeros(acc_ref.shape, F32)
+    tabs = (tab_a, tab_b)
     table(0, tab_a)
-
-    def step(i, carry):
-        gather(2 * i, tab_a)
-        table(2 * i + 1, tab_b)
-        gather(2 * i + 1, tab_b)
-        table(jnp.minimum(2 * i + 2, NCHUNK - 1), tab_a)
-        return carry
-
-    lax.fori_loop(0, NCHUNK // 2 - 1, step, 0)
-    table(NCHUNK - 1, tab_b)
-    gather(NCHUNK - 2, tab_a)
-    gather(NCHUNK - 1, tab_b)
+    for j in range(NCHUNK):
+        if j + 1 < NCHUNK:
+            table(j + 1, tabs[(j + 1) % 2])
+        part = jnp.dot(tabs[j % 2][...], wide_ref[j], preferred_element_type=F32)
+        if j == 0:
+            acc_ref[...] = part
+        else:
+            acc_ref[...] += part
     for n in range(len(flips)):
         for p in range(DIR_DEV):
             out_refs[n][p] = acc_ref[n * QROWS : (n + 1) * QROWS, p * COLS : (p + 1) * COLS].astype(BF16)
@@ -170,6 +181,11 @@
             pltpu.VMEM((rows, 2 * CHUNK), BF16),
             pltpu.VMEM((rows, WIDE), F32),
         ],
+        cost_estimate=pl.CostEstimate(
+            flops=2 * rows * 2 * POOL * 2 * WIDE,
+            transcendentals=0,
+            bytes_accessed=2 * (2 * POOL * WIDE + rows * WIDE),
+        ),
         compiler_params=params(16),
         name="predict",
     )(ids, uv8, lm8, wide)
@@ -228,7 +244,7 @@
     )(ids, visibilities, ridge_weight.reshape(1, COLS), *models)
 
 
-def label_kernel(ids_ref, tile_ref, uv_ref, out_ref):
+def label_kernel(ids_ref, tile_id_ref, tile_ref, uv_ref, out_ref, slot_ref, seen_ref):
     half = ids_ref[1]
     offset = ids_ref[2]
     tiles = tile_ref[...].astype(F32)
@@ -255,64 +271,71 @@
     value = jnp.where(row % 8 == 0, u, jnp.where(row % 8 == 1, v, 0.0))
     value = jnp.where((row // 8).astype(F32) == tile_of_lane, value, 0.0).astype(BF16)
     out = jnp.dot(value, spot, preferred_element_type=F32)
-    out_ref[...] = out.reshape(N_TB, 8, COLS).astype(BF16)
-
-
-def label(ids, block_tile, uv_coords):
+    out_ref[:, : SLOTS * HALF, :] = jnp.zeros((N_TB, SLOTS * HALF, COLS), BF16)
+    out_ref[:, SLOTS * HALF :, :] = out.reshape(N_TB, 8, COLS).astype(BF16)
+    for t in range(N_TB):
+        seen_ref[t] = 0
+    for b in range(NB):
+        tile = tile_id_ref[b]
+        slot_ref[b] = seen_ref[tile]
+        seen_ref[tile] = 1
+
+
+def label(ids, tile_ids, block_tile, uv_coords):
     return pl.pallas_call(
         label_kernel,
-        out_shape=jax.ShapeDtypeStruct((N_TB, 8, COLS), BF16),
-        in_specs=[smem(), vmem(), vmem()],
-        out_specs=vmem(),
+        out_shape=(
+            jax.ShapeDtypeStruct((N_TB, SEND_ROWS, COLS), BF16),
+            jax.ShapeDtypeStruct((NB,), jnp.int32),
+        ),
+        in_specs=[smem(), smem(), vmem(), vmem()],
+        out_specs=(vmem(), smem()),
+        scratch_shapes=[pltpu.SMEM((N_TB,), jnp.int32)],
         compiler_params=params(16),
         name="label",
-    )(ids, block_tile, uv_coords)
-
-
-def pack_kernel(ids_ref, tile_ref, r0_ref, r1_ref, r2_ref, r3_ref, coords_ref, out_ref, all_ref, stage_ref, seen_ref):
+    )(ids, tile_ids, block_tile, uv_coords)
+
+
+def pack_kernel(ids_ref, tile_ref, slot_ref, r0_ref, r1_ref, r2_ref, r3_ref, base_ref, out_ref, stage_ref):
     me = ids_ref[0]
     half = ids_ref[1]
+    out_ref[...] = base_ref[...]
     for x, ref in enumerate((r0_ref, r1_ref, r2_ref, r3_ref)):
-        rows = ref[...]
-        all_ref[pl.ds(pl.multiple_of((me ^ x) * QROWS, QROWS), QROWS), :] = rows
-        stage_ref[pl.ds((me ^ x) * (2 * QROWS // BB), 2 * QROWS // BB)] = rows.reshape(
+        stage_ref[pl.ds((me ^ x) * (2 * QROWS // BB), 2 * QROWS // BB)] = ref[...].reshape(
             2 * QROWS // BB, HALF, COLS
         )
-    out_ref[:, : SLOTS * HALF, :] = jnp.zeros((N_TB, SLOTS * HALF, COLS), BF16)
-    out_ref[:, SLOTS * HALF :, :] = coords_ref[...]
-
-    def clear(t, carry):
-        seen_ref[t] = 0
-        return carry
-
-    lax.fori_loop(0, N_TB, clear, 0)
-
-    def place(b, carry):
-        tile = tile_ref[b]
-        slot = seen_ref[tile]
-        seen_ref[tile] = slot + 1
-        out_ref[tile, pl.ds(pl.multiple_of(slot * HALF, HALF), HALF), :] = stage_ref[2 * b + half]
-        return carry
-
-    lax.fori_loop(0, NB, place, 0)
-
-
-def pack(ids, tile_ids, rows, coords):
+    for b in range(NB):
+        first = pl.multiple_of(slot_ref[b] * HALF, HALF)
+        out_ref[tile_ref[b], pl.ds(first, HALF), :] = stage_ref[2 * b + half]
+
+
+def pack(ids, tile_ids, slots, rows, base):
     return pl.pallas_call(
         pack_kernel,
-        out_shape=(
-            jax.ShapeDtypeStruct((N_TB, SEND_ROWS, COLS), BF16),
-            jax.ShapeDtypeStruct((ROWS_DEV, COLS), BF16),
-        ),
-        in_specs=[smem(), smem()] + [vmem()] * 5,
-        out_specs=(vmem(), vmem()),
-        scratch_shapes=[
-            pltpu.VMEM((2 * NB, HALF, COLS), BF16),
-            pltpu.SMEM((N_TB,), jnp.int32),
-        ],
+        out_shape=jax.ShapeDtypeStruct((N_TB, SEND_ROWS, COLS), BF16),
+        in_specs=[smem(), smem(), smem()] + [vmem()] * 5,
+        out_specs=vmem(),
+        scratch_shapes=[pltpu.VMEM((2 * NB, HALF, COLS), BF16)],
         compiler_params=params(16),
         name="pack",
-    )(ids, tile_ids, *rows, coords)
+    )(ids, tile_ids, slots, *rows, base)
+
+
+def join_kernel(ids_ref, r0_ref, r1_ref, r2_ref, r3_ref, out_ref):
+    me = ids_ref[0]
+    for x, ref in enumerate((r0_ref, r1_ref, r2_ref, r3_ref)):
+        out_ref[pl.ds(pl.multiple_of((me ^ x) * QROWS, QROWS), QROWS), :] = ref[...]
+
+
+def join(ids, rows):
+    return pl.pallas_call(
+        join_kernel,
+        out_shape=jax.ShapeDtypeStruct((ROWS_DEV, COLS), BF16),
+        in_specs=[smem()] + [vmem()] * 4,
+        out_specs=vmem(),
+        compiler_params=params(16),
+        name="join",
+    )(ids, *rows)
 
 
 def grid_kernel(ids_ref, got_ref, keep_ref, give_ref, tab_ref):
@@ -358,6 +381,10 @@
     )(ids, got)
 
 
+def after(value, done):
+    return lax.optimization_barrier((value, done))[0]
+
+
 def swap(value, flip):
     return lax.ppermute(value, "dir", [(i, i ^ flip) for i in range(N_DIR)])
 
@@ -376,11 +403,13 @@
     near, own = predict((1, 0), ids, uv8, lm8, wide)
     got_near = swap(near, 1)
     rows = peel(ids, visibilities, ridge_weight, (own, got_near, got_a, got_b))
-    coords = label(ids, block_tile, uv_coords)
     gathered = (rows, swap(rows, 1), swap(rows, 2), swap(rows, 3))
-    send, residual = pack(ids, block_tile[:, 0], gathered, coords)
+    tile_ids = block_tile[:, 0]
+    base, slots = label(after(ids, rows), tile_ids, block_tile, uv_coords)
+    send = pack(ids, tile_ids, slots, gathered, base)
     got = lax.all_to_all(send, "tb", split_axis=0, concat_axis=0, tiled=True)
-    keep, give = grid_rows(ids, got)
+    residual = join(after(ids, send), gathered)
+    keep, give = grid_rows(after(ids, residual), got)
     subgrids = (keep + swap(give, 1))[None]
     return residual, subgrids
 

time: 87.8 us -> 75.8 us (0.86)
  blocking collectives: 32.4 us -> 0 us
  waiting for transfers between devices: 4.13 us -> 22.4 us
  starting transfers between devices: 10.3 us -> 23.5 us
  Pallas kernels: 34.8 us -> 27.9 us
  local copies, waits for them, and re-layouts: 4.31 us -> 0.11 us
    all_to_all x1 -> x0, blocking collectives: 32.4 us -> none  [local(): got = lax.all_to_all(send, 'tb', split_axis=0, concat_axis=0, tiled=True)]
    all_to_all x0 -> x1, waiting for transfers between devices: none -> 18.3 us  [local(): got = lax.all_to_all(send, 'tb', split_axis=0, concat_axis=0, tiled=True)]
    all_to_all x0 -> x1, starting transfers between devices: none -> 13.1 us  [local(): got = lax.all_to_all(send, 'tb', split_axis=0, concat_axis=0, tiled=True)]
    pallas_call x3, Pallas kernels: 21.1 us -> 14.1 us  [predict(): pl.pallas_call(kernel, out_shape=tuple((jax.ShapeDtypeStruct((DIR_DEV, QR...]
    unnamed x19 -> x9, local copies, waits for them, and re-layouts: 4.31 us -> 0.11 us
    pallas_call x2 -> x3, Pallas kernels: 3.67 us -> 4.34 us  [the longest x1 1.57 us: label(): pl.pallas_call(label_kernel, out_shape=(jax.ShapeDtypeStruct((N_TB, SEND_...]
  transfers between devices with their start and end apart: 7 -> 8, of which waited for: 3 -> 4; matrix products, arithmetic and copies ran while one was open for 0% -> 0% of each run, Pallas kernels for 19% -> 17%
where the time goes in v2:
time: 75.8 us; the launch traced here: 75.5 us
  Pallas kernels  27.9 us (37%)
  starting transfers between devices  23.5 us (31%)
  waiting for transfers between devices  22.4 us (30%)
  other arithmetic  0.81 us (1%)
  between operations  0.79 us (1%)
    all_to_all x1, waiting for transfers between devices, local(): got = lax.all_to_all(send, 'tb', split_axis=0, concat_axis=0, tiled=True)  18.3 us
    pallas_call x3, Pallas kernels, predict(): pl.pallas_call(kernel, out_shape=tuple((jax.ShapeDtypeStruct((DIR_DEV, QR...  14.1 us
    all_to_all x1, starting transfers between devices, local(): got = lax.all_to_all(send, 'tb', split_axis=0, concat_axis=0, tiled=True)  13.1 us
    ppermute x7, starting transfers between devices, swap(): return lax.ppermute(value, 'dir', [(i, i ^ flip) for i in range(N_DIR)])  10.4 us
    ppermute x7, waiting for transfers between devices, swap(): return lax.ppermute(value, 'dir', [(i, i ^ flip) for i in range(N_DIR)])  4.11 us
    pallas_call x1, Pallas kernels, peel(): pl.pallas_call(peel_kernel, out_shape=jax.ShapeDtypeStruct((QROWS, COLS),...  3.71 us
    pallas_call x1, Pallas kernels, grid_rows(): pl.pallas_call(grid_kernel, out_shape=(jax.ShapeDtypeStruct((2, PIX // N_...  2.94 us
    pallas_call x1, Pallas kernels, prepare(): pl.pallas_call(prepare_kernel, out_shape=(jax.ShapeDtypeStruct((8, POOL),...  2.85 us
  transfers between devices with their start and end apart: 8, of which 4 were waited for; matrix products, arithmetic and copies ran while one was open for 0% of the time, Pallas kernels for 17%

profile of v2, /device:TPU:1, one launch (start us, length us, event | category | flops | bytes accessed | tf_op | source)
XLA Modules:
  0.0 75.5 jit_solution(18226336280908261362)
XLA Ops:
  0.6 0.1 pad_add_fusion.refs_0_.ids_ref
  0.7 2.9 %prepare.1 = (bf16[8,3072]{1,0:T(8,128)(2,1)S(1)}, bf16[4,8,256]{2,1,0:T(8,128)(2,1)S(1)}, bf16[12,512,384]{2,1,0:T(8,128)(2,1)S(1)}) custom-call(s32[3]{0:T(128)} %order_hbm.1, s32[1,3072]{1,0:T(1,128)} %bitcast.11, f32[2,3072]{1,0:T(2,128)} %lm_hbm.1, bf16[2,1024]{1,0:T(2,128)(2,1)} %uv_ref.1, bf16[2,3072,128]{2,1,0:T(8,128)(2,1)} %spec_hbm.1), custom_call_target="tpu_custom_call" | custom-call | tf_op jit(solution)/shard_map/prepare/pallas_call | solution.py:114
  3.6 3.9 %predict.5 = bf16[3,256,128]{2,1,0:T(8,128)(2,1)S(1)} custom-call(s32[3]{0:T(128)S(1)} %pad_add_fusion.refs_0_.ids_ref, bf16[4,8,256]{2,1,0:T(8,128)(2,1)S(1)} %get-tuple-element.14.refs_1_, bf16[8,3072]{1,0:T(8,128)(2,1)S(1)} %get-tuple-element.15.refs_2_, bf16[12,512,384]{2,1,0:T(8,128)(2,1)S(1)} %get-tuple-element.16.refs_3_), custom_call_target="tpu_custom_call" | custom-call | flops 2415919104 | bytes 4915200 | tf_op jit(solution)/shard_map/predict/pallas_call | solution.py:174
  7.5 2.7 %collective-permute-start.2 = (bf16[3,256,128]{2,1,0:T(8,128)(2,1)S(1)}, bf16[3,256,128]{2,1,0:T(8,128)(2,1)S(1)}, u32[]{:S(2)}, u32[]{:S(2)}) collective-permute-start(bf16[3,256,128]{2,1,0:T(8,128)(2,1)S(1)} %predict.5), channel_id=1, source_target_pairs={{0,192},{64,128},{128,64},{192,0},{1,193},{65,129},{129,65},{193,1... | collective-permute-start | bytes 589832 | tf_op jit(solution)/shard_map/ppermute | solution.py:389
  10.2 3.9 %predict.4 = bf16[3,256,128]{2,1,0:T(8,128)(2,1)S(1)} custom-call(s32[3]{0:T(128)S(1)} %pad_add_fusion.refs_0_.ids_ref, bf16[4,8,256]{2,1,0:T(8,128)(2,1)S(1)} %get-tuple-element.14.refs_1_, bf16[8,3072]{1,0:T(8,128)(2,1)S(1)} %get-tuple-element.15.refs_2_, bf16[12,512,384]{2,1,0:T(8,128)(2,1)S(1)} %get-tuple-element.16.refs_3_), custom_call_target="tpu_custom_call" | custom-call | flops 2415919104 | bytes 4915200 | tf_op jit(solution)/shard_map/predict/pallas_call | solution.py:174
  14.2 2.3 %collective-permute-start.1 = (bf16[3,256,128]{2,1,0:T(8,128)(2,1)S(1)}, bf16[3,256,128]{2,1,0:T(8,128)(2,1)S(1)}, u32[]{:S(2)}, u32[]{:S(2)}) collective-permute-start(bf16[3,256,128]{2,1,0:T(8,128)(2,1)S(1)} %predict.4), channel_id=1, source_target_pairs={{0,128},{64,192},{128,0},{192,64},{1,129},{65,193},{129,1},{193,65... | collective-permute-start | bytes 589832 | tf_op jit(solution)/shard_map/ppermute | solution.py:389
  16.4 6.2 %predict.3 = (bf16[3,256,128]{2,1,0:T(8,128)(2,1)S(1)}, bf16[3,256,128]{2,1,0:T(8,128)(2,1)S(1)}) custom-call(s32[3]{0:T(128)S(1)} %pad_add_fusion.refs_0_.ids_ref, bf16[4,8,256]{2,1,0:T(8,128)(2,1)S(1)} %get-tuple-element.14.refs_1_, bf16[8,3072]{1,0:T(8,128)(2,1)S(1)} %get-tuple-element.15.refs_2_, bf16[12,512,384]{2,1,0:T(8,128)(2,1)S(1)} %get-tuple-element.16.refs_3_), custom_call_target="tpu_custom_call" | custom-call | flops 4831838208 | bytes 5111808 | tf_op jit(solution)/shard_map/predict/pallas_call | solution.py:174
  22.7 0.1 collective-permute-start
  22.8 1.4 %collective-permute-done.m1_ref = bf16[3,256,128]{2,1,0:T(8,128)(2,1)S(1)} collective-permute-done((bf16[3,256,128]{2,1,0:T(8,128)(2,1)S(1)}, bf16[3,256,128]{2,1,0:T(8,128)(2,1)S(1)}, u32[]{:S(2)}, u32[]{:S(2)}) %collective-permute-start) | collective-permute-done | bytes 196640 | tf_op jit(solution)/shard_map/ppermute | solution.py:389
  24.2 3.7 %peel.1.r0_ref = bf16[256,128]{1,0:T(8,128)(2,1)S(1)} custom-call(s32[3]{0:T(128)S(1)} %pad_add_fusion.refs_0_.ids_ref, bf16[1024,128]{1,0:T(8,128)(2,1)S(1)} %copy-done, f32[1,128]{1,0:T(1,128)S(1)} %bitcast.10, bf16[3,256,128]{2,1,0:T(8,128)(2,1)S(1)} %get-tuple-element.17.m0_ref, bf16[3,256,128]{2,1,0:T(8,128)(2,1)S(1)} %collective-permute-done.m1_ref, ...), custom_call_target="tpu_custom_call" | custom-call | tf_op jit(solution)/shard_map/peel/pallas_call | solution.py:233
  27.9 0.2 collective-permute-start.3
  28.1 0.3 collective-permute-start.4
  28.4 1.7 %collective-permute-start.5 = (bf16[256,128]{1,0:T(8,128)(2,1)S(1)}, bf16[256,128]{1,0:T(8,128)(2,1)S(1)}, u32[]{:S(2)}, u32[]{:S(2)}) collective-permute-start(bf16[256,128]{1,0:T(8,128)(2,1)S(1)} %peel.1.r0_ref), channel_id=1, source_target_pairs={{0,192},{64,128},{128,64},{192,0},{1,193},{65,129},{129,65},{193,1... | collective-permute-start | bytes 196616 | tf_op jit(solution)/shard_map/ppermute | solution.py:389
  30.1 0.1 copy.10.tile_ref
  30.2 1.6 %label.1 = (bf16[64,40,128]{2,1,0:T(8,128)(2,1)S(1)}, s32[32]{0:T(128)S(1)}) custom-call(s32[3]{0:T(128)S(1)} %pad_add_fusion.refs_0_.ids_ref, s32[32]{0:T(128)S(1)} %bitcast.8, s32[32,1]{1,0:T(8,128)S(1)} %copy.10.tile_ref, bf16[2,1024]{1,0:T(2,128)(2,1)S(1)} %copy-done.1), custom_call_target="tpu_custom_call" | custom-call | tf_op jit(solution)/shard_map/label/pallas_call | solution.py:285
  31.8 1.5 %collective-permute-done.5.r3_ref = bf16[256,128]{1,0:T(8,128)(2,1)S(1)} collective-permute-done((bf16[256,128]{1,0:T(8,128)(2,1)S(1)}, bf16[256,128]{1,0:T(8,128)(2,1)S(1)}, u32[]{:S(2)}, u32[]{:S(2)}) %collective-permute-start.5) | collective-permute-done | bytes 65568 | tf_op jit(solution)/shard_map/ppermute | solution.py:389
  33.4 1.5 %pack.1 = bf16[64,40,128]{2,1,0:T(8,128)(2,1)} custom-call(s32[3]{0:T(128)S(1)} %pad_add_fusion.refs_0_.ids_ref, s32[32]{0:T(128)S(1)} %bitcast.9, s32[32]{0:T(128)S(1)} %get-tuple-element.20.slot_ref, bf16[256,128]{1,0:T(8,128)(2,1)S(1)} %peel.1.r0_ref, bf16[256,128]{1,0:T(8,128)(2,1)S(1)} %collective-permute-done.3.r1_ref, ...), custom_call_target="tpu_custom_call" | custom-call | tf_op jit(solution)/shard_map/pack/pallas_call | solution.py:313
  34.9 13.1 %all-to-all-start = ((bf16[64,40,128]{2,1,0:T(8,128)(2,1)}), bf16[64,40,128]{2,1,0:T(8,128)(2,1)S(1)}, u32[]{:S(2)}, u32[]{:S(2)}) async-start(bf16[64,40,128]{2,1,0:T(8,128)(2,1)} %pack.1), calls=%async_computation | async-start | bytes 1310720 | tf_op jit(solution)/shard_map/all_to_all | solution.py:410
  47.9 1.3 %join.1 = bf16[1024,128]{1,0:T(8,128)(2,1)} custom-call(s32[3]{0:T(128)S(1)} %pad_add_fusion.refs_0_.ids_ref, bf16[256,128]{1,0:T(8,128)(2,1)S(1)} %peel.1.r0_ref, bf16[256,128]{1,0:T(8,128)(2,1)S(1)} %collective-permute-done.3.r1_ref, bf16[256,128]{1,0:T(8,128)(2,1)S(1)} %collective-permute-done.4.r2_ref, bf16[256,128]{1,0:T(8,128)(2,1)S(1)} %collective-permute-done.5.r3_ref), custom_call_target="tpu_custom_call" | custom-call | tf_op jit(solution)/shard_map/join/pallas_call | solution.py:331
  49.2 18.3 %all-to-all-done.got_ref = bf16[64,40,128]{2,1,0:T(8,128)(2,1)S(1)} async-done(((bf16[64,40,128]{2,1,0:T(8,128)(2,1)}), bf16[64,40,128]{2,1,0:T(8,128)(2,1)S(1)}, u32[]{:S(2)}, u32[]{:S(2)}) %all-to-all-start) | async-done | bytes 655392 | tf_op jit(solution)/shard_map/all_to_all | solution.py:410
  67.5 2.9 %grid.1 = (f32[2,256,128]{2,1,0:T(8,128)S(1)}, f32[2,256,128]{2,1,0:T(8,128)S(1)}) custom-call(s32[3]{0:T(128)S(1)} %pad_add_fusion.refs_0_.ids_ref, bf16[64,40,128]{2,1,0:T(8,128)(2,1)S(1)} %all-to-all-done.got_ref), custom_call_target="tpu_custom_call" | custom-call | tf_op jit(solution)/shard_map/grid/pallas_call | solution.py:370
  70.5 3.2 %collective-permute-start.6 = (f32[2,256,128]{2,1,0:T(8,128)S(1)}, f32[2,256,128]{2,1,0:T(8,128)S(1)}, u32[]{:S(2)}, u32[]{:S(2)}) collective-permute-start(f32[2,256,128]{2,1,0:T(8,128)S(1)} %get-tuple-element.25), channel_id=1, source_target_pairs={{0,64},{64,0},{128,192},{192,128},{1,65},{65,1},{129,193},{193,129... | collective-permute-start | bytes 786440 | tf_op jit(solution)/shard_map/ppermute | solution.py:389
  73.6 1.2 %collective-permute-done.6 = f32[2,256,128]{2,1,0:T(8,128)S(1)} collective-permute-done((f32[2,256,128]{2,1,0:T(8,128)S(1)}, f32[2,256,128]{2,1,0:T(8,128)S(1)}, u32[]{:S(2)}, u32[]{:S(2)}) %collective-permute-start.6) | collective-permute-done | bytes 262176 | tf_op jit(solution)/shard_map/ppermute | solution.py:389
  74.8 0.7 add_bitcast_fusion
  (12 shorter events, 0.0 us)
Async XLA Ops:
  7.5 15.3 %collective-permute-start.2 = (bf16[3,256,128]{2,1,0:T(8,128)(2,1)S(1)}, bf16[3,256,128]{2,1,0:T(8,128)(2,1)S(1)}, u32[]{:S(2)}, u32[]{:S(2)}) collective-permute-start(bf16[3,256,128]{2,1,0:T(8,128)(2,1)S(1)} %predict.5), channel_id=1, source_target_pairs={{0,192},{64,128},{128,64},{192,0},{1,193},{65,129},{129,65},{193,1... | collective-permute-start | bytes 589832 | tf_op jit(solution)/shard_map/ppermute | solution.py:389
  14.1 10.1 %copy-start = (bf16[1024,128]{1,0:T(8,128)(2,1)S(1)}, bf16[1024,128]{1,0:T(8,128)(2,1)}, u32[]{:S(2)}) copy-start(bf16[1024,128]{1,0:T(8,128)(2,1)} %vis_ref.1) | copy-start | bytes 786436
  14.1 10.1 %copy-start.3 = (f32[128]{0:T(128)S(1)}, f32[128]{0:T(128)}, u32[]{:S(2)}) copy-start(f32[128]{0:T(128)} %param.12) | copy-start | bytes 1540
  14.1 16.0 %copy-start.2 = (s32[32,1]{0,1:T(1,128)S(1)}, s32[32,1]{0,1:T(1,128)}, u32[]{:S(2)}) copy-start(s32[32,1]{0,1:T(1,128)} %param.15) | copy-start | bytes 388
  14.2 16.1 %copy-start.1 = (bf16[2,1024]{1,0:T(2,128)(2,1)S(1)}, bf16[2,1024]{1,0:T(2,128)(2,1)}, u32[]{:S(2)}) copy-start(bf16[2,1024]{1,0:T(2,128)(2,1)} %uv_ref.1) | copy-start | bytes 12292
  14.2 8.6 %collective-permute-start.1 = (bf16[3,256,128]{2,1,0:T(8,128)(2,1)S(1)}, bf16[3,256,128]{2,1,0:T(8,128)(2,1)S(1)}, u32[]{:S(2)}, u32[]{:S(2)}) collective-permute-start(bf16[3,256,128]{2,1,0:T(8,128)(2,1)S(1)} %predict.4), channel_id=1, source_target_pairs={{0,128},{64,192},{128,0},{192,64},{1,129},{65,193},{129,1},{193,65... | collective-permute-start | bytes 589832 | tf_op jit(solution)/shard_map/ppermute | solution.py:389
  22.7 1.5 %collective-permute-start = (bf16[3,256,128]{2,1,0:T(8,128)(2,1)S(1)}, bf16[3,256,128]{2,1,0:T(8,128)(2,1)S(1)}, u32[]{:S(2)}, u32[]{:S(2)}) collective-permute-start(bf16[3,256,128]{2,1,0:T(8,128)(2,1)S(1)} %get-tuple-element.18), channel_id=1, source_target_pairs={{0,64},{64,0},{128,192},{192,128},{1,65},{65,1},{129,193},{193,129... | collective-permute-start | bytes 589832 | tf_op jit(solution)/shard_map/ppermute | solution.py:389
  27.9 3.9 %collective-permute-start.3 = (bf16[256,128]{1,0:T(8,128)(2,1)S(1)}, bf16[256,128]{1,0:T(8,128)(2,1)S(1)}, u32[]{:S(2)}, u32[]{:S(2)}) collective-permute-start(bf16[256,128]{1,0:T(8,128)(2,1)S(1)} %peel.1.r0_ref), channel_id=1, source_target_pairs={{0,64},{64,0},{128,192},{192,128},{1,65},{65,1},{129,193},{193,129... | collective-permute-start | bytes 196616 | tf_op jit(solution)/shard_map/ppermute | solution.py:389
  28.1 3.7 %collective-permute-start.4 = (bf16[256,128]{1,0:T(8,128)(2,1)S(1)}, bf16[256,128]{1,0:T(8,128)(2,1)S(1)}, u32[]{:S(2)}, u32[]{:S(2)}) collective-permute-start(bf16[256,128]{1,0:T(8,128)(2,1)S(1)} %peel.1.r0_ref), channel_id=1, source_target_pairs={{0,128},{64,192},{128,0},{192,64},{1,129},{65,193},{129,1},{193,65... | collective-permute-start | bytes 196616 | tf_op jit(solution)/shard_map/ppermute | solution.py:389
  28.4 5.0 %collective-permute-start.5 = (bf16[256,128]{1,0:T(8,128)(2,1)S(1)}, bf16[256,128]{1,0:T(8,128)(2,1)S(1)}, u32[]{:S(2)}, u32[]{:S(2)}) collective-permute-start(bf16[256,128]{1,0:T(8,128)(2,1)S(1)} %peel.1.r0_ref), channel_id=1, source_target_pairs={{0,192},{64,128},{128,64},{192,0},{1,193},{65,129},{129,65},{193,1... | collective-permute-start | bytes 196616 | tf_op jit(solution)/shard_map/ppermute | solution.py:389
  34.9 32.7 %all-to-all-start = ((bf16[64,40,128]{2,1,0:T(8,128)(2,1)}), bf16[64,40,128]{2,1,0:T(8,128)(2,1)S(1)}, u32[]{:S(2)}, u32[]{:S(2)}) async-start(bf16[64,40,128]{2,1,0:T(8,128)(2,1)} %pack.1), calls=%async_computation | async-start | bytes 1310720 | tf_op jit(solution)/shard_map/all_to_all | solution.py:410
  70.5 4.3 %collective-permute-start.6 = (f32[2,256,128]{2,1,0:T(8,128)S(1)}, f32[2,256,128]{2,1,0:T(8,128)S(1)}, u32[]{:S(2)}, u32[]{:S(2)}) collective-permute-start(f32[2,256,128]{2,1,0:T(8,128)S(1)} %get-tuple-element.25), channel_id=1, source_target_pairs={{0,64},{64,0},{128,192},{192,128},{1,65},{65,1},{129,193},{193,129... | collective-permute-start | bytes 786440 | tf_op jit(solution)/shard_map/ppermute | solution.py:389

commit v3 on v2

--- a/solution.py
+++ b/solution.py
@@ -19,12 +19,13 @@
 NB = 32
 SLOTS = 2
 QROWS = ROWS_DEV // N_DIR
-HALF = BB // 2
+PART = BB // N_DIR
 POOL = DIR_DEV * NCOMP
 WIDE = DIR_DEV * COLS
 CHUNK = 256
 NCHUNK = POOL // CHUNK
-SEND_ROWS = SLOTS * HALF + 8
+SEND_ROWS = SLOTS * PART + 8
+QBLOCKS = QROWS // BB
 
 F32 = jnp.float32
 BF16 = jnp.bfloat16
@@ -195,7 +196,8 @@
     return jnp.sum(value.reshape(QROWS // GB, GB, COLS), axis=1)
 
 
-def peel_kernel(ids_ref, vis_ref, ridge_ref, m0_ref, m1_ref, m2_ref, m3_ref, out_ref, model_ref, inv_ref):
+def peel_kernel(ids_ref, vis_ref, ridge_ref, m0_ref, m1_ref, m2_ref, m3_ref, out_ref, *rest):
+    part_refs, (model_ref, inv_ref, part_ref) = rest[:N_DIR], rest[N_DIR:]
     me = ids_ref[0]
     ridge = ridge_ref[...]
     for x, ref in enumerate((m0_ref, m1_ref, m2_ref, m3_ref)):
@@ -227,25 +229,31 @@
         if (j + 1) % DIR_DEV == 0:
             remains = remains.astype(BF16).astype(F32)
     out_ref[...] = remains.astype(BF16)
+    part_ref[...] = remains.reshape(QBLOCKS, N_DIR, PART, COLS)
+    for x in range(N_DIR):
+        part_refs[x][...] = part_ref[:, me ^ x].astype(BF16)
 
 
 def peel(ids, visibilities, ridge_weight, models):
-    return pl.pallas_call(
+    out = pl.pallas_call(
         peel_kernel,
-        out_shape=jax.ShapeDtypeStruct((QROWS, COLS), BF16),
+        out_shape=(jax.ShapeDtypeStruct((QROWS, COLS), BF16),)
+        + (jax.ShapeDtypeStruct((QBLOCKS, PART, COLS), BF16),) * N_DIR,
         in_specs=[smem()] + [vmem()] * 6,
-        out_specs=vmem(),
+        out_specs=(vmem(),) * (1 + N_DIR),
         scratch_shapes=[
             pltpu.VMEM((N_DIR * DIR_DEV, QROWS, COLS), F32),
             pltpu.VMEM((N_DIR * DIR_DEV, QROWS // GB, COLS), F32),
+            pltpu.VMEM((QBLOCKS, N_DIR, PART, COLS), F32),
         ],
         compiler_params=params(16),
         name="peel",
     )(ids, visibilities, ridge_weight.reshape(1, COLS), *models)
+    return out[0], out[1:]
 
 
 def label_kernel(ids_ref, tile_id_ref, tile_ref, uv_ref, out_ref, slot_ref, seen_ref):
-    half = ids_ref[1]
+    me = ids_ref[0]
     offset = ids_ref[2]
     tiles = tile_ref[...].astype(F32)
     block_of_lane = lax.broadcasted_iota(jnp.int32, (NB, ROWS_DEV), 1) // BB
@@ -261,18 +269,18 @@
         (((0,), (0,)), ((), ())),
         preferred_element_type=F32,
     )
-    within = lax.broadcasted_iota(jnp.int32, (ROWS_DEV, COLS), 0) % BB - half * HALF
+    within = lax.broadcasted_iota(jnp.int32, (ROWS_DEV, COLS), 0) % BB - me * PART
     lane = lax.broadcasted_iota(jnp.int32, (ROWS_DEV, COLS), 1)
-    goal = slot_of_row.astype(jnp.int32) * HALF + within + offset
-    spot = jnp.where((goal == lane) & (within >= 0) & (within < HALF), 1.0, 0.0).astype(BF16)
+    goal = slot_of_row.astype(jnp.int32) * PART + within + offset
+    spot = jnp.where((goal == lane) & (within >= 0) & (within < PART), 1.0, 0.0).astype(BF16)
     row = lax.broadcasted_iota(jnp.int32, (N_TB * 8, ROWS_DEV), 0)
     u = uv_ref[0:1, :].astype(F32)
     v = uv_ref[1:2, :].astype(F32)
     value = jnp.where(row % 8 == 0, u, jnp.where(row % 8 == 1, v, 0.0))
     value = jnp.where((row // 8).astype(F32) == tile_of_lane, value, 0.0).astype(BF16)
     out = jnp.dot(value, spot, preferred_element_type=F32)
-    out_ref[:, : SLOTS * HALF, :] = jnp.zeros((N_TB, SLOTS * HALF, COLS), BF16)
-    out_ref[:, SLOTS * HALF :, :] = out.reshape(N_TB, 8, COLS).astype(BF16)
+    out_ref[:, : SLOTS * PART, :] = jnp.zeros((N_TB, SLOTS * PART, COLS), BF16)
+    out_ref[:, SLOTS * PART :, :] = out.reshape(N_TB, 8, COLS).astype(BF16)
     for t in range(N_TB):
         seen_ref[t] = 0
     for b in range(NB):
@@ -298,15 +306,12 @@
 
 def pack_kernel(ids_ref, tile_ref, slot_ref, r0_ref, r1_ref, r2_ref, r3_ref, base_ref, out_ref, stage_ref):
     me = ids_ref[0]
-    half = ids_ref[1]
     out_ref[...] = base_ref[...]
     for x, ref in enumerate((r0_ref, r1_ref, r2_ref, r3_ref)):
-        stage_ref[pl.ds((me ^ x) * (2 * QROWS // BB), 2 * QROWS // BB)] = ref[...].reshape(
-            2 * QROWS // BB, HALF, COLS
-        )
+        stage_ref[pl.ds((me ^ x) * QBLOCKS, QBLOCKS)] = ref[...]
     for b in range(NB):
-        first = pl.multiple_of(slot_ref[b] * HALF, HALF)
-        out_ref[tile_ref[b], pl.ds(first, HALF), :] = stage_ref[2 * b + half]
+        first = pl.multiple_of(slot_ref[b] * PART, PART)
+        out_ref[tile_ref[b], pl.ds(first, PART), :] = stage_ref[b]
 
 
 def pack(ids, tile_ids, slots, rows, base):
@@ -315,7 +320,7 @@
         out_shape=jax.ShapeDtypeStruct((N_TB, SEND_ROWS, COLS), BF16),
         in_specs=[smem(), smem(), smem()] + [vmem()] * 5,
         out_specs=vmem(),
-        scratch_shapes=[pltpu.VMEM((2 * NB, HALF, COLS), BF16)],
+        scratch_shapes=[pltpu.VMEM((NB, PART, COLS), BF16)],
         compiler_params=params(16),
         name="pack",
     )(ids, tile_ids, slots, *rows, base)
@@ -338,47 +343,50 @@
     )(ids, *rows)
 
 
-def grid_kernel(ids_ref, got_ref, keep_ref, give_ref, tab_ref):
-    chip = ids_ref[0] // 2
-    half = ids_ref[1]
-    tiles = N_TB * SLOTS * HALF // 128
+def grid_kernel(other, ids_ref, mine_ref, partner_ref, out_ref, tab_ref, row_ref):
+    chip = (ids_ref[0] // 2) ^ other
+    core = ids_ref[1]
+    tiles = N_TB * SLOTS * PART // 128
     groups = N_TB // tiles
-    coords = got_ref[:, SLOTS * HALF :, :].astype(F32).reshape(tiles, groups, 8, COLS)
-    coords = jnp.sum(coords, axis=1)
     y_pixel = (lax.broadcasted_iota(jnp.int32, (GRID, 1), 0) - GRID // 2).astype(F32)
-    order = lax.broadcasted_iota(jnp.int32, (16, 1), 0)
-    x_pixel = (16 * chip + 8 * ((order // 8) ^ half) + order % 8 - GRID // 2).astype(F32)
+    order = lax.broadcasted_iota(jnp.int32, (8, 1), 0)
+    x_pixel = (16 * chip + 8 * core + order - GRID // 2).astype(F32)
     scale = 1.0 / (2.0 * GRID)
-    for tile in range(tiles):
-        u = coords[tile, 0:1, :] * scale
-        v = coords[tile, 1:2, :] * scale
-        cx, sx = cos_sin_turns(x_pixel * u)
-        cy, sy = cos_sin_turns(y_pixel * v)
-        lanes = slice(tile * 128, (tile + 1) * 128)
-        for x in range(16):
-            a, b = cx[x : x + 1], sx[x : x + 1]
-            tab_ref[x * GRID : (x + 1) * GRID, lanes] = (a * cy - b * sy).astype(BF16)
-            tab_ref[512 + x * GRID : 512 + (x + 1) * GRID, lanes] = (b * cy + a * sy).astype(BF16)
-    rows = got_ref[:, : SLOTS * HALF, :].reshape(N_TB * SLOTS * HALF, COLS)
-    total = jnp.dot(tab_ref[...], rows, preferred_element_type=F32) * float(ROWS_DEV) ** (-0.5)
-    for part in range(2):
-        keep_ref[part] = total[part * 512 : part * 512 + 256]
-        give_ref[part] = total[part * 512 + 256 : part * 512 + 512]
-
-
-def grid_rows(ids, got):
-    return pl.pallas_call(
-        grid_kernel,
-        out_shape=(
-            jax.ShapeDtypeStruct((2, PIX // N_DIR, COLS), F32),
-            jax.ShapeDtypeStruct((2, PIX // N_DIR, COLS), F32),
-        ),
-        in_specs=[smem(), vmem()],
-        out_specs=(vmem(), vmem()),
-        scratch_shapes=[pltpu.VMEM((1024, N_TB * SLOTS * HALF), BF16)],
+    for n, ref in enumerate((mine_ref, partner_ref)):
+        coords = ref[:, SLOTS * PART :, :].astype(F32).reshape(tiles, groups, 8, COLS)
+        coords = jnp.sum(coords, axis=1)
+        for tile in range(tiles):
+            u = coords[tile, 0:1, :] * scale
+            v = coords[tile, 1:2, :] * scale
+            cx, sx = cos_sin_turns(x_pixel * u)
+            cy, sy = cos_sin_turns(y_pixel * v)
+            first = (n * tiles + tile) * 128
+            lanes = slice(first, first + 128)
+            for x in range(8):
+                a, b = cx[x : x + 1], sx[x : x + 1]
+                tab_ref[x * GRID : (x + 1) * GRID, lanes] = (a * cy - b * sy).astype(BF16)
+                tab_ref[256 + x * GRID : 256 + (x + 1) * GRID, lanes] = (b * cy + a * sy).astype(BF16)
+        row_ref[n * tiles * 128 : (n + 1) * tiles * 128, :] = ref[:, : SLOTS * PART, :].reshape(
+            tiles * 128, COLS
+        )
+    total = jnp.dot(tab_ref[...], row_ref[...], preferred_element_type=F32) * float(ROWS_DEV) ** (-0.5)
+    out_ref[...] = total.reshape(2, PIX // N_DIR, COLS)
+
+
+def grid_rows(other, ids, mine, partner):
+    def kernel(*refs):
+        grid_kernel(other, *refs)
+
+    return pl.pallas_call(
+        kernel,
+        out_shape=jax.ShapeDtypeStruct((2, PIX // N_DIR, COLS), F32),
+        in_specs=[smem(), vmem(), vmem()],
+        out_specs=vmem(),
+        scratch_shapes=[pltpu.VMEM((512, 2048), BF16), pltpu.VMEM((2048, COLS), BF16)],
+        cost_estimate=pl.CostEstimate(flops=2 * 10**9, transcendentals=0, bytes_accessed=10**6),
         compiler_params=params(24),
         name="grid",
-    )(ids, got)
+    )(ids, mine, partner)
 
 
 def after(value, done):
@@ -394,7 +402,7 @@
 ):
     me = lax.axis_index("dir")
     station = lax.axis_index("tb")
-    ids = jnp.stack([me, me % 2, (station % 4) * BB]).astype(jnp.int32)
+    ids = jnp.stack([me, me % 2, (station % 8) * (SLOTS * PART)]).astype(jnp.int32)
     lm8, uv8, wide = prepare(peel_order, assignment, comp_lm, uv_coords, spectra)
     (far_a,) = predict((2,), ids, uv8, lm8, wide)
     got_a = swap(far_a, 2)
@@ -402,16 +410,20 @@
     got_b = swap(far_b, 3)
     near, own = predict((1, 0), ids, uv8, lm8, wide)
     got_near = swap(near, 1)
-    rows = peel(ids, visibilities, ridge_weight, (own, got_near, got_a, got_b))
-    gathered = (rows, swap(rows, 1), swap(rows, 2), swap(rows, 3))
+    rows, parts = peel(ids, visibilities, ridge_weight, (own, got_near, got_a, got_b))
     tile_ids = block_tile[:, 0]
     base, slots = label(after(ids, rows), tile_ids, block_tile, uv_coords)
-    send = pack(ids, tile_ids, slots, gathered, base)
+    shared = [parts[0]] + [swap(parts[x], x) for x in range(1, N_DIR)]
+    send = pack(ids, tile_ids, slots, shared, base)
     got = lax.all_to_all(send, "tb", split_axis=0, concat_axis=0, tiled=True)
-    residual = join(after(ids, send), gathered)
-    keep, give = grid_rows(after(ids, residual), got)
-    subgrids = (keep + swap(give, 1))[None]
-    return residual, subgrids
+    late = after(rows, send)
+    residual = join(ids, [late] + [swap(late, x) for x in range(1, N_DIR)])
+    got = after(got, residual)
+    partner = swap(got, 1)
+    give = grid_rows(1, ids, got, partner)
+    moved = swap(give, 2)
+    keep = grid_rows(0, ids, got, partner)
+    return residual, (keep + moved)[None]
 
 
 def solution(mesh):

time: 75.8 us -> 76 us (level)
  waiting for transfers between devices: 22.4 us -> 19.3 us
  starting transfers between devices: 23.5 us -> 26 us
  Pallas kernels: 27.9 us -> 28.8 us
    all_to_all x1, waiting for transfers between devices: 18.3 us -> 4.82 us  [local(): got = lax.all_to_all(send, 'tb', split_axis=0, concat_axis=0, tiled=True)]
    ppermute x7 -> x11, waiting for transfers between devices: 4.11 us -> 14.5 us  [swap(): return lax.ppermute(value, 'dir', [(i, i ^ flip) for i in range(N_DIR)])]
    ppermute x7 -> x11, starting transfers between devices: 10.4 us -> 12.7 us  [swap(): return lax.ppermute(value, 'dir', [(i, i ^ flip) for i in range(N_DIR)])]
    pallas_call x2 -> x3, Pallas kernels: 6.65 us -> 7.62 us  [the longest x2 3.88 us: grid_rows(): pl.pallas_call(kernel, out_shape=jax.ShapeDtypeStruct((2, PIX // N_DIR, C...]
  transfers between devices with their start and end apart: 8 -> 12, of which waited for: 4 -> 6; matrix products, arithmetic and copies ran while one was open for 0% -> 0% of each run, Pallas kernels for 17% -> 20%
where the time goes in v3:
time: 76 us; the launch traced here: 75.7 us
  Pallas kernels  28.8 us (38%)
  starting transfers between devices  26 us (34%)
  waiting for transfers between devices  19.3 us (25%)
  other arithmetic  0.81 us (1%)
  between operations  0.81 us (1%)
    ppermute x11, waiting for transfers between devices, swap(): return lax.ppermute(value, 'dir', [(i, i ^ flip) for i in range(N_DIR)])  14.5 us
    pallas_call x3, Pallas kernels, predict(): pl.pallas_call(kernel, out_shape=tuple((jax.ShapeDtypeStruct((DIR_DEV, QR...  14.1 us
    all_to_all x1, starting transfers between devices, local(): got = lax.all_to_all(send, 'tb', split_axis=0, concat_axis=0, tiled=True)  13.3 us
    ppermute x11, starting transfers between devices, swap(): return lax.ppermute(value, 'dir', [(i, i ^ flip) for i in range(N_DIR)])  12.7 us
    all_to_all x1, waiting for transfers between devices, local(): got = lax.all_to_all(send, 'tb', split_axis=0, concat_axis=0, tiled=True)  4.82 us
    pallas_call x2, Pallas kernels, grid_rows(): pl.pallas_call(kernel, out_shape=jax.ShapeDtypeStruct((2, PIX // N_DIR, C...  3.88 us
    pallas_call x1, Pallas kernels, peel(): pl.pallas_call(peel_kernel, out_shape=(jax.ShapeDtypeStruct((QROWS, COLS)...  3.74 us
    pallas_call x1, Pallas kernels, prepare(): pl.pallas_call(prepare_kernel, out_shape=(jax.ShapeDtypeStruct((8, POOL),...  2.85 us
  transfers between devices with their start and end apart: 12, of which 6 were waited for; matrix products, arithmetic and copies ran while one was open for 0% of the time, Pallas kernels for 20%

profile of v3, /device:TPU:1, one launch (start us, length us, event | category | flops | bytes accessed | tf_op | source)
XLA Modules:
  0.0 75.7 jit_solution(16575836361154582571)
XLA Ops:
  0.7 2.9 %prepare.1 = (bf16[8,3072]{1,0:T(8,128)(2,1)S(1)}, bf16[4,8,256]{2,1,0:T(8,128)(2,1)S(1)}, bf16[12,512,384]{2,1,0:T(8,128)(2,1)S(1)}) custom-call(s32[3]{0:T(128)} %order_hbm.1, s32[1,3072]{1,0:T(1,128)} %bitcast.11, f32[2,3072]{1,0:T(2,128)} %lm_hbm.1, bf16[2,1024]{1,0:T(2,128)(2,1)} %uv_ref.1, bf16[2,3072,128]{2,1,0:T(8,128)(2,1)} %spec_hbm.1), custom_call_target="tpu_custom_call" | custom-call | tf_op jit(solution)/shard_map/prepare/pallas_call | solution.py:115
  3.6 3.9 %predict.5 = bf16[3,256,128]{2,1,0:T(8,128)(2,1)S(1)} custom-call(s32[3]{0:T(128)S(1)} %pad_add_fusion.refs_0_.ids_ref, bf16[4,8,256]{2,1,0:T(8,128)(2,1)S(1)} %get-tuple-element.17.refs_1_, bf16[8,3072]{1,0:T(8,128)(2,1)S(1)} %get-tuple-element.18.refs_2_, bf16[12,512,384]{2,1,0:T(8,128)(2,1)S(1)} %get-tuple-element.19.refs_3_), custom_call_target="tpu_custom_call" | custom-call | flops 2415919104 | bytes 4915200 | tf_op jit(solution)/shard_map/predict/pallas_call | solution.py:175
  7.5 2.7 %collective-permute-start.2 = (bf16[3,256,128]{2,1,0:T(8,128)(2,1)S(1)}, bf16[3,256,128]{2,1,0:T(8,128)(2,1)S(1)}, u32[]{:S(2)}, u32[]{:S(2)}) collective-permute-start(bf16[3,256,128]{2,1,0:T(8,128)(2,1)S(1)} %predict.5), channel_id=1, source_target_pairs={{0,192},{64,128},{128,64},{192,0},{1,193},{65,129},{129,65},{193,1... | collective-permute-start | bytes 589832 | tf_op jit(solution)/shard_map/ppermute | solution.py:397
  10.2 3.9 %predict.4 = bf16[3,256,128]{2,1,0:T(8,128)(2,1)S(1)} custom-call(s32[3]{0:T(128)S(1)} %pad_add_fusion.refs_0_.ids_ref, bf16[4,8,256]{2,1,0:T(8,128)(2,1)S(1)} %get-tuple-element.17.refs_1_, bf16[8,3072]{1,0:T(8,128)(2,1)S(1)} %get-tuple-element.18.refs_2_, bf16[12,512,384]{2,1,0:T(8,128)(2,1)S(1)} %get-tuple-element.19.refs_3_), custom_call_target="tpu_custom_call" | custom-call | flops 2415919104 | bytes 4915200 | tf_op jit(solution)/shard_map/predict/pallas_call | solution.py:175
  14.2 2.3 %collective-permute-start.1 = (bf16[3,256,128]{2,1,0:T(8,128)(2,1)S(1)}, bf16[3,256,128]{2,1,0:T(8,128)(2,1)S(1)}, u32[]{:S(2)}, u32[]{:S(2)}) collective-permute-start(bf16[3,256,128]{2,1,0:T(8,128)(2,1)S(1)} %predict.4), channel_id=1, source_target_pairs={{0,128},{64,192},{128,0},{192,64},{1,129},{65,193},{129,1},{193,65... | collective-permute-start | bytes 589832 | tf_op jit(solution)/shard_map/ppermute | solution.py:397
  16.4 6.2 %predict.3 = (bf16[3,256,128]{2,1,0:T(8,128)(2,1)S(1)}, bf16[3,256,128]{2,1,0:T(8,128)(2,1)S(1)}) custom-call(s32[3]{0:T(128)S(1)} %pad_add_fusion.refs_0_.ids_ref, bf16[4,8,256]{2,1,0:T(8,128)(2,1)S(1)} %get-tuple-element.17.refs_1_, bf16[8,3072]{1,0:T(8,128)(2,1)S(1)} %get-tuple-element.18.refs_2_, bf16[12,512,384]{2,1,0:T(8,128)(2,1)S(1)} %get-tuple-element.19.refs_3_), custom_call_target="tpu_custom_call" | custom-call | flops 4831838208 | bytes 5111808 | tf_op jit(solution)/shard_map/predict/pallas_call | solution.py:175
  22.8 1.4 %collective-permute-done.m1_ref = bf16[3,256,128]{2,1,0:T(8,128)(2,1)S(1)} collective-permute-done((bf16[3,256,128]{2,1,0:T(8,128)(2,1)S(1)}, bf16[3,256,128]{2,1,0:T(8,128)(2,1)S(1)}, u32[]{:S(2)}, u32[]{:S(2)}) %collective-permute-start) | collective-permute-done | bytes 196640 | tf_op jit(solution)/shard_map/ppermute | solution.py:397
  24.2 3.7 %peel.1 = (bf16[256,128]{1,0:T(8,128)(2,1)S(1)}, bf16[8,8,128]{2,1,0:T(8,128)(2,1)S(1)}, bf16[8,8,128]{2,1,0:T(8,128)(2,1)S(1)}, bf16[8,8,128]{2,1,0:T(8,128)(2,1)S(1)}, bf16[8,8,128]{2,1,0:T(8,128)(2,1)S(1)}) custom-call(s32[3]{0:T(128)S(1)} %pad_add_fusion.refs_0_.ids_ref, bf16[1024,128]{1,0:T(8,128)(2,1)S(1)} %copy-done, f32[1,128]{1,0:T(1,128)S(1)} %bitcast.10, ...), custom_call_target="tpu_custom_call" | custom-call | tf_op jit(solution)/shard_map/peel/pallas_call | solution.py:238
  28.5 1.7 %collective-permute-start.5 = (bf16[8,8,128]{2,1,0:T(8,128)(2,1)S(1)}, bf16[8,8,128]{2,1,0:T(8,128)(2,1)S(1)}, u32[]{:S(2)}, u32[]{:S(2)}) collective-permute-start(bf16[8,8,128]{2,1,0:T(8,128)(2,1)S(1)} %get-tuple-element.28), channel_id=1, source_target_pairs={{0,192},{64,128},{128,64},{192,0},{1,193},{65,129},{129,65},{193,1... | collective-permute-start | bytes 49160 | tf_op jit(solution)/shard_map/ppermute | solution.py:397
  30.3 1.6 %label.1 = (bf16[64,24,128]{2,1,0:T(8,128)(2,1)S(1)}, s32[32]{0:T(128)S(1)}) custom-call(s32[3]{0:T(128)S(1)} %pad_add_fusion.refs_0_.ids_ref, s32[32]{0:T(128)S(1)} %bitcast.8, s32[32,1]{1,0:T(8,128)S(1)} %copy.10.tile_ref, bf16[2,1024]{1,0:T(2,128)(2,1)S(1)} %copy-done.1), custom_call_target="tpu_custom_call" | custom-call | tf_op jit(solution)/shard_map/label/pallas_call | solution.py:293
  31.9 1.4 %pack.1 = bf16[64,24,128]{2,1,0:T(8,128)(2,1)} custom-call(s32[3]{0:T(128)S(1)} %pad_add_fusion.refs_0_.ids_ref, s32[32]{0:T(128)S(1)} %bitcast.9, s32[32]{0:T(128)S(1)} %get-tuple-element.24.slot_ref, bf16[8,8,128]{2,1,0:T(8,128)(2,1)S(1)} %get-tuple-element.25.r0_ref, bf16[8,8,128]{2,1,0:T(8,128)(2,1)S(1)} %collective-permute-done.3.r1_ref, ...), custom_call_target="tpu_custom_call" | custom-call | tf_op jit(solution)/shard_map/pack/pallas_call | solution.py:318
  33.3 13.3 %all-to-all-start = ((bf16[64,24,128]{2,1,0:T(8,128)(2,1)}), bf16[64,24,128]{2,1,0:T(8,128)(2,1)S(1)}, u32[]{:S(2)}, u32[]{:S(2)}) async-start(bf16[64,24,128]{2,1,0:T(8,128)(2,1)} %pack.1), calls=%async_computation | async-start | bytes 786432 | tf_op jit(solution)/shard_map/all_to_all | solution.py:418
  46.6 0.8 %collective-permute-start.6 = (bf16[256,128]{1,0:T(8,128)(2,1)S(1)}, bf16[256,128]{1,0:T(8,128)(2,1)S(1)}, u32[]{:S(2)}, u32[]{:S(2)}) collective-permute-start(bf16[256,128]{1,0:T(8,128)(2,1)S(1)} %get-tuple-element.30.r0_ref), channel_id=1, source_target_pairs={{0,64},{64,0},{128,192},{192,128},{1,65},{65,1},{129,193},{193,129... | collective-permute-start | bytes 196616 | tf_op jit(solution)/shard_map/ppermute | solution.py:397
  47.4 1.7 %collective-permute-start.8 = (bf16[256,128]{1,0:T(8,128)(2,1)S(1)}, bf16[256,128]{1,0:T(8,128)(2,1)S(1)}, u32[]{:S(2)}, u32[]{:S(2)}) collective-permute-start(bf16[256,128]{1,0:T(8,128)(2,1)S(1)} %get-tuple-element.30.r0_ref), channel_id=1, source_target_pairs={{0,192},{64,128},{128,64},{192,0},{1,193},{65,129},{129,65},{193,1... | collective-permute-start | bytes 196616 | tf_op jit(solution)/shard_map/ppermute | solution.py:397
  49.1 3.0 %collective-permute-done.7.r2_ref = bf16[256,128]{1,0:T(8,128)(2,1)S(1)} collective-permute-done((bf16[256,128]{1,0:T(8,128)(2,1)S(1)}, bf16[256,128]{1,0:T(8,128)(2,1)S(1)}, u32[]{:S(2)}, u32[]{:S(2)}) %collective-permute-start.7) | collective-permute-done | bytes 65568 | tf_op jit(solution)/shard_map/ppermute | solution.py:397
  52.1 3.1 %collective-permute-done.8.r3_ref = bf16[256,128]{1,0:T(8,128)(2,1)S(1)} collective-permute-done((bf16[256,128]{1,0:T(8,128)(2,1)S(1)}, bf16[256,128]{1,0:T(8,128)(2,1)S(1)}, u32[]{:S(2)}, u32[]{:S(2)}) %collective-permute-start.8) | collective-permute-done | bytes 65568 | tf_op jit(solution)/shard_map/ppermute | solution.py:397
  55.2 1.3 %join.1 = bf16[1024,128]{1,0:T(8,128)(2,1)} custom-call(s32[3]{0:T(128)S(1)} %pad_add_fusion.refs_0_.ids_ref, bf16[256,128]{1,0:T(8,128)(2,1)S(1)} %get-tuple-element.30.r0_ref, bf16[256,128]{1,0:T(8,128)(2,1)S(1)} %collective-permute-done.6.r1_ref, bf16[256,128]{1,0:T(8,128)(2,1)S(1)} %collective-permute-done.7.r2_ref, ...), custom_call_target="tpu_custom_call" | custom-call | tf_op jit(solution)/shard_map/join/pallas_call | solution.py:336
  56.5 4.8 %all-to-all-done.refs_1_ = bf16[64,24,128]{2,1,0:T(8,128)(2,1)S(1)} async-done(((bf16[64,24,128]{2,1,0:T(8,128)(2,1)}), bf16[64,24,128]{2,1,0:T(8,128)(2,1)S(1)}, u32[]{:S(2)}, u32[]{:S(2)}) %all-to-all-start) | async-done | bytes 393248 | tf_op jit(solution)/shard_map/all_to_all | solution.py:418
  61.3 2.8 %collective-permute-start.9 = (bf16[64,24,128]{2,1,0:T(8,128)(2,1)S(1)}, bf16[64,24,128]{2,1,0:T(8,128)(2,1)S(1)}, u32[]{:S(2)}, u32[]{:S(2)}) collective-permute-start(bf16[64,24,128]{2,1,0:T(8,128)(2,1)S(1)} %all-to-all-done.refs_1_), channel_id=1, source_target_pairs={{0,64},{64,0},{128,192},{192,128},{1,65},{65,1},{129,193},{193,129... | collective-permute-start | bytes 1179656 | tf_op jit(solution)/shard_map/ppermute | solution.py:397
  64.1 1.3 %collective-permute-done.9.refs_2_ = bf16[64,24,128]{2,1,0:T(8,128)(2,1)S(1)} collective-permute-done((bf16[64,24,128]{2,1,0:T(8,128)(2,1)S(1)}, bf16[64,24,128]{2,1,0:T(8,128)(2,1)S(1)}, u32[]{:S(2)}, u32[]{:S(2)}) %collective-permute-start.9) | collective-permute-done | bytes 393248 | tf_op jit(solution)/shard_map/ppermute | solution.py:397
  65.5 1.9 %grid.3 = f32[2,256,128]{2,1,0:T(8,128)S(1)} custom-call(s32[3]{0:T(128)S(1)} %pad_add_fusion.refs_0_.ids_ref, bf16[64,24,128]{2,1,0:T(8,128)(2,1)S(1)} %all-to-all-done.refs_1_, bf16[64,24,128]{2,1,0:T(8,128)(2,1)S(1)} %collective-permute-done.9.refs_2_), custom_call_target="tpu_custom_call" | custom-call | flops 2000000000 | bytes 1000000 | tf_op jit(solution)/shard_map/grid/pallas_call | solution.py:380
  67.5 1.9 %grid.2 = f32[2,256,128]{2,1,0:T(8,128)S(1)} custom-call(s32[3]{0:T(128)S(1)} %pad_add_fusion.refs_0_.ids_ref, bf16[64,24,128]{2,1,0:T(8,128)(2,1)S(1)} %all-to-all-done.refs_1_, bf16[64,24,128]{2,1,0:T(8,128)(2,1)S(1)} %collective-permute-done.9.refs_2_), custom_call_target="tpu_custom_call" | custom-call | flops 2000000000 | bytes 1000000 | tf_op jit(solution)/shard_map/grid/pallas_call | solution.py:380
  69.5 5.6 %collective-permute-done.10 = f32[2,256,128]{2,1,0:T(8,128)S(1)} collective-permute-done((f32[2,256,128]{2,1,0:T(8,128)S(1)}, f32[2,256,128]{2,1,0:T(8,128)S(1)}, u32[]{:S(2)}, u32[]{:S(2)}) %collective-permute-start.10) | collective-permute-done | bytes 262176 | tf_op jit(solution)/shard_map/ppermute | solution.py:397
  75.0 0.7 add_bitcast_fusion
  (21 shorter events, 0.9 us)
Async XLA Ops:
  7.5 15.3 %collective-permute-start.2 = (bf16[3,256,128]{2,1,0:T(8,128)(2,1)S(1)}, bf16[3,256,128]{2,1,0:T(8,128)(2,1)S(1)}, u32[]{:S(2)}, u32[]{:S(2)}) collective-permute-start(bf16[3,256,128]{2,1,0:T(8,128)(2,1)S(1)} %predict.5), channel_id=1, source_target_pairs={{0,192},{64,128},{128,64},{192,0},{1,193},{65,129},{129,65},{193,1... | collective-permute-start | bytes 589832 | tf_op jit(solution)/shard_map/ppermute | solution.py:397
  14.1 10.1 %copy-start = (bf16[1024,128]{1,0:T(8,128)(2,1)S(1)}, bf16[1024,128]{1,0:T(8,128)(2,1)}, u32[]{:S(2)}) copy-start(bf16[1024,128]{1,0:T(8,128)(2,1)} %vis_ref.1) | copy-start | bytes 786436
  14.1 10.1 %copy-start.3 = (f32[128]{0:T(128)S(1)}, f32[128]{0:T(128)}, u32[]{:S(2)}) copy-start(f32[128]{0:T(128)} %param.12) | copy-start | bytes 1540
  14.1 16.0 %copy-start.2 = (s32[32,1]{0,1:T(1,128)S(1)}, s32[32,1]{0,1:T(1,128)}, u32[]{:S(2)}) copy-start(s32[32,1]{0,1:T(1,128)} %param.15) | copy-start | bytes 388
  14.2 16.1 %copy-start.1 = (bf16[2,1024]{1,0:T(2,128)(2,1)S(1)}, bf16[2,1024]{1,0:T(2,128)(2,1)}, u32[]{:S(2)}) copy-start(bf16[2,1024]{1,0:T(2,128)(2,1)} %uv_ref.1) | copy-start | bytes 12292
  14.2 8.6 %collective-permute-start.1 = (bf16[3,256,128]{2,1,0:T(8,128)(2,1)S(1)}, bf16[3,256,128]{2,1,0:T(8,128)(2,1)S(1)}, u32[]{:S(2)}, u32[]{:S(2)}) collective-permute-start(bf16[3,256,128]{2,1,0:T(8,128)(2,1)S(1)} %predict.4), channel_id=1, source_target_pairs={{0,128},{64,192},{128,0},{192,64},{1,129},{65,193},{129,1},{193,65... | collective-permute-start | bytes 589832 | tf_op jit(solution)/shard_map/ppermute | solution.py:397
  22.7 1.5 %collective-permute-start = (bf16[3,256,128]{2,1,0:T(8,128)(2,1)S(1)}, bf16[3,256,128]{2,1,0:T(8,128)(2,1)S(1)}, u32[]{:S(2)}, u32[]{:S(2)}) collective-permute-start(bf16[3,256,128]{2,1,0:T(8,128)(2,1)S(1)} %get-tuple-element.21), channel_id=1, source_target_pairs={{0,64},{64,0},{128,192},{192,128},{1,65},{65,1},{129,193},{193,129... | collective-permute-start | bytes 589832 | tf_op jit(solution)/shard_map/ppermute | solution.py:397
  28.0 3.9 %collective-permute-start.3 = (bf16[8,8,128]{2,1,0:T(8,128)(2,1)S(1)}, bf16[8,8,128]{2,1,0:T(8,128)(2,1)S(1)}, u32[]{:S(2)}, u32[]{:S(2)}) collective-permute-start(bf16[8,8,128]{2,1,0:T(8,128)(2,1)S(1)} %get-tuple-element.26), channel_id=1, source_target_pairs={{0,64},{64,0},{128,192},{192,128},{1,65},{65,1},{129,193},{193,129... | collective-permute-start | bytes 49160 | tf_op jit(solution)/shard_map/ppermute | solution.py:397
  28.2 3.7 %collective-permute-start.4 = (bf16[8,8,128]{2,1,0:T(8,128)(2,1)S(1)}, bf16[8,8,128]{2,1,0:T(8,128)(2,1)S(1)}, u32[]{:S(2)}, u32[]{:S(2)}) collective-permute-start(bf16[8,8,128]{2,1,0:T(8,128)(2,1)S(1)} %get-tuple-element.27), channel_id=1, source_target_pairs={{0,128},{64,192},{128,0},{192,64},{1,129},{65,193},{129,1},{193,65... | collective-permute-start | bytes 49160 | tf_op jit(solution)/shard_map/ppermute | solution.py:397
  28.5 3.4 %collective-permute-start.5 = (bf16[8,8,128]{2,1,0:T(8,128)(2,1)S(1)}, bf16[8,8,128]{2,1,0:T(8,128)(2,1)S(1)}, u32[]{:S(2)}, u32[]{:S(2)}) collective-permute-start(bf16[8,8,128]{2,1,0:T(8,128)(2,1)S(1)} %get-tuple-element.28), channel_id=1, source_target_pairs={{0,192},{64,128},{128,64},{192,0},{1,193},{65,129},{129,65},{193,1... | collective-permute-start | bytes 49160 | tf_op jit(solution)/shard_map/ppermute | solution.py:397
  33.3 28.0 %all-to-all-start = ((bf16[64,24,128]{2,1,0:T(8,128)(2,1)}), bf16[64,24,128]{2,1,0:T(8,128)(2,1)S(1)}, u32[]{:S(2)}, u32[]{:S(2)}) async-start(bf16[64,24,128]{2,1,0:T(8,128)(2,1)} %pack.1), calls=%async_computation | async-start | bytes 786432 | tf_op jit(solution)/shard_map/all_to_all | solution.py:418
  46.6 2.5 %collective-permute-start.6 = (bf16[256,128]{1,0:T(8,128)(2,1)S(1)}, bf16[256,128]{1,0:T(8,128)(2,1)S(1)}, u32[]{:S(2)}, u32[]{:S(2)}) collective-permute-start(bf16[256,128]{1,0:T(8,128)(2,1)S(1)} %get-tuple-element.30.r0_ref), channel_id=1, source_target_pairs={{0,64},{64,0},{128,192},{192,128},{1,65},{65,1},{129,193},{193,129... | collective-permute-start | bytes 196616 | tf_op jit(solution)/shard_map/ppermute | solution.py:397
  47.4 4.7 %collective-permute-start.7 = (bf16[256,128]{1,0:T(8,128)(2,1)S(1)}, bf16[256,128]{1,0:T(8,128)(2,1)S(1)}, u32[]{:S(2)}, u32[]{:S(2)}) collective-permute-start(bf16[256,128]{1,0:T(8,128)(2,1)S(1)} %get-tuple-element.30.r0_ref), channel_id=1, source_target_pairs={{0,128},{64,192},{128,0},{192,64},{1,129},{65,193},{129,1},{193,65... | collective-permute-start | bytes 196616 | tf_op jit(solution)/shard_map/ppermute | solution.py:397
  47.4 7.8 %collective-permute-start.8 = (bf16[256,128]{1,0:T(8,128)(2,1)S(1)}, bf16[256,128]{1,0:T(8,128)(2,1)S(1)}, u32[]{:S(2)}, u32[]{:S(2)}) collective-permute-start(bf16[256,128]{1,0:T(8,128)(2,1)S(1)} %get-tuple-element.30.r0_ref), channel_id=1, source_target_pairs={{0,192},{64,128},{128,64},{192,0},{1,193},{65,129},{129,65},{193,1... | collective-permute-start | bytes 196616 | tf_op jit(solution)/shard_map/ppermute | solution.py:397
  61.3 4.2 %collective-permute-start.9 = (bf16[64,24,128]{2,1,0:T(8,128)(2,1)S(1)}, bf16[64,24,128]{2,1,0:T(8,128)(2,1)S(1)}, u32[]{:S(2)}, u32[]{:S(2)}) collective-permute-start(bf16[64,24,128]{2,1,0:T(8,128)(2,1)S(1)} %all-to-all-done.refs_1_), channel_id=1, source_target_pairs={{0,64},{64,0},{128,192},{192,128},{1,65},{65,1},{129,193},{193,129... | collective-permute-start | bytes 1179656 | tf_op jit(solution)/shard_map/ppermute | solution.py:397
  67.4 7.6 %collective-permute-start.10 = (f32[2,256,128]{2,1,0:T(8,128)S(1)}, f32[2,256,128]{2,1,0:T(8,128)S(1)}, u32[]{:S(2)}, u32[]{:S(2)}) collective-permute-start(f32[2,256,128]{2,1,0:T(8,128)S(1)} %grid.3), channel_id=1, source_target_pairs={{0,128},{64,192},{128,0},{192,64},{1,129},{65,193},{129,1},{193,65... | collective-permute-start | bytes 786440 | tf_op jit(solution)/shard_map/ppermute | solution.py:397

commit v4 on v2

--- a/solution.py
+++ b/solution.py
@@ -19,12 +19,13 @@
 NB = 32
 SLOTS = 2
 QROWS = ROWS_DEV // N_DIR
-HALF = BB // 2
+PART = BB // 2
 POOL = DIR_DEV * NCOMP
 WIDE = DIR_DEV * COLS
 CHUNK = 256
 NCHUNK = POOL // CHUNK
-SEND_ROWS = SLOTS * HALF + 8
+SEND_ROWS = SLOTS * PART + 8
+QBLOCKS = QROWS // BB
 
 F32 = jnp.float32
 BF16 = jnp.bfloat16
@@ -195,7 +196,8 @@
     return jnp.sum(value.reshape(QROWS // GB, GB, COLS), axis=1)
 
 
-def peel_kernel(ids_ref, vis_ref, ridge_ref, m0_ref, m1_ref, m2_ref, m3_ref, out_ref, model_ref, inv_ref):
+def peel_kernel(ids_ref, vis_ref, ridge_ref, m0_ref, m1_ref, m2_ref, m3_ref, out_ref, *rest):
+    part_refs, (model_ref, inv_ref, part_ref) = rest[:N_DIR], rest[N_DIR:]
     me = ids_ref[0]
     ridge = ridge_ref[...]
     for x, ref in enumerate((m0_ref, m1_ref, m2_ref, m3_ref)):
@@ -227,21 +229,27 @@
         if (j + 1) % DIR_DEV == 0:
             remains = remains.astype(BF16).astype(F32)
     out_ref[...] = remains.astype(BF16)
+    part_ref[...] = remains.reshape(QBLOCKS, 2, PART, COLS)
+    for x in range(N_DIR):
+        part_refs[x][...] = part_ref[:, (me ^ x) & 1].astype(BF16)
 
 
 def peel(ids, visibilities, ridge_weight, models):
-    return pl.pallas_call(
+    out = pl.pallas_call(
         peel_kernel,
-        out_shape=jax.ShapeDtypeStruct((QROWS, COLS), BF16),
+        out_shape=(jax.ShapeDtypeStruct((QROWS, COLS), BF16),)
+        + (jax.ShapeDtypeStruct((QBLOCKS, PART, COLS), BF16),) * N_DIR,
         in_specs=[smem()] + [vmem()] * 6,
-        out_specs=vmem(),
+        out_specs=(vmem(),) * (1 + N_DIR),
         scratch_shapes=[
             pltpu.VMEM((N_DIR * DIR_DEV, QROWS, COLS), F32),
             pltpu.VMEM((N_DIR * DIR_DEV, QROWS // GB, COLS), F32),
+            pltpu.VMEM((QBLOCKS, 2, PART, COLS), F32),
         ],
         compiler_params=params(16),
         name="peel",
     )(ids, visibilities, ridge_weight.reshape(1, COLS), *models)
+    return out[0], out[1:]
 
 
 def label_kernel(ids_ref, tile_id_ref, tile_ref, uv_ref, out_ref, slot_ref, seen_ref):
@@ -261,18 +269,18 @@
         (((0,), (0,)), ((), ())),
         preferred_element_type=F32,
     )
-    within = lax.broadcasted_iota(jnp.int32, (ROWS_DEV, COLS), 0) % BB - half * HALF
+    within = lax.broadcasted_iota(jnp.int32, (ROWS_DEV, COLS), 0) % BB - half * PART
     lane = lax.broadcasted_iota(jnp.int32, (ROWS_DEV, COLS), 1)
-    goal = slot_of_row.astype(jnp.int32) * HALF + within + offset
-    spot = jnp.where((goal == lane) & (within >= 0) & (within < HALF), 1.0, 0.0).astype(BF16)
+    goal = slot_of_row.astype(jnp.int32) * PART + within + offset
+    spot = jnp.where((goal == lane) & (within >= 0) & (within < PART), 1.0, 0.0).astype(BF16)
     row = lax.broadcasted_iota(jnp.int32, (N_TB * 8, ROWS_DEV), 0)
     u = uv_ref[0:1, :].astype(F32)
     v = uv_ref[1:2, :].astype(F32)
     value = jnp.where(row % 8 == 0, u, jnp.where(row % 8 == 1, v, 0.0))
     value = jnp.where((row // 8).astype(F32) == tile_of_lane, value, 0.0).astype(BF16)
     out = jnp.dot(value, spot, preferred_element_type=F32)
-    out_ref[:, : SLOTS * HALF, :] = jnp.zeros((N_TB, SLOTS * HALF, COLS), BF16)
-    out_ref[:, SLOTS * HALF :, :] = out.reshape(N_TB, 8, COLS).astype(BF16)
+    out_ref[:, : SLOTS * PART, :] = jnp.zeros((N_TB, SLOTS * PART, COLS), BF16)
+    out_ref[:, SLOTS * PART :, :] = out.reshape(N_TB, 8, COLS).astype(BF16)
     for t in range(N_TB):
         seen_ref[t] = 0
     for b in range(NB):
@@ -298,15 +306,12 @@
 
 def pack_kernel(ids_ref, tile_ref, slot_ref, r0_ref, r1_ref, r2_ref, r3_ref, base_ref, out_ref, stage_ref):
     me = ids_ref[0]
-    half = ids_ref[1]
     out_ref[...] = base_ref[...]
     for x, ref in enumerate((r0_ref, r1_ref, r2_ref, r3_ref)):
-        stage_ref[pl.ds((me ^ x) * (2 * QROWS // BB), 2 * QROWS // BB)] = ref[...].reshape(
-            2 * QROWS // BB, HALF, COLS
-        )
+        stage_ref[pl.ds((me ^ x) * QBLOCKS, QBLOCKS)] = ref[...]
     for b in range(NB):
-        first = pl.multiple_of(slot_ref[b] * HALF, HALF)
-        out_ref[tile_ref[b], pl.ds(first, HALF), :] = stage_ref[2 * b + half]
+        first = pl.multiple_of(slot_ref[b] * PART, PART)
+        out_ref[tile_ref[b], pl.ds(first, PART), :] = stage_ref[b]
 
 
 def pack(ids, tile_ids, slots, rows, base):
@@ -315,7 +320,7 @@
         out_shape=jax.ShapeDtypeStruct((N_TB, SEND_ROWS, COLS), BF16),
         in_specs=[smem(), smem(), smem()] + [vmem()] * 5,
         out_specs=vmem(),
-        scratch_shapes=[pltpu.VMEM((2 * NB, HALF, COLS), BF16)],
+        scratch_shapes=[pltpu.VMEM((NB, PART, COLS), BF16)],
         compiler_params=params(16),
         name="pack",
     )(ids, tile_ids, slots, *rows, base)
@@ -341,9 +346,9 @@
 def grid_kernel(ids_ref, got_ref, keep_ref, give_ref, tab_ref):
     chip = ids_ref[0] // 2
     half = ids_ref[1]
-    tiles = N_TB * SLOTS * HALF // 128
+    tiles = N_TB * SLOTS * PART // 128
     groups = N_TB // tiles
-    coords = got_ref[:, SLOTS * HALF :, :].astype(F32).reshape(tiles, groups, 8, COLS)
+    coords = got_ref[:, SLOTS * PART :, :].astype(F32).reshape(tiles, groups, 8, COLS)
     coords = jnp.sum(coords, axis=1)
     y_pixel = (lax.broadcasted_iota(jnp.int32, (GRID, 1), 0) - GRID // 2).astype(F32)
     order = lax.broadcasted_iota(jnp.int32, (16, 1), 0)
@@ -359,7 +364,7 @@
             a, b = cx[x : x + 1], sx[x : x + 1]
             tab_ref[x * GRID : (x + 1) * GRID, lanes] = (a * cy - b * sy).astype(BF16)
             tab_ref[512 + x * GRID : 512 + (x + 1) * GRID, lanes] = (b * cy + a * sy).astype(BF16)
-    rows = got_ref[:, : SLOTS * HALF, :].reshape(N_TB * SLOTS * HALF, COLS)
+    rows = got_ref[:, : SLOTS * PART, :].reshape(N_TB * SLOTS * PART, COLS)
     total = jnp.dot(tab_ref[...], rows, preferred_element_type=F32) * float(ROWS_DEV) ** (-0.5)
     for part in range(2):
         keep_ref[part] = total[part * 512 : part * 512 + 256]
@@ -375,7 +380,7 @@
         ),
         in_specs=[smem(), vmem()],
         out_specs=(vmem(), vmem()),
-        scratch_shapes=[pltpu.VMEM((1024, N_TB * SLOTS * HALF), BF16)],
+        scratch_shapes=[pltpu.VMEM((1024, N_TB * SLOTS * PART), BF16)],
         compiler_params=params(24),
         name="grid",
     )(ids, got)
@@ -394,24 +399,22 @@
 ):
     me = lax.axis_index("dir")
     station = lax.axis_index("tb")
-    ids = jnp.stack([me, me % 2, (station % 4) * BB]).astype(jnp.int32)
+    ids = jnp.stack([me, me % 2, (station % 4) * (SLOTS * PART)]).astype(jnp.int32)
     lm8, uv8, wide = prepare(peel_order, assignment, comp_lm, uv_coords, spectra)
-    (far_a,) = predict((2,), ids, uv8, lm8, wide)
-    got_a = swap(far_a, 2)
-    (far_b,) = predict((3,), ids, uv8, lm8, wide)
-    got_b = swap(far_b, 3)
+    far_a, far_b = predict((2, 3), ids, uv8, lm8, wide)
+    got_a, got_b = swap(far_a, 2), swap(far_b, 3)
     near, own = predict((1, 0), ids, uv8, lm8, wide)
     got_near = swap(near, 1)
-    rows = peel(ids, visibilities, ridge_weight, (own, got_near, got_a, got_b))
-    gathered = (rows, swap(rows, 1), swap(rows, 2), swap(rows, 3))
     tile_ids = block_tile[:, 0]
-    base, slots = label(after(ids, rows), tile_ids, block_tile, uv_coords)
-    send = pack(ids, tile_ids, slots, gathered, base)
+    base, slots = label(after(ids, own), tile_ids, block_tile, uv_coords)
+    rows, parts = peel(after(ids, slots), visibilities, ridge_weight, (own, got_near, got_a, got_b))
+    shared = [parts[0]] + [swap(parts[x], x) for x in range(1, N_DIR)]
+    send = pack(ids, tile_ids, slots, shared, base)
     got = lax.all_to_all(send, "tb", split_axis=0, concat_axis=0, tiled=True)
-    residual = join(after(ids, send), gathered)
+    late = after(rows, send)
+    residual = join(ids, [late] + [swap(late, x) for x in range(1, N_DIR)])
     keep, give = grid_rows(after(ids, residual), got)
-    subgrids = (keep + swap(give, 1))[None]
-    return residual, subgrids
+    return residual, (keep + swap(give, 1))[None]
 
 
 def solution(mesh):

time: 75.8 us -> 74.1 us (0.978)
  starting transfers between devices: 23.5 us -> 26.6 us
  waiting for transfers between devices: 22.4 us -> 19.3 us
  Pallas kernels: 27.9 us -> 26.3 us
    all_to_all x1, waiting for transfers between devices: 18.3 us -> 9.84 us  [local(): got = lax.all_to_all(send, 'tb', split_axis=0, concat_axis=0, tiled=True)]
    ppermute x7 -> x10, waiting for transfers between devices: 4.11 us -> 9.48 us  [swap(): return lax.ppermute(value, 'dir', [(i, i ^ flip) for i in range(N_DIR)])]
    ppermute x7 -> x10, starting transfers between devices: 10.4 us -> 13.3 us  [swap(): return lax.ppermute(value, 'dir', [(i, i ^ flip) for i in range(N_DIR)])]
    pallas_call x3 -> x2, Pallas kernels: 14.1 us -> 12.4 us  [predict(): pl.pallas_call(kernel, out_shape=tuple((jax.ShapeDtypeStruct((DIR_DEV, QR...]
  transfers between devices with their start and end apart: 8 -> 11, of which waited for: 4 -> 6; matrix products, arithmetic and copies ran while one was open for 0% -> 0% of each run, Pallas kernels for 17% -> 12%
where the time goes in v4:
time: 74.1 us; the launch traced here: 73.9 us
  starting transfers between devices  26.6 us (36%)
  Pallas kernels  26.3 us (35%)
  waiting for transfers between devices  19.3 us (26%)
  other arithmetic  0.81 us (1%)
  between operations  0.77 us (1%)
    ppermute x10, starting transfers between devices, swap(): return lax.ppermute(value, 'dir', [(i, i ^ flip) for i in range(N_DIR)])  13.3 us
    all_to_all x1, starting transfers between devices, local(): got = lax.all_to_all(send, 'tb', split_axis=0, concat_axis=0, tiled=True)  13.3 us
    pallas_call x2, Pallas kernels, predict(): pl.pallas_call(kernel, out_shape=tuple((jax.ShapeDtypeStruct((DIR_DEV, QR...  12.4 us
    all_to_all x1, waiting for transfers between devices, local(): got = lax.all_to_all(send, 'tb', split_axis=0, concat_axis=0, tiled=True)  9.84 us
    ppermute x10, waiting for transfers between devices, swap(): return lax.ppermute(value, 'dir', [(i, i ^ flip) for i in range(N_DIR)])  9.48 us
    pallas_call x1, Pallas kernels, peel(): pl.pallas_call(peel_kernel, out_shape=(jax.ShapeDtypeStruct((QROWS, COLS)...  3.74 us
    pallas_call x1, Pallas kernels, grid_rows(): pl.pallas_call(grid_kernel, out_shape=(jax.ShapeDtypeStruct((2, PIX // N_...  2.94 us
    pallas_call x1, Pallas kernels, prepare(): pl.pallas_call(prepare_kernel, out_shape=(jax.ShapeDtypeStruct((8, POOL),...  2.85 us
  transfers between devices with their start and end apart: 11, of which 6 were waited for; matrix products, arithmetic and copies ran while one was open for 0% of the time, Pallas kernels for 12%

profile of v4, /device:TPU:1, one launch (start us, length us, event | category | flops | bytes accessed | tf_op | source)
XLA Modules:
  0.0 73.9 jit_solution(2856496410034423201)
XLA Ops:
  0.7 2.9 %prepare.1 = (bf16[8,3072]{1,0:T(8,128)(2,1)S(1)}, bf16[4,8,256]{2,1,0:T(8,128)(2,1)S(1)}, bf16[12,512,384]{2,1,0:T(8,128)(2,1)S(1)}) custom-call(s32[3]{0:T(128)} %order_hbm.1, s32[1,3072]{1,0:T(1,128)} %bitcast.11, f32[2,3072]{1,0:T(2,128)} %lm_hbm.1, bf16[2,1024]{1,0:T(2,128)(2,1)} %uv_ref.1, bf16[2,3072,128]{2,1,0:T(8,128)(2,1)} %spec_hbm.1), custom_call_target="tpu_custom_call" | custom-call | tf_op jit(solution)/shard_map/prepare/pallas_call | solution.py:115
  3.6 6.2 %predict.3 = (bf16[3,256,128]{2,1,0:T(8,128)(2,1)S(1)}, bf16[3,256,128]{2,1,0:T(8,128)(2,1)S(1)}) custom-call(s32[3]{0:T(128)S(1)} %pad_add_fusion.refs_0_.ids_ref, bf16[4,8,256]{2,1,0:T(8,128)(2,1)S(1)} %get-tuple-element.22.refs_1_, bf16[8,3072]{1,0:T(8,128)(2,1)S(1)} %get-tuple-element.23.refs_2_, bf16[12,512,384]{2,1,0:T(8,128)(2,1)S(1)} %get-tuple-element.24.refs_3_), custom_call_target="tpu_custom_call" | custom-call | flops 4831838208 | bytes 5111808 | tf_op jit(solution)/shard_map/predict/pallas_call | solution.py:175
  9.8 2.1 %collective-permute-start.1 = (bf16[3,256,128]{2,1,0:T(8,128)(2,1)S(1)}, bf16[3,256,128]{2,1,0:T(8,128)(2,1)S(1)}, u32[]{:S(2)}, u32[]{:S(2)}) collective-permute-start(bf16[3,256,128]{2,1,0:T(8,128)(2,1)S(1)} %get-tuple-element.30), channel_id=1, source_target_pairs={{0,128},{64,192},{128,0},{192,64},{1,129},{65,193},{129,1},{193,65... | collective-permute-start | bytes 589832 | tf_op jit(solution)/shard_map/ppermute | solution.py:394
  12.0 3.1 %collective-permute-start.2 = (bf16[3,256,128]{2,1,0:T(8,128)(2,1)S(1)}, bf16[3,256,128]{2,1,0:T(8,128)(2,1)S(1)}, u32[]{:S(2)}, u32[]{:S(2)}) collective-permute-start(bf16[3,256,128]{2,1,0:T(8,128)(2,1)S(1)} %get-tuple-element.31), channel_id=1, source_target_pairs={{0,192},{64,128},{128,64},{192,0},{1,193},{65,129},{129,65},{193,1... | collective-permute-start | bytes 589832 | tf_op jit(solution)/shard_map/ppermute | solution.py:394
  15.1 6.2 %predict.2 = (bf16[3,256,128]{2,1,0:T(8,128)(2,1)S(1)}, bf16[3,256,128]{2,1,0:T(8,128)(2,1)S(1)}) custom-call(s32[3]{0:T(128)S(1)} %pad_add_fusion.refs_0_.ids_ref, bf16[4,8,256]{2,1,0:T(8,128)(2,1)S(1)} %get-tuple-element.22.refs_1_, bf16[8,3072]{1,0:T(8,128)(2,1)S(1)} %get-tuple-element.23.refs_2_, bf16[12,512,384]{2,1,0:T(8,128)(2,1)S(1)} %get-tuple-element.24.refs_3_), custom_call_target="tpu_custom_call" | custom-call | flops 4831838208 | bytes 5111808 | tf_op jit(solution)/shard_map/predict/pallas_call | solution.py:175
  21.5 1.6 %label.1 = (bf16[64,40,128]{2,1,0:T(8,128)(2,1)S(1)}, s32[32]{0:T(128)S(1)}) custom-call(s32[3]{0:T(128)S(1)} %pad_add_fusion.refs_0_.ids_ref, s32[32]{0:T(128)S(1)} %bitcast.8, s32[32,1]{1,0:T(8,128)S(1)} %copy.10.tile_ref, bf16[2,1024]{1,0:T(2,128)(2,1)S(1)} %copy-done.1), custom_call_target="tpu_custom_call" | custom-call | tf_op jit(solution)/shard_map/label/pallas_call | solution.py:293
  23.1 3.7 %peel.1 = (bf16[256,128]{1,0:T(8,128)(2,1)S(1)}, bf16[8,16,128]{2,1,0:T(8,128)(2,1)S(1)}, bf16[8,16,128]{2,1,0:T(8,128)(2,1)S(1)}, bf16[8,16,128]{2,1,0:T(8,128)(2,1)S(1)}, bf16[8,16,128]{2,1,0:T(8,128)(2,1)S(1)}) custom-call(s32[3]{0:T(128)S(1)} %pad_add_fusion.refs_0_.ids_ref, bf16[1024,128]{1,0:T(8,128)(2,1)S(1)} %copy-done, f32[1,128]{1,0:T(1,128)S(1)} %bitcast.10, ...), custom_call_target="tpu_custom_call" | custom-call | tf_op jit(solution)/shard_map/peel/pallas_call | solution.py:238
  26.9 0.6 collective-permute-start.3
  27.4 1.7 %collective-permute-start.5 = (bf16[8,16,128]{2,1,0:T(8,128)(2,1)S(1)}, bf16[8,16,128]{2,1,0:T(8,128)(2,1)S(1)}, u32[]{:S(2)}, u32[]{:S(2)}) collective-permute-start(bf16[8,16,128]{2,1,0:T(8,128)(2,1)S(1)} %get-tuple-element.36), channel_id=1, source_target_pairs={{0,192},{64,128},{128,64},{192,0},{1,193},{65,129},{129,65},{193,1... | collective-permute-start | bytes 98312 | tf_op jit(solution)/shard_map/ppermute | solution.py:394
  29.2 1.0 %collective-permute-done.4.r2_ref = bf16[8,16,128]{2,1,0:T(8,128)(2,1)S(1)} collective-permute-done((bf16[8,16,128]{2,1,0:T(8,128)(2,1)S(1)}, bf16[8,16,128]{2,1,0:T(8,128)(2,1)S(1)}, u32[]{:S(2)}, u32[]{:S(2)}) %collective-permute-start.4) | collective-permute-done | bytes 32800 | tf_op jit(solution)/shard_map/ppermute | solution.py:394
  30.2 1.1 %collective-permute-done.5.r3_ref = bf16[8,16,128]{2,1,0:T(8,128)(2,1)S(1)} collective-permute-done((bf16[8,16,128]{2,1,0:T(8,128)(2,1)S(1)}, bf16[8,16,128]{2,1,0:T(8,128)(2,1)S(1)}, u32[]{:S(2)}, u32[]{:S(2)}) %collective-permute-start.5) | collective-permute-done | bytes 32800 | tf_op jit(solution)/shard_map/ppermute | solution.py:394
  31.3 1.5 %pack.1 = bf16[64,40,128]{2,1,0:T(8,128)(2,1)} custom-call(s32[3]{0:T(128)S(1)} %pad_add_fusion.refs_0_.ids_ref, s32[32]{0:T(128)S(1)} %bitcast.9, s32[32]{0:T(128)S(1)} %get-tuple-element.27.slot_ref, bf16[8,16,128]{2,1,0:T(8,128)(2,1)S(1)} %get-tuple-element.33.r0_ref, bf16[8,16,128]{2,1,0:T(8,128)(2,1)S(1)} %collective-permute-done.3.r1_ref, ...), custom_call_target="tpu_custom_call" | custom-call | tf_op jit(solution)/shard_map/pack/pallas_call | solution.py:318
  32.8 13.3 %all-to-all-start = ((bf16[64,40,128]{2,1,0:T(8,128)(2,1)}), bf16[64,40,128]{2,1,0:T(8,128)(2,1)S(1)}, u32[]{:S(2)}, u32[]{:S(2)}) async-start(bf16[64,40,128]{2,1,0:T(8,128)(2,1)} %pack.1), calls=%async_computation | async-start | bytes 1310720 | tf_op jit(solution)/shard_map/all_to_all | solution.py:413
  46.1 0.8 %collective-permute-start.6 = (bf16[256,128]{1,0:T(8,128)(2,1)S(1)}, bf16[256,128]{1,0:T(8,128)(2,1)S(1)}, u32[]{:S(2)}, u32[]{:S(2)}) collective-permute-start(bf16[256,128]{1,0:T(8,128)(2,1)S(1)} %get-tuple-element.38.r0_ref), channel_id=1, source_target_pairs={{0,64},{64,0},{128,192},{192,128},{1,65},{65,1},{129,193},{193,129... | collective-permute-start | bytes 196616 | tf_op jit(solution)/shard_map/ppermute | solution.py:394
  46.8 0.1 collective-permute-start.7
  46.9 1.6 %collective-permute-start.8 = (bf16[256,128]{1,0:T(8,128)(2,1)S(1)}, bf16[256,128]{1,0:T(8,128)(2,1)S(1)}, u32[]{:S(2)}, u32[]{:S(2)}) collective-permute-start(bf16[256,128]{1,0:T(8,128)(2,1)S(1)} %get-tuple-element.38.r0_ref), channel_id=1, source_target_pairs={{0,192},{64,128},{128,64},{192,0},{1,193},{65,129},{129,65},{193,1... | collective-permute-start | bytes 196616 | tf_op jit(solution)/shard_map/ppermute | solution.py:394
  48.6 3.0 %collective-permute-done.7.r2_ref = bf16[256,128]{1,0:T(8,128)(2,1)S(1)} collective-permute-done((bf16[256,128]{1,0:T(8,128)(2,1)S(1)}, bf16[256,128]{1,0:T(8,128)(2,1)S(1)}, u32[]{:S(2)}, u32[]{:S(2)}) %collective-permute-start.7) | collective-permute-done | bytes 65568 | tf_op jit(solution)/shard_map/ppermute | solution.py:394
  51.6 3.2 %collective-permute-done.8.r3_ref = bf16[256,128]{1,0:T(8,128)(2,1)S(1)} collective-permute-done((bf16[256,128]{1,0:T(8,128)(2,1)S(1)}, bf16[256,128]{1,0:T(8,128)(2,1)S(1)}, u32[]{:S(2)}, u32[]{:S(2)}) %collective-permute-start.8) | collective-permute-done | bytes 65568 | tf_op jit(solution)/shard_map/ppermute | solution.py:394
  54.8 1.3 %join.1 = bf16[1024,128]{1,0:T(8,128)(2,1)} custom-call(s32[3]{0:T(128)S(1)} %pad_add_fusion.refs_0_.ids_ref, bf16[256,128]{1,0:T(8,128)(2,1)S(1)} %get-tuple-element.38.r0_ref, bf16[256,128]{1,0:T(8,128)(2,1)S(1)} %collective-permute-done.6.r1_ref, bf16[256,128]{1,0:T(8,128)(2,1)S(1)} %collective-permute-done.7.r2_ref, ...), custom_call_target="tpu_custom_call" | custom-call | tf_op jit(solution)/shard_map/join/pallas_call | solution.py:336
  56.0 9.8 %all-to-all-done.got_ref = bf16[64,40,128]{2,1,0:T(8,128)(2,1)S(1)} async-done(((bf16[64,40,128]{2,1,0:T(8,128)(2,1)}), bf16[64,40,128]{2,1,0:T(8,128)(2,1)S(1)}, u32[]{:S(2)}, u32[]{:S(2)}) %all-to-all-start) | async-done | bytes 655392 | tf_op jit(solution)/shard_map/all_to_all | solution.py:413
  65.9 2.9 %grid.1 = (f32[2,256,128]{2,1,0:T(8,128)S(1)}, f32[2,256,128]{2,1,0:T(8,128)S(1)}) custom-call(s32[3]{0:T(128)S(1)} %pad_add_fusion.refs_0_.ids_ref, bf16[64,40,128]{2,1,0:T(8,128)(2,1)S(1)} %all-to-all-done.got_ref), custom_call_target="tpu_custom_call" | custom-call | tf_op jit(solution)/shard_map/grid/pallas_call | solution.py:375
  68.8 3.2 %collective-permute-start.9 = (f32[2,256,128]{2,1,0:T(8,128)S(1)}, f32[2,256,128]{2,1,0:T(8,128)S(1)}, u32[]{:S(2)}, u32[]{:S(2)}) collective-permute-start(f32[2,256,128]{2,1,0:T(8,128)S(1)} %get-tuple-element.41), channel_id=1, source_target_pairs={{0,64},{64,0},{128,192},{192,128},{1,65},{65,1},{129,193},{193,129... | collective-permute-start | bytes 786440 | tf_op jit(solution)/shard_map/ppermute | solution.py:394
  72.0 1.2 %collective-permute-done.9 = f32[2,256,128]{2,1,0:T(8,128)S(1)} collective-permute-done((f32[2,256,128]{2,1,0:T(8,128)S(1)}, f32[2,256,128]{2,1,0:T(8,128)S(1)}, u32[]{:S(2)}, u32[]{:S(2)}) %collective-permute-start.9) | collective-permute-done | bytes 262176 | tf_op jit(solution)/shard_map/ppermute | solution.py:394
  73.1 0.7 add_bitcast_fusion
  (17 shorter events, 0.3 us)
Async XLA Ops:
  9.8 13.3 %collective-permute-start.1 = (bf16[3,256,128]{2,1,0:T(8,128)(2,1)S(1)}, bf16[3,256,128]{2,1,0:T(8,128)(2,1)S(1)}, u32[]{:S(2)}, u32[]{:S(2)}) collective-permute-start(bf16[3,256,128]{2,1,0:T(8,128)(2,1)S(1)} %get-tuple-element.30), channel_id=1, source_target_pairs={{0,128},{64,192},{128,0},{192,64},{1,129},{65,193},{129,1},{193,65... | collective-permute-start | bytes 589832 | tf_op jit(solution)/shard_map/ppermute | solution.py:394
  11.9 9.4 %copy-start.2 = (s32[32,1]{0,1:T(1,128)S(1)}, s32[32,1]{0,1:T(1,128)}, u32[]{:S(2)}) copy-start(s32[32,1]{0,1:T(1,128)} %param.15) | copy-start | bytes 388
  11.9 9.5 %copy-start.1 = (bf16[2,1024]{1,0:T(2,128)(2,1)S(1)}, bf16[2,1024]{1,0:T(2,128)(2,1)}, u32[]{:S(2)}) copy-start(bf16[2,1024]{1,0:T(2,128)(2,1)} %uv_ref.1) | copy-start | bytes 12292
  12.0 11.2 %copy-start = (bf16[1024,128]{1,0:T(8,128)(2,1)S(1)}, bf16[1024,128]{1,0:T(8,128)(2,1)}, u32[]{:S(2)}) copy-start(bf16[1024,128]{1,0:T(8,128)(2,1)} %vis_ref.1) | copy-start | bytes 786436
  12.0 11.2 %copy-start.3 = (f32[128]{0:T(128)S(1)}, f32[128]{0:T(128)}, u32[]{:S(2)}) copy-start(f32[128]{0:T(128)} %param.12) | copy-start | bytes 1540
  12.0 11.1 %collective-permute-start.2 = (bf16[3,256,128]{2,1,0:T(8,128)(2,1)S(1)}, bf16[3,256,128]{2,1,0:T(8,128)(2,1)S(1)}, u32[]{:S(2)}, u32[]{:S(2)}) collective-permute-start(bf16[3,256,128]{2,1,0:T(8,128)(2,1)S(1)} %get-tuple-element.31), channel_id=1, source_target_pairs={{0,192},{64,128},{128,64},{192,0},{1,193},{65,129},{129,65},{193,1... | collective-permute-start | bytes 589832 | tf_op jit(solution)/shard_map/ppermute | solution.py:394
  21.3 1.8 %collective-permute-start = (bf16[3,256,128]{2,1,0:T(8,128)(2,1)S(1)}, bf16[3,256,128]{2,1,0:T(8,128)(2,1)S(1)}, u32[]{:S(2)}, u32[]{:S(2)}) collective-permute-start(bf16[3,256,128]{2,1,0:T(8,128)(2,1)S(1)} %get-tuple-element.29), channel_id=1, source_target_pairs={{0,64},{64,0},{128,192},{192,128},{1,65},{65,1},{129,193},{193,129... | collective-permute-start | bytes 589832 | tf_op jit(solution)/shard_map/ppermute | solution.py:394
  26.9 2.3 %collective-permute-start.3 = (bf16[8,16,128]{2,1,0:T(8,128)(2,1)S(1)}, bf16[8,16,128]{2,1,0:T(8,128)(2,1)S(1)}, u32[]{:S(2)}, u32[]{:S(2)}) collective-permute-start(bf16[8,16,128]{2,1,0:T(8,128)(2,1)S(1)} %get-tuple-element.34), channel_id=1, source_target_pairs={{0,64},{64,0},{128,192},{192,128},{1,65},{65,1},{129,193},{193,129... | collective-permute-start | bytes 98312 | tf_op jit(solution)/shard_map/ppermute | solution.py:394
  27.4 2.8 %collective-permute-start.4 = (bf16[8,16,128]{2,1,0:T(8,128)(2,1)S(1)}, bf16[8,16,128]{2,1,0:T(8,128)(2,1)S(1)}, u32[]{:S(2)}, u32[]{:S(2)}) collective-permute-start(bf16[8,16,128]{2,1,0:T(8,128)(2,1)S(1)} %get-tuple-element.35), channel_id=1, source_target_pairs={{0,128},{64,192},{128,0},{192,64},{1,129},{65,193},{129,1},{193,65... | collective-permute-start | bytes 98312 | tf_op jit(solution)/shard_map/ppermute | solution.py:394
  27.4 3.8 %collective-permute-start.5 = (bf16[8,16,128]{2,1,0:T(8,128)(2,1)S(1)}, bf16[8,16,128]{2,1,0:T(8,128)(2,1)S(1)}, u32[]{:S(2)}, u32[]{:S(2)}) collective-permute-start(bf16[8,16,128]{2,1,0:T(8,128)(2,1)S(1)} %get-tuple-element.36), channel_id=1, source_target_pairs={{0,192},{64,128},{128,64},{192,0},{1,193},{65,129},{129,65},{193,1... | collective-permute-start | bytes 98312 | tf_op jit(solution)/shard_map/ppermute | solution.py:394
  32.8 33.1 %all-to-all-start = ((bf16[64,40,128]{2,1,0:T(8,128)(2,1)}), bf16[64,40,128]{2,1,0:T(8,128)(2,1)S(1)}, u32[]{:S(2)}, u32[]{:S(2)}) async-start(bf16[64,40,128]{2,1,0:T(8,128)(2,1)} %pack.1), calls=%async_computation | async-start | bytes 1310720 | tf_op jit(solution)/shard_map/all_to_all | solution.py:413
  46.1 2.5 %collective-permute-start.6 = (bf16[256,128]{1,0:T(8,128)(2,1)S(1)}, bf16[256,128]{1,0:T(8,128)(2,1)S(1)}, u32[]{:S(2)}, u32[]{:S(2)}) collective-permute-start(bf16[256,128]{1,0:T(8,128)(2,1)S(1)} %get-tuple-element.38.r0_ref), channel_id=1, source_target_pairs={{0,64},{64,0},{128,192},{192,128},{1,65},{65,1},{129,193},{193,129... | collective-permute-start | bytes 196616 | tf_op jit(solution)/shard_map/ppermute | solution.py:394
  46.8 4.7 %collective-permute-start.7 = (bf16[256,128]{1,0:T(8,128)(2,1)S(1)}, bf16[256,128]{1,0:T(8,128)(2,1)S(1)}, u32[]{:S(2)}, u32[]{:S(2)}) collective-permute-start(bf16[256,128]{1,0:T(8,128)(2,1)S(1)} %get-tuple-element.38.r0_ref), channel_id=1, source_target_pairs={{0,128},{64,192},{128,0},{192,64},{1,129},{65,193},{129,1},{193,65... | collective-permute-start | bytes 196616 | tf_op jit(solution)/shard_map/ppermute | solution.py:394
  46.9 7.8 %collective-permute-start.8 = (bf16[256,128]{1,0:T(8,128)(2,1)S(1)}, bf16[256,128]{1,0:T(8,128)(2,1)S(1)}, u32[]{:S(2)}, u32[]{:S(2)}) collective-permute-start(bf16[256,128]{1,0:T(8,128)(2,1)S(1)} %get-tuple-element.38.r0_ref), channel_id=1, source_target_pairs={{0,192},{64,128},{128,64},{192,0},{1,193},{65,129},{129,65},{193,1... | collective-permute-start | bytes 196616 | tf_op jit(solution)/shard_map/ppermute | solution.py:394
  68.8 4.3 %collective-permute-start.9 = (f32[2,256,128]{2,1,0:T(8,128)S(1)}, f32[2,256,128]{2,1,0:T(8,128)S(1)}, u32[]{:S(2)}, u32[]{:S(2)}) collective-permute-start(f32[2,256,128]{2,1,0:T(8,128)S(1)} %get-tuple-element.41), channel_id=1, source_target_pairs={{0,64},{64,0},{128,192},{192,128},{1,65},{65,1},{129,193},{193,129... | collective-permute-start | bytes 786440 | tf_op jit(solution)/shard_map/ppermute | solution.py:394

commit v5 on v4

--- a/solution.py
+++ b/solution.py
@@ -196,34 +196,60 @@
     return jnp.sum(value.reshape(QROWS // GB, GB, COLS), axis=1)
 
 
+def lane_shift(value, by):
+    return pltpu.roll(value, (-by) % COLS, 1)
+
+
+def sweeps(pull):
+    lane = lax.broadcasted_iota(jnp.int32, pull.shape, 1)
+    first, last = lane < 2, lane >= COLS - 2
+    band = {0: jnp.ones_like(pull)}
+    free = pull
+    for _ in range(ITERS - 1):
+        lower = {d: lane_shift(value, -2) for d, value in band.items()}
+        upper = {d: lane_shift(value, 2) for d, value in band.items()}
+        new = {}
+        for d, value in band.items():
+            for at, inside, kept in ((d - 2, lower[d], first), (d + 2, upper[d], last)):
+                moved = jnp.where(kept, 0.0, inside)
+                new[at] = new[at] + moved if at in new else moved
+                stays = jnp.where(kept, value, 0.0)
+                new[d] = new[d] + stays if d in new else stays
+        band = {d: (0.5 * pull) * value for d, value in new.items()}
+        band[0] = band[0] + 1.0
+        around = jnp.where(first, free, lane_shift(free, -2)) + jnp.where(last, free, lane_shift(free, 2))
+        free = pull * (0.5 * around)
+    return band, free
+
+
+SHIFTS = tuple(range(-2 * (ITERS - 1), 2 * ITERS, 2))
+
+
 def peel_kernel(ids_ref, vis_ref, ridge_ref, m0_ref, m1_ref, m2_ref, m3_ref, out_ref, *rest):
-    part_refs, (model_ref, inv_ref, part_ref) = rest[:N_DIR], rest[N_DIR:]
+    part_refs, (model_ref, inv_ref, band_ref, part_ref) = rest[:N_DIR], rest[N_DIR:]
     me = ids_ref[0]
     ridge = ridge_ref[...]
+    blocks = QROWS // GB
     for x, ref in enumerate((m0_ref, m1_ref, m2_ref, m3_ref)):
         owner = me ^ x
         for p in range(DIR_DEV):
             model = ref[p].astype(F32)
             model_ref[owner * DIR_DEV + p] = model
-            inv_ref[owner * DIR_DEV + p] = 1.0 / (per_block_sum(model * model) + ridge)
-    lane = lax.broadcasted_iota(jnp.int32, (QROWS // GB, COLS), 1)
-
-    def neighbours(gain):
-        lower = jnp.where(lane < 2, gain, pltpu.roll(gain, 2, 1))
-        upper = jnp.where(lane >= COLS - 2, gain, pltpu.roll(gain, COLS - 2, 1))
-        return 0.5 * (lower + upper)
-
+            inv_ref[pl.ds((owner * DIR_DEV + p) * 8, blocks), :] = per_block_sum(model * model)
+    inv = 1.0 / (inv_ref[...] + ridge)
+    band, free = sweeps(ridge * inv)
+    for n, d in enumerate(SHIFTS):
+        band_ref[n] = band[d] * lane_shift(inv, d)
+    band_ref[len(SHIFTS)] = free
     remains = vis_ref[pl.ds(pl.multiple_of(me * QROWS, QROWS), QROWS), :].astype(F32)
     for j in range(N_DIR * DIR_DEV):
         model = model_ref[j]
-        inv = inv_ref[j]
-        cross = per_block_sum(remains * model) * inv
-        pull = ridge * inv
-        gain = cross + pull
-        for _ in range(ITERS - 1):
-            gain = cross + pull * neighbours(gain)
+        cross = per_block_sum(remains * model)
+        gain = band_ref[len(SHIFTS), j * 8 : j * 8 + blocks, :]
+        for n, d in enumerate(SHIFTS):
+            gain = gain + band_ref[n, j * 8 : j * 8 + blocks, :] * (lane_shift(cross, d) if d else cross)
         spread = jnp.concatenate(
-            [jnp.broadcast_to(gain[b : b + 1], (GB, COLS)) for b in range(QROWS // GB)], axis=0
+            [jnp.broadcast_to(gain[b : b + 1], (GB, COLS)) for b in range(blocks)], axis=0
         )
         remains = remains - spread * model
         if (j + 1) % DIR_DEV == 0:
@@ -243,7 +269,8 @@
         out_specs=(vmem(),) * (1 + N_DIR),
         scratch_shapes=[
             pltpu.VMEM((N_DIR * DIR_DEV, QROWS, COLS), F32),
-            pltpu.VMEM((N_DIR * DIR_DEV, QROWS // GB, COLS), F32),
+            pltpu.VMEM((N_DIR * DIR_DEV * 8, COLS), F32),
+            pltpu.VMEM((len(SHIFTS) + 1, N_DIR * DIR_DEV * 8, COLS), F32),
             pltpu.VMEM((QBLOCKS, 2, PART, COLS), F32),
         ],
         compiler_params=params(16),
@@ -343,7 +370,7 @@
     )(ids, *rows)
 
 
-def grid_kernel(ids_ref, got_ref, keep_ref, give_ref, tab_ref):
+def grid_kernel(ids_ref, got_ref, keep_ref, give_ref, tab_ref, acc_ref):
     chip = ids_ref[0] // 2
     half = ids_ref[1]
     tiles = N_TB * SLOTS * PART // 128
@@ -354,18 +381,30 @@
     order = lax.broadcasted_iota(jnp.int32, (16, 1), 0)
     x_pixel = (16 * chip + 8 * ((order // 8) ^ half) + order % 8 - GRID // 2).astype(F32)
     scale = 1.0 / (2.0 * GRID)
+    step = 256
+    per_step = step // 128
+
+    def product(n):
+        sources = step // (SLOTS * PART)
+        rows = got_ref[n * sources : (n + 1) * sources, : SLOTS * PART, :].reshape(step, COLS)
+        return jnp.dot(tab_ref[n], rows, preferred_element_type=F32)
+
     for tile in range(tiles):
         u = coords[tile, 0:1, :] * scale
         v = coords[tile, 1:2, :] * scale
         cx, sx = cos_sin_turns(x_pixel * u)
         cy, sy = cos_sin_turns(y_pixel * v)
-        lanes = slice(tile * 128, (tile + 1) * 128)
+        n, lanes = tile // per_step, slice(tile % per_step * 128, (tile % per_step + 1) * 128)
         for x in range(16):
             a, b = cx[x : x + 1], sx[x : x + 1]
-            tab_ref[x * GRID : (x + 1) * GRID, lanes] = (a * cy - b * sy).astype(BF16)
-            tab_ref[512 + x * GRID : 512 + (x + 1) * GRID, lanes] = (b * cy + a * sy).astype(BF16)
-    rows = got_ref[:, : SLOTS * PART, :].reshape(N_TB * SLOTS * PART, COLS)
-    total = jnp.dot(tab_ref[...], rows, preferred_element_type=F32) * float(ROWS_DEV) ** (-0.5)
+            tab_ref[n, x * GRID : (x + 1) * GRID, lanes] = (a * cy - b * sy).astype(BF16)
+            tab_ref[n, 512 + x * GRID : 512 + (x + 1) * GRID, lanes] = (b * cy + a * sy).astype(BF16)
+        if tile % per_step == per_step - 1:
+            if n == 0:
+                acc_ref[...] = product(n)
+            else:
+                acc_ref[...] += product(n)
+    total = acc_ref[...] * float(ROWS_DEV) ** (-0.5)
     for part in range(2):
         keep_ref[part] = total[part * 512 : part * 512 + 256]
         give_ref[part] = total[part * 512 + 256 : part * 512 + 512]
@@ -380,7 +419,10 @@
         ),
         in_specs=[smem(), vmem()],
         out_specs=(vmem(), vmem()),
-        scratch_shapes=[pltpu.VMEM((1024, N_TB * SLOTS * PART), BF16)],
+        scratch_shapes=[
+            pltpu.VMEM((N_TB * SLOTS * PART // 256, 1024, 256), BF16),
+            pltpu.VMEM((1024, COLS), F32),
+        ],
         compiler_params=params(24),
         name="grid",
     )(ids, got)

time: 74.1 us -> 72.5 us (0.978)
  Pallas kernels: 26.3 us -> 24.7 us
    pallas_call x1, Pallas kernels: 3.74 us -> 2.31 us  [peel(): pl.pallas_call(peel_kernel, out_shape=(jax.ShapeDtypeStruct((QROWS, COLS)...]
  transfers between devices with their start and end apart: 11 -> 11, of which waited for: 6 -> 6; matrix products, arithmetic and copies ran while one was open for 0% -> 0% of each run, Pallas kernels for 12% -> 13%
where the time goes in v5:
time: 72.5 us; the launch traced here: 72.3 us
  starting transfers between devices  26.5 us (37%)
  Pallas kernels  24.7 us (34%)
  waiting for transfers between devices  19.3 us (27%)
  other arithmetic  0.81 us (1%)
  between operations  0.78 us (1%)
    ppermute x10, starting transfers between devices, swap(): return lax.ppermute(value, 'dir', [(i, i ^ flip) for i in range(N_DIR)])  13.3 us
    all_to_all x1, starting transfers between devices, local(): got = lax.all_to_all(send, 'tb', split_axis=0, concat_axis=0, tiled=True)  13.3 us
    pallas_call x2, Pallas kernels, predict(): pl.pallas_call(kernel, out_shape=tuple((jax.ShapeDtypeStruct((DIR_DEV, QR...  12.4 us
    all_to_all x1, waiting for transfers between devices, local(): got = lax.all_to_all(send, 'tb', split_axis=0, concat_axis=0, tiled=True)  9.84 us
    ppermute x10, waiting for transfers between devices, swap(): return lax.ppermute(value, 'dir', [(i, i ^ flip) for i in range(N_DIR)])  9.48 us
    pallas_call x1, Pallas kernels, prepare(): pl.pallas_call(prepare_kernel, out_shape=(jax.ShapeDtypeStruct((8, POOL),...  2.85 us
    pallas_call x1, Pallas kernels, grid_rows(): pl.pallas_call(grid_kernel, out_shape=(jax.ShapeDtypeStruct((2, PIX // N_...  2.77 us
    pallas_call x1, Pallas kernels, peel(): pl.pallas_call(peel_kernel, out_shape=(jax.ShapeDtypeStruct((QROWS, COLS)...  2.31 us
  transfers between devices with their start and end apart: 11, of which 6 were waited for; matrix products, arithmetic and copies ran while one was open for 0% of the time, Pallas kernels for 13%

profile of v5, /device:TPU:1, one launch (start us, length us, event | category | flops | bytes accessed | tf_op | source)
XLA Modules:
  0.0 72.3 jit_solution(9819613706165824564)
XLA Ops:
  0.7 2.9 %prepare.1 = (bf16[8,3072]{1,0:T(8,128)(2,1)S(1)}, bf16[4,8,256]{2,1,0:T(8,128)(2,1)S(1)}, bf16[12,512,384]{2,1,0:T(8,128)(2,1)S(1)}) custom-call(s32[3]{0:T(128)} %order_hbm.1, s32[1,3072]{1,0:T(1,128)} %bitcast.11, f32[2,3072]{1,0:T(2,128)} %lm_hbm.1, bf16[2,1024]{1,0:T(2,128)(2,1)} %uv_ref.1, bf16[2,3072,128]{2,1,0:T(8,128)(2,1)} %spec_hbm.1), custom_call_target="tpu_custom_call" | custom-call | tf_op jit(solution)/shard_map/prepare/pallas_call | solution.py:115
  3.6 6.2 %predict.3 = (bf16[3,256,128]{2,1,0:T(8,128)(2,1)S(1)}, bf16[3,256,128]{2,1,0:T(8,128)(2,1)S(1)}) custom-call(s32[3]{0:T(128)S(1)} %pad_add_fusion.refs_0_.ids_ref, bf16[4,8,256]{2,1,0:T(8,128)(2,1)S(1)} %get-tuple-element.22.refs_1_, bf16[8,3072]{1,0:T(8,128)(2,1)S(1)} %get-tuple-element.23.refs_2_, bf16[12,512,384]{2,1,0:T(8,128)(2,1)S(1)} %get-tuple-element.24.refs_3_), custom_call_target="tpu_custom_call" | custom-call | flops 4831838208 | bytes 5111808 | tf_op jit(solution)/shard_map/predict/pallas_call | solution.py:175
  9.8 2.1 %collective-permute-start.1 = (bf16[3,256,128]{2,1,0:T(8,128)(2,1)S(1)}, bf16[3,256,128]{2,1,0:T(8,128)(2,1)S(1)}, u32[]{:S(2)}, u32[]{:S(2)}) collective-permute-start(bf16[3,256,128]{2,1,0:T(8,128)(2,1)S(1)} %get-tuple-element.30), channel_id=1, source_target_pairs={{0,128},{64,192},{128,0},{192,64},{1,129},{65,193},{129,1},{193,65... | collective-permute-start | bytes 589832 | tf_op jit(solution)/shard_map/ppermute | solution.py:436
  12.0 3.1 %collective-permute-start.2 = (bf16[3,256,128]{2,1,0:T(8,128)(2,1)S(1)}, bf16[3,256,128]{2,1,0:T(8,128)(2,1)S(1)}, u32[]{:S(2)}, u32[]{:S(2)}) collective-permute-start(bf16[3,256,128]{2,1,0:T(8,128)(2,1)S(1)} %get-tuple-element.31), channel_id=1, source_target_pairs={{0,192},{64,128},{128,64},{192,0},{1,193},{65,129},{129,65},{193,1... | collective-permute-start | bytes 589832 | tf_op jit(solution)/shard_map/ppermute | solution.py:436
  15.1 6.2 %predict.2 = (bf16[3,256,128]{2,1,0:T(8,128)(2,1)S(1)}, bf16[3,256,128]{2,1,0:T(8,128)(2,1)S(1)}) custom-call(s32[3]{0:T(128)S(1)} %pad_add_fusion.refs_0_.ids_ref, bf16[4,8,256]{2,1,0:T(8,128)(2,1)S(1)} %get-tuple-element.22.refs_1_, bf16[8,3072]{1,0:T(8,128)(2,1)S(1)} %get-tuple-element.23.refs_2_, bf16[12,512,384]{2,1,0:T(8,128)(2,1)S(1)} %get-tuple-element.24.refs_3_), custom_call_target="tpu_custom_call" | custom-call | flops 4831838208 | bytes 5111808 | tf_op jit(solution)/shard_map/predict/pallas_call | solution.py:175
  21.5 1.6 %label.1 = (bf16[64,40,128]{2,1,0:T(8,128)(2,1)S(1)}, s32[32]{0:T(128)S(1)}) custom-call(s32[3]{0:T(128)S(1)} %pad_add_fusion.refs_0_.ids_ref, s32[32]{0:T(128)S(1)} %bitcast.8, s32[32,1]{1,0:T(8,128)S(1)} %copy.10.tile_ref, bf16[2,1024]{1,0:T(2,128)(2,1)S(1)} %copy-done.1), custom_call_target="tpu_custom_call" | custom-call | tf_op jit(solution)/shard_map/label/pallas_call | solution.py:320
  23.1 2.3 %peel.1 = (bf16[256,128]{1,0:T(8,128)(2,1)S(1)}, bf16[8,16,128]{2,1,0:T(8,128)(2,1)S(1)}, bf16[8,16,128]{2,1,0:T(8,128)(2,1)S(1)}, bf16[8,16,128]{2,1,0:T(8,128)(2,1)S(1)}, bf16[8,16,128]{2,1,0:T(8,128)(2,1)S(1)}) custom-call(s32[3]{0:T(128)S(1)} %pad_add_fusion.refs_0_.ids_ref, bf16[1024,128]{1,0:T(8,128)(2,1)S(1)} %copy-done, f32[1,128]{1,0:T(1,128)S(1)} %bitcast.10, ...), custom_call_target="tpu_custom_call" | custom-call | tf_op jit(solution)/shard_map/peel/pallas_call | solution.py:264
  25.4 0.6 collective-permute-start.3
  26.0 1.7 %collective-permute-start.5 = (bf16[8,16,128]{2,1,0:T(8,128)(2,1)S(1)}, bf16[8,16,128]{2,1,0:T(8,128)(2,1)S(1)}, u32[]{:S(2)}, u32[]{:S(2)}) collective-permute-start(bf16[8,16,128]{2,1,0:T(8,128)(2,1)S(1)} %get-tuple-element.36), channel_id=1, source_target_pairs={{0,192},{64,128},{128,64},{192,0},{1,193},{65,129},{129,65},{193,1... | collective-permute-start | bytes 98312 | tf_op jit(solution)/shard_map/ppermute | solution.py:436
  27.7 1.0 %collective-permute-done.4.r2_ref = bf16[8,16,128]{2,1,0:T(8,128)(2,1)S(1)} collective-permute-done((bf16[8,16,128]{2,1,0:T(8,128)(2,1)S(1)}, bf16[8,16,128]{2,1,0:T(8,128)(2,1)S(1)}, u32[]{:S(2)}, u32[]{:S(2)}) %collective-permute-start.4) | collective-permute-done | bytes 32800 | tf_op jit(solution)/shard_map/ppermute | solution.py:436
  28.8 1.1 %collective-permute-done.5.r3_ref = bf16[8,16,128]{2,1,0:T(8,128)(2,1)S(1)} collective-permute-done((bf16[8,16,128]{2,1,0:T(8,128)(2,1)S(1)}, bf16[8,16,128]{2,1,0:T(8,128)(2,1)S(1)}, u32[]{:S(2)}, u32[]{:S(2)}) %collective-permute-start.5) | collective-permute-done | bytes 32800 | tf_op jit(solution)/shard_map/ppermute | solution.py:436
  29.8 1.5 %pack.1 = bf16[64,40,128]{2,1,0:T(8,128)(2,1)} custom-call(s32[3]{0:T(128)S(1)} %pad_add_fusion.refs_0_.ids_ref, s32[32]{0:T(128)S(1)} %bitcast.9, s32[32]{0:T(128)S(1)} %get-tuple-element.27.slot_ref, bf16[8,16,128]{2,1,0:T(8,128)(2,1)S(1)} %get-tuple-element.33.r0_ref, bf16[8,16,128]{2,1,0:T(8,128)(2,1)S(1)} %collective-permute-done.3.r1_ref, ...), custom_call_target="tpu_custom_call" | custom-call | tf_op jit(solution)/shard_map/pack/pallas_call | solution.py:345
  31.4 13.3 %all-to-all-start = ((bf16[64,40,128]{2,1,0:T(8,128)(2,1)}), bf16[64,40,128]{2,1,0:T(8,128)(2,1)S(1)}, u32[]{:S(2)}, u32[]{:S(2)}) async-start(bf16[64,40,128]{2,1,0:T(8,128)(2,1)} %pack.1), calls=%async_computation | async-start | bytes 1310720 | tf_op jit(solution)/shard_map/all_to_all | solution.py:455
  44.6 0.8 %collective-permute-start.6 = (bf16[256,128]{1,0:T(8,128)(2,1)S(1)}, bf16[256,128]{1,0:T(8,128)(2,1)S(1)}, u32[]{:S(2)}, u32[]{:S(2)}) collective-permute-start(bf16[256,128]{1,0:T(8,128)(2,1)S(1)} %get-tuple-element.38.r0_ref), channel_id=1, source_target_pairs={{0,64},{64,0},{128,192},{192,128},{1,65},{65,1},{129,193},{193,129... | collective-permute-start | bytes 196616 | tf_op jit(solution)/shard_map/ppermute | solution.py:436
  45.4 0.1 collective-permute-start.7
  45.5 1.6 %collective-permute-start.8 = (bf16[256,128]{1,0:T(8,128)(2,1)S(1)}, bf16[256,128]{1,0:T(8,128)(2,1)S(1)}, u32[]{:S(2)}, u32[]{:S(2)}) collective-permute-start(bf16[256,128]{1,0:T(8,128)(2,1)S(1)} %get-tuple-element.38.r0_ref), channel_id=1, source_target_pairs={{0,192},{64,128},{128,64},{192,0},{1,193},{65,129},{129,65},{193,1... | collective-permute-start | bytes 196616 | tf_op jit(solution)/shard_map/ppermute | solution.py:436
  47.1 3.0 %collective-permute-done.7.r2_ref = bf16[256,128]{1,0:T(8,128)(2,1)S(1)} collective-permute-done((bf16[256,128]{1,0:T(8,128)(2,1)S(1)}, bf16[256,128]{1,0:T(8,128)(2,1)S(1)}, u32[]{:S(2)}, u32[]{:S(2)}) %collective-permute-start.7) | collective-permute-done | bytes 65568 | tf_op jit(solution)/shard_map/ppermute | solution.py:436
  50.1 3.2 %collective-permute-done.8.r3_ref = bf16[256,128]{1,0:T(8,128)(2,1)S(1)} collective-permute-done((bf16[256,128]{1,0:T(8,128)(2,1)S(1)}, bf16[256,128]{1,0:T(8,128)(2,1)S(1)}, u32[]{:S(2)}, u32[]{:S(2)}) %collective-permute-start.8) | collective-permute-done | bytes 65568 | tf_op jit(solution)/shard_map/ppermute | solution.py:436
  53.3 1.3 %join.1 = bf16[1024,128]{1,0:T(8,128)(2,1)} custom-call(s32[3]{0:T(128)S(1)} %pad_add_fusion.refs_0_.ids_ref, bf16[256,128]{1,0:T(8,128)(2,1)S(1)} %get-tuple-element.38.r0_ref, bf16[256,128]{1,0:T(8,128)(2,1)S(1)} %collective-permute-done.6.r1_ref, bf16[256,128]{1,0:T(8,128)(2,1)S(1)} %collective-permute-done.7.r2_ref, ...), custom_call_target="tpu_custom_call" | custom-call | tf_op jit(solution)/shard_map/join/pallas_call | solution.py:363
  54.6 9.8 %all-to-all-done.got_ref = bf16[64,40,128]{2,1,0:T(8,128)(2,1)S(1)} async-done(((bf16[64,40,128]{2,1,0:T(8,128)(2,1)}), bf16[64,40,128]{2,1,0:T(8,128)(2,1)S(1)}, u32[]{:S(2)}, u32[]{:S(2)}) %all-to-all-start) | async-done | bytes 655392 | tf_op jit(solution)/shard_map/all_to_all | solution.py:455
  64.4 2.8 %grid.1 = (f32[2,256,128]{2,1,0:T(8,128)S(1)}, f32[2,256,128]{2,1,0:T(8,128)S(1)}) custom-call(s32[3]{0:T(128)S(1)} %pad_add_fusion.refs_0_.ids_ref, bf16[64,40,128]{2,1,0:T(8,128)(2,1)S(1)} %all-to-all-done.got_ref), custom_call_target="tpu_custom_call" | custom-call | tf_op jit(solution)/shard_map/grid/pallas_call | solution.py:414
  67.2 3.2 %collective-permute-start.9 = (f32[2,256,128]{2,1,0:T(8,128)S(1)}, f32[2,256,128]{2,1,0:T(8,128)S(1)}, u32[]{:S(2)}, u32[]{:S(2)}) collective-permute-start(f32[2,256,128]{2,1,0:T(8,128)S(1)} %get-tuple-element.41), channel_id=1, source_target_pairs={{0,64},{64,0},{128,192},{192,128},{1,65},{65,1},{129,193},{193,129... | collective-permute-start | bytes 786440 | tf_op jit(solution)/shard_map/ppermute | solution.py:436
  70.4 1.2 %collective-permute-done.9 = f32[2,256,128]{2,1,0:T(8,128)S(1)} collective-permute-done((f32[2,256,128]{2,1,0:T(8,128)S(1)}, f32[2,256,128]{2,1,0:T(8,128)S(1)}, u32[]{:S(2)}, u32[]{:S(2)}) %collective-permute-start.9) | collective-permute-done | bytes 262176 | tf_op jit(solution)/shard_map/ppermute | solution.py:436
  71.5 0.7 %add_bitcast_fusion = f32[1,2,256,128]{3,2,1,0:T(8,128)} fusion(f32[2,256,128]{2,1,0:T(8,128)S(1)} %get-tuple-element.40, f32[2,256,128]{2,1,0:T(8,128)S(1)} %collective-permute-done.9), kind=kLoop, calls=%fused_computation | loop fusion | flops 65536 | bytes 786432 | tf_op jit(solution)/shard_map/broadcast_in_dim | solution.py:459
  (17 shorter events, 0.3 us)
Async XLA Ops:
  9.8 13.3 %collective-permute-start.1 = (bf16[3,256,128]{2,1,0:T(8,128)(2,1)S(1)}, bf16[3,256,128]{2,1,0:T(8,128)(2,1)S(1)}, u32[]{:S(2)}, u32[]{:S(2)}) collective-permute-start(bf16[3,256,128]{2,1,0:T(8,128)(2,1)S(1)} %get-tuple-element.30), channel_id=1, source_target_pairs={{0,128},{64,192},{128,0},{192,64},{1,129},{65,193},{129,1},{193,65... | collective-permute-start | bytes 589832 | tf_op jit(solution)/shard_map/ppermute | solution.py:436
  11.9 9.4 %copy-start.2 = (s32[32,1]{0,1:T(1,128)S(1)}, s32[32,1]{0,1:T(1,128)}, u32[]{:S(2)}) copy-start(s32[32,1]{0,1:T(1,128)} %param.15) | copy-start | bytes 388
  11.9 9.5 %copy-start.1 = (bf16[2,1024]{1,0:T(2,128)(2,1)S(1)}, bf16[2,1024]{1,0:T(2,128)(2,1)}, u32[]{:S(2)}) copy-start(bf16[2,1024]{1,0:T(2,128)(2,1)} %uv_ref.1) | copy-start | bytes 12292
  12.0 11.2 %copy-start = (bf16[1024,128]{1,0:T(8,128)(2,1)S(1)}, bf16[1024,128]{1,0:T(8,128)(2,1)}, u32[]{:S(2)}) copy-start(bf16[1024,128]{1,0:T(8,128)(2,1)} %vis_ref.1) | copy-start | bytes 786436
  12.0 11.2 %copy-start.3 = (f32[128]{0:T(128)S(1)}, f32[128]{0:T(128)}, u32[]{:S(2)}) copy-start(f32[128]{0:T(128)} %param.12) | copy-start | bytes 1540
  12.0 11.1 %collective-permute-start.2 = (bf16[3,256,128]{2,1,0:T(8,128)(2,1)S(1)}, bf16[3,256,128]{2,1,0:T(8,128)(2,1)S(1)}, u32[]{:S(2)}, u32[]{:S(2)}) collective-permute-start(bf16[3,256,128]{2,1,0:T(8,128)(2,1)S(1)} %get-tuple-element.31), channel_id=1, source_target_pairs={{0,192},{64,128},{128,64},{192,0},{1,193},{65,129},{129,65},{193,1... | collective-permute-start | bytes 589832 | tf_op jit(solution)/shard_map/ppermute | solution.py:436
  21.3 1.8 %collective-permute-start = (bf16[3,256,128]{2,1,0:T(8,128)(2,1)S(1)}, bf16[3,256,128]{2,1,0:T(8,128)(2,1)S(1)}, u32[]{:S(2)}, u32[]{:S(2)}) collective-permute-start(bf16[3,256,128]{2,1,0:T(8,128)(2,1)S(1)} %get-tuple-element.29), channel_id=1, source_target_pairs={{0,64},{64,0},{128,192},{192,128},{1,65},{65,1},{129,193},{193,129... | collective-permute-start | bytes 589832 | tf_op jit(solution)/shard_map/ppermute | solution.py:436
  25.4 2.3 %collective-permute-start.3 = (bf16[8,16,128]{2,1,0:T(8,128)(2,1)S(1)}, bf16[8,16,128]{2,1,0:T(8,128)(2,1)S(1)}, u32[]{:S(2)}, u32[]{:S(2)}) collective-permute-start(bf16[8,16,128]{2,1,0:T(8,128)(2,1)S(1)} %get-tuple-element.34), channel_id=1, source_target_pairs={{0,64},{64,0},{128,192},{192,128},{1,65},{65,1},{129,193},{193,129... | collective-permute-start | bytes 98312 | tf_op jit(solution)/shard_map/ppermute | solution.py:436
  26.0 2.8 %collective-permute-start.4 = (bf16[8,16,128]{2,1,0:T(8,128)(2,1)S(1)}, bf16[8,16,128]{2,1,0:T(8,128)(2,1)S(1)}, u32[]{:S(2)}, u32[]{:S(2)}) collective-permute-start(bf16[8,16,128]{2,1,0:T(8,128)(2,1)S(1)} %get-tuple-element.35), channel_id=1, source_target_pairs={{0,128},{64,192},{128,0},{192,64},{1,129},{65,193},{129,1},{193,65... | collective-permute-start | bytes 98312 | tf_op jit(solution)/shard_map/ppermute | solution.py:436
  26.0 3.8 %collective-permute-start.5 = (bf16[8,16,128]{2,1,0:T(8,128)(2,1)S(1)}, bf16[8,16,128]{2,1,0:T(8,128)(2,1)S(1)}, u32[]{:S(2)}, u32[]{:S(2)}) collective-permute-start(bf16[8,16,128]{2,1,0:T(8,128)(2,1)S(1)} %get-tuple-element.36), channel_id=1, source_target_pairs={{0,192},{64,128},{128,64},{192,0},{1,193},{65,129},{129,65},{193,1... | collective-permute-start | bytes 98312 | tf_op jit(solution)/shard_map/ppermute | solution.py:436
  31.4 33.1 %all-to-all-start = ((bf16[64,40,128]{2,1,0:T(8,128)(2,1)}), bf16[64,40,128]{2,1,0:T(8,128)(2,1)S(1)}, u32[]{:S(2)}, u32[]{:S(2)}) async-start(bf16[64,40,128]{2,1,0:T(8,128)(2,1)} %pack.1), calls=%async_computation | async-start | bytes 1310720 | tf_op jit(solution)/shard_map/all_to_all | solution.py:455
  44.6 2.5 %collective-permute-start.6 = (bf16[256,128]{1,0:T(8,128)(2,1)S(1)}, bf16[256,128]{1,0:T(8,128)(2,1)S(1)}, u32[]{:S(2)}, u32[]{:S(2)}) collective-permute-start(bf16[256,128]{1,0:T(8,128)(2,1)S(1)} %get-tuple-element.38.r0_ref), channel_id=1, source_target_pairs={{0,64},{64,0},{128,192},{192,128},{1,65},{65,1},{129,193},{193,129... | collective-permute-start | bytes 196616 | tf_op jit(solution)/shard_map/ppermute | solution.py:436
  45.4 4.7 %collective-permute-start.7 = (bf16[256,128]{1,0:T(8,128)(2,1)S(1)}, bf16[256,128]{1,0:T(8,128)(2,1)S(1)}, u32[]{:S(2)}, u32[]{:S(2)}) collective-permute-start(bf16[256,128]{1,0:T(8,128)(2,1)S(1)} %get-tuple-element.38.r0_ref), channel_id=1, source_target_pairs={{0,128},{64,192},{128,0},{192,64},{1,129},{65,193},{129,1},{193,65... | collective-permute-start | bytes 196616 | tf_op jit(solution)/shard_map/ppermute | solution.py:436
  45.5 7.8 %collective-permute-start.8 = (bf16[256,128]{1,0:T(8,128)(2,1)S(1)}, bf16[256,128]{1,0:T(8,128)(2,1)S(1)}, u32[]{:S(2)}, u32[]{:S(2)}) collective-permute-start(bf16[256,128]{1,0:T(8,128)(2,1)S(1)} %get-tuple-element.38.r0_ref), channel_id=1, source_target_pairs={{0,192},{64,128},{128,64},{192,0},{1,193},{65,129},{129,65},{193,1... | collective-permute-start | bytes 196616 | tf_op jit(solution)/shard_map/ppermute | solution.py:436
  67.2 4.3 %collective-permute-start.9 = (f32[2,256,128]{2,1,0:T(8,128)S(1)}, f32[2,256,128]{2,1,0:T(8,128)S(1)}, u32[]{:S(2)}, u32[]{:S(2)}) collective-permute-start(f32[2,256,128]{2,1,0:T(8,128)S(1)} %get-tuple-element.41), channel_id=1, source_target_pairs={{0,64},{64,0},{128,192},{192,128},{1,65},{65,1},{129,193},{193,129... | collective-permute-start | bytes 786440 | tf_op jit(solution)/shard_map/ppermute | solution.py:436

commit v6 on v5

--- a/solution.py
+++ b/solution.py
@@ -24,6 +24,7 @@
 WIDE = DIR_DEV * COLS
 CHUNK = 256
 NCHUNK = POOL // CHUNK
+PIECES = 4
 SEND_ROWS = SLOTS * PART + 8
 QBLOCKS = QROWS // BB
 
@@ -33,6 +34,11 @@
 SIN_C = (2.6417407853784525, -1.0859537956447276, 0.1306204657138272)
 COS_C = (1.681792784129167, -2.074822793580374, 0.42650038149094444, -0.03432262097868313)
 ROOT2 = 1.4142135623730951
+
+
+def own_place():
+    me = lax.axis_index("dir")
+    return me, me & 1, (lax.axis_index("tb") & 3) * (SLOTS * PART)
 
 
 def vmem():
@@ -69,9 +75,10 @@
     order_hbm, assign_hbm, lm_hbm, uv_hbm, spec_hbm, lm8_ref, uv8_ref, wide_ref,
     order_ref, assign_ref, lm_ref, uv_ref, spec_ref, pos_ref, sems
 ):
-    pairs = (
-        (assign_hbm, assign_ref), (order_hbm, order_ref), (lm_hbm, lm_ref), (uv_hbm, uv_ref), (spec_hbm, spec_ref)
-    )
+    pairs = [(assign_hbm, assign_ref), (order_hbm, order_ref), (lm_hbm, lm_ref), (uv_hbm, uv_ref)]
+    for n in range(PIECES):
+        piece = slice(n * (POOL // PIECES), (n + 1) * (POOL // PIECES))
+        pairs.append((spec_hbm.at[:, piece, :], spec_ref.at[:, piece, :]))
     copies = [pltpu.make_async_copy(src, dst, sems.at[n]) for n, (src, dst) in enumerate(pairs)]
     for copy in copies:
         copy.start()
@@ -99,8 +106,9 @@
     column = lax.broadcasted_iota(jnp.int32, (32, POOL), 1) // 128
     pick = (column == lax.broadcasted_iota(jnp.int32, (32, POOL), 0)).astype(F32).astype(BF16)
     pos_ref[...] = jnp.dot(pos.astype(BF16), pick, preferred_element_type=F32)
-    copies[4].wait()
     for column in range(POOL // 128):
+        if column % (POOL // 128 // PIECES) == 0:
+            copies[4 + column // (POOL // 128 // PIECES)].wait()
         place_here = pos_ref[:, column * 128 : (column + 1) * 128]
         for p in range(DIR_DEV):
             mask = jnp.where(place_here == float(p), 1.0, 0.0).astype(BF16)
@@ -128,7 +136,7 @@
             pltpu.VMEM((2, ROWS_DEV), BF16),
             pltpu.VMEM((2, POOL, COLS), BF16),
             pltpu.VMEM((128, POOL), F32),
-            pltpu.SemaphoreType.DMA((5,)),
+            pltpu.SemaphoreType.DMA((4 + PIECES,)),
         ],
         compiler_params=params(16),
         name="prepare",
@@ -138,10 +146,10 @@
     ))
 
 
-def predict_kernel(flips, ids_ref, uv8_ref, lm8_ref, wide_ref, *rest):
+def predict_kernel(flips, uv8_ref, lm8_ref, wide_ref, *rest):
     out_refs = rest[: len(flips)]
     tab_a, tab_b, acc_ref = rest[len(flips) :]
-    me = ids_ref[0]
+    me = own_place()[0]
     uv_rows = jnp.concatenate([uv8_ref[me ^ x].astype(F32).T for x in flips], axis=0).astype(BF16)
 
     def table(j, tab_ref):
@@ -166,7 +174,7 @@
             out_refs[n][p] = acc_ref[n * QROWS : (n + 1) * QROWS, p * COLS : (p + 1) * COLS].astype(BF16)
 
 
-def predict(flips, ids, uv8, lm8, wide):
+def predict(flips, uv8, lm8, wide):
     rows = QROWS * len(flips)
 
     def kernel(*refs):
@@ -175,7 +183,7 @@
     return pl.pallas_call(
         kernel,
         out_shape=tuple(jax.ShapeDtypeStruct((DIR_DEV, QROWS, COLS), BF16) for _ in flips),
-        in_specs=[smem(), vmem(), vmem(), vmem()],
+        in_specs=[vmem(), vmem(), vmem()],
         out_specs=tuple(vmem() for _ in flips),
         scratch_shapes=[
             pltpu.VMEM((rows, 2 * CHUNK), BF16),
@@ -189,7 +197,7 @@
         ),
         compiler_params=params(16),
         name="predict",
-    )(ids, uv8, lm8, wide)
+    )(uv8, lm8, wide)
 
 
 def per_block_sum(value):
@@ -225,9 +233,9 @@
 SHIFTS = tuple(range(-2 * (ITERS - 1), 2 * ITERS, 2))
 
 
-def peel_kernel(ids_ref, vis_ref, ridge_ref, m0_ref, m1_ref, m2_ref, m3_ref, out_ref, *rest):
+def peel_kernel(vis_ref, ridge_ref, m0_ref, m1_ref, m2_ref, m3_ref, out_ref, *rest):
     part_refs, (model_ref, inv_ref, band_ref, part_ref) = rest[:N_DIR], rest[N_DIR:]
-    me = ids_ref[0]
+    me = own_place()[0]
     ridge = ridge_ref[...]
     blocks = QROWS // GB
     for x, ref in enumerate((m0_ref, m1_ref, m2_ref, m3_ref)):
@@ -260,12 +268,12 @@
         part_refs[x][...] = part_ref[:, (me ^ x) & 1].astype(BF16)
 
 
-def peel(ids, visibilities, ridge_weight, models):
+def peel(visibilities, ridge_weight, models):
     out = pl.pallas_call(
         peel_kernel,
         out_shape=(jax.ShapeDtypeStruct((QROWS, COLS), BF16),)
         + (jax.ShapeDtypeStruct((QBLOCKS, PART, COLS), BF16),) * N_DIR,
-        in_specs=[smem()] + [vmem()] * 6,
+        in_specs=[vmem()] * 6,
         out_specs=(vmem(),) * (1 + N_DIR),
         scratch_shapes=[
             pltpu.VMEM((N_DIR * DIR_DEV, QROWS, COLS), F32),
@@ -275,13 +283,13 @@
         ],
         compiler_params=params(16),
         name="peel",
-    )(ids, visibilities, ridge_weight.reshape(1, COLS), *models)
+    )(visibilities, ridge_weight.reshape(1, COLS), *models)
     return out[0], out[1:]
 
 
-def label_kernel(ids_ref, tile_id_ref, tile_ref, uv_ref, out_ref, slot_ref, seen_ref):
-    half = ids_ref[1]
-    offset = ids_ref[2]
+def label_kernel(tile_id_ref, tile_ref, uv_ref, out_ref, slot_ref, seen_ref):
+    half = own_place()[1]
+    offset = own_place()[2]
     tiles = tile_ref[...].astype(F32)
     block_of_lane = lax.broadcasted_iota(jnp.int32, (NB, ROWS_DEV), 1) // BB
     expand = (block_of_lane == lax.broadcasted_iota(jnp.int32, (NB, ROWS_DEV), 0)).astype(F32)
@@ -316,23 +324,23 @@
         seen_ref[tile] = 1
 
 
-def label(ids, tile_ids, block_tile, uv_coords):
+def label(tile_ids, block_tile, uv_coords):
     return pl.pallas_call(
         label_kernel,
         out_shape=(
             jax.ShapeDtypeStruct((N_TB, SEND_ROWS, COLS), BF16),
             jax.ShapeDtypeStruct((NB,), jnp.int32),
         ),
-        in_specs=[smem(), smem(), vmem(), vmem()],
+        in_specs=[smem(), vmem(), vmem()],
         out_specs=(vmem(), smem()),
         scratch_shapes=[pltpu.SMEM((N_TB,), jnp.int32)],
         compiler_params=params(16),
         name="label",
-    )(ids, tile_ids, block_tile, uv_coords)
-
-
-def pack_kernel(ids_ref, tile_ref, slot_ref, r0_ref, r1_ref, r2_ref, r3_ref, base_ref, out_ref, stage_ref):
-    me = ids_ref[0]
+    )(tile_ids, block_tile, uv_coords)
+
+
+def pack_kernel(tile_ref, slot_ref, r0_ref, r1_ref, r2_ref, r3_ref, base_ref, out_ref, stage_ref):
+    me = own_place()[0]
     out_ref[...] = base_ref[...]
     for x, ref in enumerate((r0_ref, r1_ref, r2_ref, r3_ref)):
         stage_ref[pl.ds((me ^ x) * QBLOCKS, QBLOCKS)] = ref[...]
@@ -341,38 +349,38 @@
         out_ref[tile_ref[b], pl.ds(first, PART), :] = stage_ref[b]
 
 
-def pack(ids, tile_ids, slots, rows, base):
+def pack(tile_ids, slots, rows, base):
     return pl.pallas_call(
         pack_kernel,
         out_shape=jax.ShapeDtypeStruct((N_TB, SEND_ROWS, COLS), BF16),
-        in_specs=[smem(), smem(), smem()] + [vmem()] * 5,
+        in_specs=[smem(), smem()] + [vmem()] * 5,
         out_specs=vmem(),
         scratch_shapes=[pltpu.VMEM((NB, PART, COLS), BF16)],
         compiler_params=params(16),
         name="pack",
-    )(ids, tile_ids, slots, *rows, base)
-
-
-def join_kernel(ids_ref, r0_ref, r1_ref, r2_ref, r3_ref, out_ref):
-    me = ids_ref[0]
+    )(tile_ids, slots, *rows, base)
+
+
+def join_kernel(r0_ref, r1_ref, r2_ref, r3_ref, out_ref):
+    me = own_place()[0]
     for x, ref in enumerate((r0_ref, r1_ref, r2_ref, r3_ref)):
         out_ref[pl.ds(pl.multiple_of((me ^ x) * QROWS, QROWS), QROWS), :] = ref[...]
 
 
-def join(ids, rows):
+def join(rows):
     return pl.pallas_call(
         join_kernel,
         out_shape=jax.ShapeDtypeStruct((ROWS_DEV, COLS), BF16),
-        in_specs=[smem()] + [vmem()] * 4,
+        in_specs=[vmem()] * 4,
         out_specs=vmem(),
         compiler_params=params(16),
         name="join",
-    )(ids, *rows)
-
-
-def grid_kernel(ids_ref, got_ref, keep_ref, give_ref, tab_ref, acc_ref):
-    chip = ids_ref[0] // 2
-    half = ids_ref[1]
+    )(*rows)
+
+
+def grid_kernel(got_ref, keep_ref, give_ref, tab_ref, acc_ref):
+    chip = own_place()[0] // 2
+    half = own_place()[1]
     tiles = N_TB * SLOTS * PART // 128
     groups = N_TB // tiles
     coords = got_ref[:, SLOTS * PART :, :].astype(F32).reshape(tiles, groups, 8, COLS)
@@ -410,14 +418,14 @@
         give_ref[part] = total[part * 512 + 256 : part * 512 + 512]
 
 
-def grid_rows(ids, got):
+def grid_rows(got):
     return pl.pallas_call(
         grid_kernel,
         out_shape=(
             jax.ShapeDtypeStruct((2, PIX // N_DIR, COLS), F32),
             jax.ShapeDtypeStruct((2, PIX // N_DIR, COLS), F32),
         ),
-        in_specs=[smem(), vmem()],
+        in_specs=[vmem()],
         out_specs=(vmem(), vmem()),
         scratch_shapes=[
             pltpu.VMEM((N_TB * SLOTS * PART // 256, 1024, 256), BF16),
@@ -425,7 +433,7 @@
         ],
         compiler_params=params(24),
         name="grid",
-    )(ids, got)
+    )(got)
 
 
 def after(value, done):
@@ -439,23 +447,20 @@
 def local(
     visibilities, uv_coords, comp_lm, spectra, ridge_weight, assignment, peel_order, block_tile
 ):
-    me = lax.axis_index("dir")
-    station = lax.axis_index("tb")
-    ids = jnp.stack([me, me % 2, (station % 4) * (SLOTS * PART)]).astype(jnp.int32)
     lm8, uv8, wide = prepare(peel_order, assignment, comp_lm, uv_coords, spectra)
-    far_a, far_b = predict((2, 3), ids, uv8, lm8, wide)
+    far_a, far_b = predict((2, 3), uv8, lm8, wide)
     got_a, got_b = swap(far_a, 2), swap(far_b, 3)
-    near, own = predict((1, 0), ids, uv8, lm8, wide)
+    near, own = predict((1, 0), uv8, lm8, wide)
     got_near = swap(near, 1)
     tile_ids = block_tile[:, 0]
-    base, slots = label(after(ids, own), tile_ids, block_tile, uv_coords)
-    rows, parts = peel(after(ids, slots), visibilities, ridge_weight, (own, got_near, got_a, got_b))
+    base, slots = label(after(tile_ids, own), block_tile, uv_coords)
+    rows, parts = peel(after(visibilities, slots), ridge_weight, (own, got_near, got_a, got_b))
     shared = [parts[0]] + [swap(parts[x], x) for x in range(1, N_DIR)]
-    send = pack(ids, tile_ids, slots, shared, base)
+    send = pack(tile_ids, slots, shared, base)
     got = lax.all_to_all(send, "tb", split_axis=0, concat_axis=0, tiled=True)
     late = after(rows, send)
-    residual = join(ids, [late] + [swap(late, x) for x in range(1, N_DIR)])
-    keep, give = grid_rows(after(ids, residual), got)
+    residual = join([late] + [swap(late, x) for x in range(1, N_DIR)])
+    keep, give = grid_rows(after(got, residual))
     return residual, (keep + swap(give, 1))[None]
 
 

time: 72.5 us -> 70.9 us (0.978)
  Pallas kernels: 24.7 us -> 21.8 us
  waiting for transfers between devices: 19.3 us -> 20.2 us
    pallas_call x2, Pallas kernels: 12.4 us -> 11.2 us  [predict(): pl.pallas_call(kernel, out_shape=tuple((jax.ShapeDtypeStruct((DIR_DEV, QR...]
  transfers between devices with their start and end apart: 11 -> 11, of which waited for: 6 -> 6; matrix products, arithmetic and copies ran while one was open for 0% -> 0% of each run, Pallas kernels for 13% -> 11%
where the time goes in v6:
time: 70.9 us; the launch traced here: 70.6 us
  starting transfers between devices  27 us (38%)
  Pallas kernels  21.8 us (31%)
  waiting for transfers between devices  20.2 us (28%)
  between operations  0.76 us (1%)
  other arithmetic  0.74 us (1%)
    all_to_all x1, starting transfers between devices, local(): got = lax.all_to_all(send, 'tb', split_axis=0, concat_axis=0, tiled=True)  13.9 us
    ppermute x10, starting transfers between devices, swap(): return lax.ppermute(value, 'dir', [(i, i ^ flip) for i in range(N_DIR)])  13 us
    pallas_call x2, Pallas kernels, predict(): pl.pallas_call(kernel, out_shape=tuple((jax.ShapeDtypeStruct((DIR_DEV, QR...  11.2 us
    all_to_all x1, waiting for transfers between devices, local(): got = lax.all_to_all(send, 'tb', split_axis=0, concat_axis=0, tiled=True)  10.5 us
    ppermute x10, waiting for transfers between devices, swap(): return lax.ppermute(value, 'dir', [(i, i ^ flip) for i in range(N_DIR)])  9.74 us
    pallas_call x1, Pallas kernels, prepare(): pl.pallas_call(prepare_kernel, out_shape=(jax.ShapeDtypeStruct((8, POOL),...  2.89 us
    pallas_call x1, Pallas kernels, grid_rows(): pl.pallas_call(grid_kernel, out_shape=(jax.ShapeDtypeStruct((2, PIX // N_...  2.23 us
    pallas_call x1, Pallas kernels, peel(): pl.pallas_call(peel_kernel, out_shape=(jax.ShapeDtypeStruct((QROWS, COLS)...  1.71 us
  transfers between devices with their start and end apart: 11, of which 6 were waited for; matrix products, arithmetic and copies ran while one was open for 0% of the time, Pallas kernels for 11%

profile of v6, /device:TPU:1, one launch (start us, length us, event | category | flops | bytes accessed | tf_op | source)
XLA Modules:
  0.0 70.6 jit_solution(1321299431971912835)
XLA Ops:
  0.6 2.9 %prepare.1 = (bf16[8,3072]{1,0:T(8,128)(2,1)S(1)}, bf16[4,8,256]{2,1,0:T(8,128)(2,1)S(1)}, bf16[12,512,384]{2,1,0:T(8,128)(2,1)S(1)}) custom-call(s32[3]{0:T(128)} %order_hbm.1, s32[1,3072]{1,0:T(1,128)} %bitcast.8, f32[2,3072]{1,0:T(2,128)} %lm_hbm.1, bf16[2,1024]{1,0:T(2,128)(2,1)} %uv_ref.1, bf16[2,3072,128]{2,1,0:T(8,128)(2,1)} %spec_hbm.1), custom_call_target="tpu_custom_call" | custom-call | tf_op jit(solution)/shard_map/prepare/pallas_call | solution.py:123
  3.5 5.6 %predict.3 = (bf16[3,256,128]{2,1,0:T(8,128)(2,1)S(1)}, bf16[3,256,128]{2,1,0:T(8,128)(2,1)S(1)}) custom-call(bf16[4,8,256]{2,1,0:T(8,128)(2,1)S(1)} %get-tuple-element.22.refs_0_, bf16[8,3072]{1,0:T(8,128)(2,1)S(1)} %get-tuple-element.23.refs_1_, bf16[12,512,384]{2,1,0:T(8,128)(2,1)S(1)} %get-tuple-element.24.refs_2_), custom_call_target="tpu_custom_call" | custom-call | flops 4831838208 | bytes 5111808 | tf_op jit(solution)/shard_map/predict/pallas_call | solution.py:183
  9.1 2.1 %collective-permute-start.1 = (bf16[3,256,128]{2,1,0:T(8,128)(2,1)S(1)}, bf16[3,256,128]{2,1,0:T(8,128)(2,1)S(1)}, u32[]{:S(2)}, u32[]{:S(2)}) collective-permute-start(bf16[3,256,128]{2,1,0:T(8,128)(2,1)S(1)} %get-tuple-element.30), channel_id=1, source_target_pairs={{0,128},{64,192},{128,0},{192,64},{1,129},{65,193},{129,1},{193,65... | collective-permute-start | bytes 589832 | tf_op jit(solution)/shard_map/ppermute | solution.py:444
  11.3 3.1 %collective-permute-start.2 = (bf16[3,256,128]{2,1,0:T(8,128)(2,1)S(1)}, bf16[3,256,128]{2,1,0:T(8,128)(2,1)S(1)}, u32[]{:S(2)}, u32[]{:S(2)}) collective-permute-start(bf16[3,256,128]{2,1,0:T(8,128)(2,1)S(1)} %get-tuple-element.31), channel_id=1, source_target_pairs={{0,192},{64,128},{128,64},{192,0},{1,193},{65,129},{129,65},{193,1... | collective-permute-start | bytes 589832 | tf_op jit(solution)/shard_map/ppermute | solution.py:444
  14.4 5.6 %predict.2 = (bf16[3,256,128]{2,1,0:T(8,128)(2,1)S(1)}, bf16[3,256,128]{2,1,0:T(8,128)(2,1)S(1)}) custom-call(bf16[4,8,256]{2,1,0:T(8,128)(2,1)S(1)} %get-tuple-element.22.refs_0_, bf16[8,3072]{1,0:T(8,128)(2,1)S(1)} %get-tuple-element.23.refs_1_, bf16[12,512,384]{2,1,0:T(8,128)(2,1)S(1)} %get-tuple-element.24.refs_2_), custom_call_target="tpu_custom_call" | custom-call | flops 4831838208 | bytes 5111808 | tf_op jit(solution)/shard_map/predict/pallas_call | solution.py:183
  20.2 1.6 %label.1 = (bf16[64,40,128]{2,1,0:T(8,128)(2,1)S(1)}, s32[32]{0:T(128)S(1)}) custom-call(s32[32]{0:T(128)S(1)} %bitcast.5, s32[32,1]{1,0:T(8,128)S(1)} %copy.10.tile_ref, bf16[2,1024]{1,0:T(2,128)(2,1)S(1)} %copy-done.1), custom_call_target="tpu_custom_call" | custom-call | tf_op jit(solution)/shard_map/label/pallas_call | solution.py:328
  21.8 1.7 %peel.1 = (bf16[256,128]{1,0:T(8,128)(2,1)S(1)}, bf16[8,16,128]{2,1,0:T(8,128)(2,1)S(1)}, bf16[8,16,128]{2,1,0:T(8,128)(2,1)S(1)}, bf16[8,16,128]{2,1,0:T(8,128)(2,1)S(1)}, bf16[8,16,128]{2,1,0:T(8,128)(2,1)S(1)}) custom-call(bf16[1024,128]{1,0:T(8,128)(2,1)S(1)} %copy-done, f32[1,128]{1,0:T(1,128)S(1)} %bitcast.7, ...), custom_call_target="tpu_custom_call" | custom-call | tf_op jit(solution)/shard_map/peel/pallas_call | solution.py:272
  23.5 0.6 collective-permute-start.3
  24.1 1.7 %collective-permute-start.5 = (bf16[8,16,128]{2,1,0:T(8,128)(2,1)S(1)}, bf16[8,16,128]{2,1,0:T(8,128)(2,1)S(1)}, u32[]{:S(2)}, u32[]{:S(2)}) collective-permute-start(bf16[8,16,128]{2,1,0:T(8,128)(2,1)S(1)} %get-tuple-element.36), channel_id=1, source_target_pairs={{0,192},{64,128},{128,64},{192,0},{1,193},{65,129},{129,65},{193,1... | collective-permute-start | bytes 98312 | tf_op jit(solution)/shard_map/ppermute | solution.py:444
  25.8 1.0 %collective-permute-done.4.r2_ref = bf16[8,16,128]{2,1,0:T(8,128)(2,1)S(1)} collective-permute-done((bf16[8,16,128]{2,1,0:T(8,128)(2,1)S(1)}, bf16[8,16,128]{2,1,0:T(8,128)(2,1)S(1)}, u32[]{:S(2)}, u32[]{:S(2)}) %collective-permute-start.4) | collective-permute-done | bytes 32800 | tf_op jit(solution)/shard_map/ppermute | solution.py:444
  26.9 1.2 %collective-permute-done.5.r3_ref = bf16[8,16,128]{2,1,0:T(8,128)(2,1)S(1)} collective-permute-done((bf16[8,16,128]{2,1,0:T(8,128)(2,1)S(1)}, bf16[8,16,128]{2,1,0:T(8,128)(2,1)S(1)}, u32[]{:S(2)}, u32[]{:S(2)}) %collective-permute-start.5) | collective-permute-done | bytes 32800 | tf_op jit(solution)/shard_map/ppermute | solution.py:444
  28.1 1.5 %pack.1 = bf16[64,40,128]{2,1,0:T(8,128)(2,1)} custom-call(s32[32]{0:T(128)S(1)} %bitcast.6, s32[32]{0:T(128)S(1)} %get-tuple-element.27.slot_ref, bf16[8,16,128]{2,1,0:T(8,128)(2,1)S(1)} %get-tuple-element.33.r0_ref, bf16[8,16,128]{2,1,0:T(8,128)(2,1)S(1)} %collective-permute-done.3.r1_ref, bf16[8,16,128]{2,1,0:T(8,128)(2,1)S(1)} %collective-permute-done.4.r2_ref, ...), custom_call_target="tpu_custom_call" | custom-call | tf_op jit(solution)/shard_map/pack/pallas_call | solution.py:353
  29.6 13.9 %all-to-all-start = ((bf16[64,40,128]{2,1,0:T(8,128)(2,1)}), bf16[64,40,128]{2,1,0:T(8,128)(2,1)S(1)}, u32[]{:S(2)}, u32[]{:S(2)}) async-start(bf16[64,40,128]{2,1,0:T(8,128)(2,1)} %pack.1), calls=%async_computation | async-start | bytes 1310720 | tf_op jit(solution)/shard_map/all_to_all | solution.py:460
  43.5 0.6 collective-permute-start.8
  44.1 1.5 %collective-permute-start.7 = (bf16[256,128]{1,0:T(8,128)(2,1)S(1)}, bf16[256,128]{1,0:T(8,128)(2,1)S(1)}, u32[]{:S(2)}, u32[]{:S(2)}) collective-permute-start(bf16[256,128]{1,0:T(8,128)(2,1)S(1)} %get-tuple-element.38.r0_ref), channel_id=1, source_target_pairs={{0,128},{64,192},{128,0},{192,64},{1,129},{65,193},{129,1},{193,65... | collective-permute-start | bytes 196616 | tf_op jit(solution)/shard_map/ppermute | solution.py:444
  45.6 0.1 collective-permute-start.6
  45.7 3.7 %collective-permute-done.8.r3_ref = bf16[256,128]{1,0:T(8,128)(2,1)S(1)} collective-permute-done((bf16[256,128]{1,0:T(8,128)(2,1)S(1)}, bf16[256,128]{1,0:T(8,128)(2,1)S(1)}, u32[]{:S(2)}, u32[]{:S(2)}) %collective-permute-start.8) | collective-permute-done | bytes 65568 | tf_op jit(solution)/shard_map/ppermute | solution.py:444
  49.4 2.7 %collective-permute-done.7.r2_ref = bf16[256,128]{1,0:T(8,128)(2,1)S(1)} collective-permute-done((bf16[256,128]{1,0:T(8,128)(2,1)S(1)}, bf16[256,128]{1,0:T(8,128)(2,1)S(1)}, u32[]{:S(2)}, u32[]{:S(2)}) %collective-permute-start.7) | collective-permute-done | bytes 65568 | tf_op jit(solution)/shard_map/ppermute | solution.py:444
  52.1 0.7 %join.1 = bf16[1024,128]{1,0:T(8,128)(2,1)} custom-call(bf16[256,128]{1,0:T(8,128)(2,1)S(1)} %get-tuple-element.38.r0_ref, bf16[256,128]{1,0:T(8,128)(2,1)S(1)} %collective-permute-done.6.r1_ref, bf16[256,128]{1,0:T(8,128)(2,1)S(1)} %collective-permute-done.7.r2_ref, bf16[256,128]{1,0:T(8,128)(2,1)S(1)} %collective-permute-done.8.r3_ref), custom_call_target="tpu_custom_call" | custom-call | tf_op jit(solution)/shard_map/join/pallas_call | solution.py:371
  52.8 10.5 %all-to-all-done.got_ref = bf16[64,40,128]{2,1,0:T(8,128)(2,1)S(1)} async-done(((bf16[64,40,128]{2,1,0:T(8,128)(2,1)}), bf16[64,40,128]{2,1,0:T(8,128)(2,1)S(1)}, u32[]{:S(2)}, u32[]{:S(2)}) %all-to-all-start) | async-done | bytes 655392 | tf_op jit(solution)/shard_map/all_to_all | solution.py:460
  63.3 2.2 %grid.1 = (f32[2,256,128]{2,1,0:T(8,128)S(1)}, f32[2,256,128]{2,1,0:T(8,128)S(1)}) custom-call(bf16[64,40,128]{2,1,0:T(8,128)(2,1)S(1)} %all-to-all-done.got_ref), custom_call_target="tpu_custom_call" | custom-call | tf_op jit(solution)/shard_map/grid/pallas_call | solution.py:422
  65.5 3.2 %collective-permute-start.9 = (f32[2,256,128]{2,1,0:T(8,128)S(1)}, f32[2,256,128]{2,1,0:T(8,128)S(1)}, u32[]{:S(2)}, u32[]{:S(2)}) collective-permute-start(f32[2,256,128]{2,1,0:T(8,128)S(1)} %get-tuple-element.41), channel_id=1, source_target_pairs={{0,64},{64,0},{128,192},{192,128},{1,65},{65,1},{129,193},{193,129... | collective-permute-start | bytes 786440 | tf_op jit(solution)/shard_map/ppermute | solution.py:444
  68.7 1.2 %collective-permute-done.9 = f32[2,256,128]{2,1,0:T(8,128)S(1)} collective-permute-done((f32[2,256,128]{2,1,0:T(8,128)S(1)}, f32[2,256,128]{2,1,0:T(8,128)S(1)}, u32[]{:S(2)}, u32[]{:S(2)}) %collective-permute-start.9) | collective-permute-done | bytes 262176 | tf_op jit(solution)/shard_map/ppermute | solution.py:444
  69.9 0.7 %add_bitcast_fusion = f32[1,2,256,128]{3,2,1,0:T(8,128)} fusion(f32[2,256,128]{2,1,0:T(8,128)S(1)} %get-tuple-element.40, f32[2,256,128]{2,1,0:T(8,128)S(1)} %collective-permute-done.9), kind=kLoop, calls=%fused_computation | loop fusion | flops 65536 | bytes 786432 | tf_op jit(solution)/shard_map/broadcast_in_dim | solution.py:464
  (16 shorter events, 0.2 us)
Async XLA Ops:
  9.1 12.6 %collective-permute-start.1 = (bf16[3,256,128]{2,1,0:T(8,128)(2,1)S(1)}, bf16[3,256,128]{2,1,0:T(8,128)(2,1)S(1)}, u32[]{:S(2)}, u32[]{:S(2)}) collective-permute-start(bf16[3,256,128]{2,1,0:T(8,128)(2,1)S(1)} %get-tuple-element.30), channel_id=1, source_target_pairs={{0,128},{64,192},{128,0},{192,64},{1,129},{65,193},{129,1},{193,65... | collective-permute-start | bytes 589832 | tf_op jit(solution)/shard_map/ppermute | solution.py:444
  11.3 8.8 %copy-start.2 = (s32[32,1]{0,1:T(1,128)S(1)}, s32[32,1]{0,1:T(1,128)}, u32[]{:S(2)}) copy-start(s32[32,1]{0,1:T(1,128)} %param.15) | copy-start | bytes 388
  11.3 8.9 %copy-start.1 = (bf16[2,1024]{1,0:T(2,128)(2,1)S(1)}, bf16[2,1024]{1,0:T(2,128)(2,1)}, u32[]{:S(2)}) copy-start(bf16[2,1024]{1,0:T(2,128)(2,1)} %uv_ref.1) | copy-start | bytes 12292
  11.3 10.5 %copy-start = (bf16[1024,128]{1,0:T(8,128)(2,1)S(1)}, bf16[1024,128]{1,0:T(8,128)(2,1)}, u32[]{:S(2)}) copy-start(bf16[1024,128]{1,0:T(8,128)(2,1)} %vis_ref) | copy-start | bytes 786436
  11.3 10.5 %copy-start.3 = (f32[128]{0:T(128)S(1)}, f32[128]{0:T(128)}, u32[]{:S(2)}) copy-start(f32[128]{0:T(128)} %param.12) | copy-start | bytes 1540
  11.3 10.5 %collective-permute-start.2 = (bf16[3,256,128]{2,1,0:T(8,128)(2,1)S(1)}, bf16[3,256,128]{2,1,0:T(8,128)(2,1)S(1)}, u32[]{:S(2)}, u32[]{:S(2)}) collective-permute-start(bf16[3,256,128]{2,1,0:T(8,128)(2,1)S(1)} %get-tuple-element.31), channel_id=1, source_target_pairs={{0,192},{64,128},{128,64},{192,0},{1,193},{65,129},{129,65},{193,1... | collective-permute-start | bytes 589832 | tf_op jit(solution)/shard_map/ppermute | solution.py:444
  20.0 1.8 %collective-permute-start = (bf16[3,256,128]{2,1,0:T(8,128)(2,1)S(1)}, bf16[3,256,128]{2,1,0:T(8,128)(2,1)S(1)}, u32[]{:S(2)}, u32[]{:S(2)}) collective-permute-start(bf16[3,256,128]{2,1,0:T(8,128)(2,1)S(1)} %get-tuple-element.29), channel_id=1, source_target_pairs={{0,64},{64,0},{128,192},{192,128},{1,65},{65,1},{129,193},{193,129... | collective-permute-start | bytes 589832 | tf_op jit(solution)/shard_map/ppermute | solution.py:444
  23.5 2.3 %collective-permute-start.3 = (bf16[8,16,128]{2,1,0:T(8,128)(2,1)S(1)}, bf16[8,16,128]{2,1,0:T(8,128)(2,1)S(1)}, u32[]{:S(2)}, u32[]{:S(2)}) collective-permute-start(bf16[8,16,128]{2,1,0:T(8,128)(2,1)S(1)} %get-tuple-element.34), channel_id=1, source_target_pairs={{0,64},{64,0},{128,192},{192,128},{1,65},{65,1},{129,193},{193,129... | collective-permute-start | bytes 98312 | tf_op jit(solution)/shard_map/ppermute | solution.py:444
  24.1 2.8 %collective-permute-start.4 = (bf16[8,16,128]{2,1,0:T(8,128)(2,1)S(1)}, bf16[8,16,128]{2,1,0:T(8,128)(2,1)S(1)}, u32[]{:S(2)}, u32[]{:S(2)}) collective-permute-start(bf16[8,16,128]{2,1,0:T(8,128)(2,1)S(1)} %get-tuple-element.35), channel_id=1, source_target_pairs={{0,128},{64,192},{128,0},{192,64},{1,129},{65,193},{129,1},{193,65... | collective-permute-start | bytes 98312 | tf_op jit(solution)/shard_map/ppermute | solution.py:444
  24.1 4.0 %collective-permute-start.5 = (bf16[8,16,128]{2,1,0:T(8,128)(2,1)S(1)}, bf16[8,16,128]{2,1,0:T(8,128)(2,1)S(1)}, u32[]{:S(2)}, u32[]{:S(2)}) collective-permute-start(bf16[8,16,128]{2,1,0:T(8,128)(2,1)S(1)} %get-tuple-element.36), channel_id=1, source_target_pairs={{0,192},{64,128},{128,64},{192,0},{1,193},{65,129},{129,65},{193,1... | collective-permute-start | bytes 98312 | tf_op jit(solution)/shard_map/ppermute | solution.py:444
  29.6 33.7 %all-to-all-start = ((bf16[64,40,128]{2,1,0:T(8,128)(2,1)}), bf16[64,40,128]{2,1,0:T(8,128)(2,1)S(1)}, u32[]{:S(2)}, u32[]{:S(2)}) async-start(bf16[64,40,128]{2,1,0:T(8,128)(2,1)} %pack.1), calls=%async_computation | async-start | bytes 1310720 | tf_op jit(solution)/shard_map/all_to_all | solution.py:460
  43.5 5.9 %collective-permute-start.8 = (bf16[256,128]{1,0:T(8,128)(2,1)S(1)}, bf16[256,128]{1,0:T(8,128)(2,1)S(1)}, u32[]{:S(2)}, u32[]{:S(2)}) collective-permute-start(bf16[256,128]{1,0:T(8,128)(2,1)S(1)} %get-tuple-element.38.r0_ref), channel_id=1, source_target_pairs={{0,192},{64,128},{128,64},{192,0},{1,193},{65,129},{129,65},{193,1... | collective-permute-start | bytes 196616 | tf_op jit(solution)/shard_map/ppermute | solution.py:444
  44.1 8.0 %collective-permute-start.7 = (bf16[256,128]{1,0:T(8,128)(2,1)S(1)}, bf16[256,128]{1,0:T(8,128)(2,1)S(1)}, u32[]{:S(2)}, u32[]{:S(2)}) collective-permute-start(bf16[256,128]{1,0:T(8,128)(2,1)S(1)} %get-tuple-element.38.r0_ref), channel_id=1, source_target_pairs={{0,128},{64,192},{128,0},{192,64},{1,129},{65,193},{129,1},{193,65... | collective-permute-start | bytes 196616 | tf_op jit(solution)/shard_map/ppermute | solution.py:444
  45.6 6.5 %collective-permute-start.6 = (bf16[256,128]{1,0:T(8,128)(2,1)S(1)}, bf16[256,128]{1,0:T(8,128)(2,1)S(1)}, u32[]{:S(2)}, u32[]{:S(2)}) collective-permute-start(bf16[256,128]{1,0:T(8,128)(2,1)S(1)} %get-tuple-element.38.r0_ref), channel_id=1, source_target_pairs={{0,64},{64,0},{128,192},{192,128},{1,65},{65,1},{129,193},{193,129... | collective-permute-start | bytes 196616 | tf_op jit(solution)/shard_map/ppermute | solution.py:444
  65.5 4.3 %collective-permute-start.9 = (f32[2,256,128]{2,1,0:T(8,128)S(1)}, f32[2,256,128]{2,1,0:T(8,128)S(1)}, u32[]{:S(2)}, u32[]{:S(2)}) collective-permute-start(f32[2,256,128]{2,1,0:T(8,128)S(1)} %get-tuple-element.41), channel_id=1, source_target_pairs={{0,64},{64,0},{128,192},{192,128},{1,65},{65,1},{129,193},{193,129... | collective-permute-start | bytes 786440 | tf_op jit(solution)/shard_map/ppermute | solution.py:444

commit v7 on v6

--- a/solution.py
+++ b/solution.py
@@ -287,9 +287,8 @@
     return out[0], out[1:]
 
 
-def label_kernel(tile_id_ref, tile_ref, uv_ref, out_ref, slot_ref, seen_ref):
-    half = own_place()[1]
-    offset = own_place()[2]
+def label_kernel(tile_ref, uv_ref, coords_ref, place_ref):
+    me, half, offset = own_place()
     tiles = tile_ref[...].astype(F32)
     block_of_lane = lax.broadcasted_iota(jnp.int32, (NB, ROWS_DEV), 1) // BB
     expand = (block_of_lane == lax.broadcasted_iota(jnp.int32, (NB, ROWS_DEV), 0)).astype(F32)
@@ -298,6 +297,15 @@
     col = lax.broadcasted_iota(jnp.int32, (NB, NB), 1)
     tile_row = jnp.sum(jnp.where(sub == col, tiles, 0.0), axis=0, keepdims=True)
     slot = jnp.sum(jnp.where((tiles == tile_row) & (col < sub), 1.0, 0.0), axis=1, keepdims=True)
+    part_lane = lax.broadcasted_iota(jnp.int32, (NB, NB * PART), 1)
+    block = ((part_lane // (QBLOCKS * PART)) ^ me) * QBLOCKS + (part_lane // PART) % QBLOCKS
+    mine = block == lax.broadcasted_iota(jnp.int32, (NB, NB * PART), 0)
+    first = (tiles * SLOTS + slot) * PART
+    goal_row = jnp.sum(jnp.where(mine, first, 0.0), axis=0, keepdims=True).astype(jnp.int32)
+    goal_row = goal_row + part_lane[0:1] % PART
+    for n in range(N_TB * SLOTS * PART // 512):
+        row = lax.broadcasted_iota(jnp.int32, (512, NB * PART), 0) + n * 512
+        place_ref[n * 512 : (n + 1) * 512, :] = jnp.where(row == goal_row, 1.0, 0.0).astype(BF16)
     slot_of_row = lax.dot_general(
         expand.astype(BF16),
         jnp.broadcast_to(slot, (NB, COLS)).astype(BF16),
@@ -314,51 +322,45 @@
     value = jnp.where(row % 8 == 0, u, jnp.where(row % 8 == 1, v, 0.0))
     value = jnp.where((row // 8).astype(F32) == tile_of_lane, value, 0.0).astype(BF16)
     out = jnp.dot(value, spot, preferred_element_type=F32)
-    out_ref[:, : SLOTS * PART, :] = jnp.zeros((N_TB, SLOTS * PART, COLS), BF16)
-    out_ref[:, SLOTS * PART :, :] = out.reshape(N_TB, 8, COLS).astype(BF16)
-    for t in range(N_TB):
-        seen_ref[t] = 0
-    for b in range(NB):
-        tile = tile_id_ref[b]
-        slot_ref[b] = seen_ref[tile]
-        seen_ref[tile] = 1
-
-
-def label(tile_ids, block_tile, uv_coords):
+    coords_ref[...] = out.reshape(N_TB, 8, COLS).astype(BF16)
+
+
+def label(block_tile, uv_coords):
     return pl.pallas_call(
         label_kernel,
         out_shape=(
-            jax.ShapeDtypeStruct((N_TB, SEND_ROWS, COLS), BF16),
-            jax.ShapeDtypeStruct((NB,), jnp.int32),
+            jax.ShapeDtypeStruct((N_TB, 8, COLS), BF16),
+            jax.ShapeDtypeStruct((N_TB * SLOTS * PART, NB * PART), BF16),
         ),
-        in_specs=[smem(), vmem(), vmem()],
-        out_specs=(vmem(), smem()),
-        scratch_shapes=[pltpu.SMEM((N_TB,), jnp.int32)],
-        compiler_params=params(16),
+        in_specs=[vmem(), vmem()],
+        out_specs=(vmem(), vmem()),
+        compiler_params=params(24),
         name="label",
-    )(tile_ids, block_tile, uv_coords)
-
-
-def pack_kernel(tile_ref, slot_ref, r0_ref, r1_ref, r2_ref, r3_ref, base_ref, out_ref, stage_ref):
-    me = own_place()[0]
-    out_ref[...] = base_ref[...]
-    for x, ref in enumerate((r0_ref, r1_ref, r2_ref, r3_ref)):
-        stage_ref[pl.ds((me ^ x) * QBLOCKS, QBLOCKS)] = ref[...]
-    for b in range(NB):
-        first = pl.multiple_of(slot_ref[b] * PART, PART)
-        out_ref[tile_ref[b], pl.ds(first, PART), :] = stage_ref[b]
-
-
-def pack(tile_ids, slots, rows, base):
+    )(block_tile, uv_coords)
+
+
+def pack_kernel(r0_ref, r1_ref, r2_ref, r3_ref, coords_ref, place_ref, out_ref):
+    rows = jnp.concatenate(
+        [ref[...].reshape(QBLOCKS * PART, COLS) for ref in (r0_ref, r1_ref, r2_ref, r3_ref)], axis=0
+    )
+    tiles = 512 // (SLOTS * PART)
+    for n in range(N_TB // tiles):
+        placed = jnp.dot(place_ref[n * 512 : (n + 1) * 512, :], rows, preferred_element_type=F32)
+        out_ref[n * tiles : (n + 1) * tiles, : SLOTS * PART, :] = placed.reshape(
+            tiles, SLOTS * PART, COLS
+        ).astype(BF16)
+    out_ref[:, SLOTS * PART :, :] = coords_ref[...]
+
+
+def pack(rows, coords, place):
     return pl.pallas_call(
         pack_kernel,
         out_shape=jax.ShapeDtypeStruct((N_TB, SEND_ROWS, COLS), BF16),
-        in_specs=[smem(), smem()] + [vmem()] * 5,
+        in_specs=[vmem()] * 6,
         out_specs=vmem(),
-        scratch_shapes=[pltpu.VMEM((NB, PART, COLS), BF16)],
         compiler_params=params(16),
         name="pack",
-    )(tile_ids, slots, *rows, base)
+    )(*rows, coords, place)
 
 
 def join_kernel(r0_ref, r1_ref, r2_ref, r3_ref, out_ref):
@@ -452,11 +454,10 @@
     got_a, got_b = swap(far_a, 2), swap(far_b, 3)
     near, own = predict((1, 0), uv8, lm8, wide)
     got_near = swap(near, 1)
-    tile_ids = block_tile[:, 0]
-    base, slots = label(after(tile_ids, own), block_tile, uv_coords)
-    rows, parts = peel(after(visibilities, slots), ridge_weight, (own, got_near, got_a, got_b))
+    rows, parts = peel(visibilities, ridge_weight, (own, got_near, got_a, got_b))
+    coords, place = label(after(block_tile, rows), uv_coords)
     shared = [parts[0]] + [swap(parts[x], x) for x in range(1, N_DIR)]
-    send = pack(tile_ids, slots, shared, base)
+    send = pack(shared, coords, place)
     got = lax.all_to_all(send, "tb", split_axis=0, concat_axis=0, tiled=True)
     late = after(rows, send)
     residual = join([late] + [swap(late, x) for x in range(1, N_DIR)])

time: 70.9 us -> 71 us (level)
  transfers between devices with their start and end apart: 11 -> 11, of which waited for: 6 -> 7; matrix products, arithmetic and copies ran while one was open for 0% -> 0% of each run, Pallas kernels for 11% -> 11%
where the time goes in v7:
time: 71 us; the launch traced here: 70.7 us
  starting transfers between devices  27.4 us (39%)
  Pallas kernels  21.8 us (31%)
  waiting for transfers between devices  19.9 us (28%)
  other arithmetic  0.74 us (1%)
  between operations  0.73 us (1%)
    all_to_all x1, starting transfers between devices, local(): got = lax.all_to_all(send, 'tb', split_axis=0, concat_axis=0, tiled=True)  14 us
    ppermute x10, starting transfers between devices, swap(): return lax.ppermute(value, 'dir', [(i, i ^ flip) for i in range(N_DIR)])  13.4 us
    pallas_call x2, Pallas kernels, predict(): pl.pallas_call(kernel, out_shape=tuple((jax.ShapeDtypeStruct((DIR_DEV, QR...  11.2 us
    all_to_all x1, waiting for transfers between devices, local(): got = lax.all_to_all(send, 'tb', split_axis=0, concat_axis=0, tiled=True)  10.2 us
    ppermute x10, waiting for transfers between devices, swap(): return lax.ppermute(value, 'dir', [(i, i ^ flip) for i in range(N_DIR)])  9.67 us
    pallas_call x1, Pallas kernels, prepare(): pl.pallas_call(prepare_kernel, out_shape=(jax.ShapeDtypeStruct((8, POOL),...  2.89 us
    pallas_call x1, Pallas kernels, grid_rows(): pl.pallas_call(grid_kernel, out_shape=(jax.ShapeDtypeStruct((2, PIX // N_...  2.23 us
    pallas_call x1, Pallas kernels, peel(): pl.pallas_call(peel_kernel, out_shape=(jax.ShapeDtypeStruct((QROWS, COLS)...  1.7 us
  transfers between devices with their start and end apart: 11, of which 7 were waited for; matrix products, arithmetic and copies ran while one was open for 0% of the time, Pallas kernels for 11%

profile of v7, /device:TPU:1, one launch (start us, length us, event | category | flops | bytes accessed | tf_op | source)
XLA Modules:
  0.0 70.7 jit_solution(10943384921852148306)
XLA Ops:
  0.6 2.9 %prepare.1 = (bf16[8,3072]{1,0:T(8,128)(2,1)S(1)}, bf16[4,8,256]{2,1,0:T(8,128)(2,1)S(1)}, bf16[12,512,384]{2,1,0:T(8,128)(2,1)S(1)}) custom-call(s32[3]{0:T(128)} %order_hbm.1, s32[1,3072]{1,0:T(1,128)} %bitcast.5, f32[2,3072]{1,0:T(2,128)} %lm_hbm.1, bf16[2,1024]{1,0:T(2,128)(2,1)} %uv_ref.1, bf16[2,3072,128]{2,1,0:T(8,128)(2,1)} %spec_hbm.1), custom_call_target="tpu_custom_call" | custom-call | tf_op jit(solution)/shard_map/prepare/pallas_call | solution.py:123
  3.5 5.6 %predict.3 = (bf16[3,256,128]{2,1,0:T(8,128)(2,1)S(1)}, bf16[3,256,128]{2,1,0:T(8,128)(2,1)S(1)}) custom-call(bf16[4,8,256]{2,1,0:T(8,128)(2,1)S(1)} %get-tuple-element.21.refs_0_, bf16[8,3072]{1,0:T(8,128)(2,1)S(1)} %get-tuple-element.22.refs_1_, bf16[12,512,384]{2,1,0:T(8,128)(2,1)S(1)} %get-tuple-element.23.refs_2_), custom_call_target="tpu_custom_call" | custom-call | flops 4831838208 | bytes 5111808 | tf_op jit(solution)/shard_map/predict/pallas_call | solution.py:183
  9.2 2.1 %collective-permute-start.1 = (bf16[3,256,128]{2,1,0:T(8,128)(2,1)S(1)}, bf16[3,256,128]{2,1,0:T(8,128)(2,1)S(1)}, u32[]{:S(2)}, u32[]{:S(2)}) collective-permute-start(bf16[3,256,128]{2,1,0:T(8,128)(2,1)S(1)} %get-tuple-element.26), channel_id=1, source_target_pairs={{0,128},{64,192},{128,0},{192,64},{1,129},{65,193},{129,1},{193,65... | collective-permute-start | bytes 589832 | tf_op jit(solution)/shard_map/ppermute | solution.py:446
  11.3 3.1 %collective-permute-start.2 = (bf16[3,256,128]{2,1,0:T(8,128)(2,1)S(1)}, bf16[3,256,128]{2,1,0:T(8,128)(2,1)S(1)}, u32[]{:S(2)}, u32[]{:S(2)}) collective-permute-start(bf16[3,256,128]{2,1,0:T(8,128)(2,1)S(1)} %get-tuple-element.27), channel_id=1, source_target_pairs={{0,192},{64,128},{128,64},{192,0},{1,193},{65,129},{129,65},{193,1... | collective-permute-start | bytes 589832 | tf_op jit(solution)/shard_map/ppermute | solution.py:446
  14.4 5.6 %predict.2 = (bf16[3,256,128]{2,1,0:T(8,128)(2,1)S(1)}, bf16[3,256,128]{2,1,0:T(8,128)(2,1)S(1)}) custom-call(bf16[4,8,256]{2,1,0:T(8,128)(2,1)S(1)} %get-tuple-element.21.refs_0_, bf16[8,3072]{1,0:T(8,128)(2,1)S(1)} %get-tuple-element.22.refs_1_, bf16[12,512,384]{2,1,0:T(8,128)(2,1)S(1)} %get-tuple-element.23.refs_2_), custom_call_target="tpu_custom_call" | custom-call | flops 4831838208 | bytes 5111808 | tf_op jit(solution)/shard_map/predict/pallas_call | solution.py:183
  20.1 1.3 %collective-permute-done.2.m3_ref = bf16[3,256,128]{2,1,0:T(8,128)(2,1)S(1)} collective-permute-done((bf16[3,256,128]{2,1,0:T(8,128)(2,1)S(1)}, bf16[3,256,128]{2,1,0:T(8,128)(2,1)S(1)}, u32[]{:S(2)}, u32[]{:S(2)}) %collective-permute-start.2) | collective-permute-done | bytes 196640 | tf_op jit(solution)/shard_map/ppermute | solution.py:446
  21.5 1.7 %peel.1 = (bf16[256,128]{1,0:T(8,128)(2,1)S(1)}, bf16[8,16,128]{2,1,0:T(8,128)(2,1)S(1)}, bf16[8,16,128]{2,1,0:T(8,128)(2,1)S(1)}, bf16[8,16,128]{2,1,0:T(8,128)(2,1)S(1)}, bf16[8,16,128]{2,1,0:T(8,128)(2,1)S(1)}) custom-call(bf16[1024,128]{1,0:T(8,128)(2,1)S(1)} %copy-done, f32[1,128]{1,0:T(1,128)S(1)} %bitcast.4, ...), custom_call_target="tpu_custom_call" | custom-call | tf_op jit(solution)/shard_map/peel/pallas_call | solution.py:272
  23.3 0.2 collective-permute-start.3
  23.5 0.5 collective-permute-start.4
  24.0 1.5 %collective-permute-start.5 = (bf16[8,16,128]{2,1,0:T(8,128)(2,1)S(1)}, bf16[8,16,128]{2,1,0:T(8,128)(2,1)S(1)}, u32[]{:S(2)}, u32[]{:S(2)}) collective-permute-start(bf16[8,16,128]{2,1,0:T(8,128)(2,1)S(1)} %get-tuple-element.32), channel_id=1, source_target_pairs={{0,192},{64,128},{128,64},{192,0},{1,193},{65,129},{129,65},{193,1... | collective-permute-start | bytes 98312 | tf_op jit(solution)/shard_map/ppermute | solution.py:446
  25.6 1.5 %label.1 = (bf16[64,8,128]{2,1,0:T(8,128)(2,1)S(1)}, bf16[2048,512]{1,0:T(8,128)(2,1)S(1)}) custom-call(s32[32,1]{1,0:T(8,128)S(1)} %copy.10.tile_ref, bf16[2,1024]{1,0:T(2,128)(2,1)S(1)} %copy-done.1), custom_call_target="tpu_custom_call" | custom-call | tf_op jit(solution)/shard_map/label/pallas_call | solution.py:329
  27.1 1.0 %collective-permute-done.5.r3_ref = bf16[8,16,128]{2,1,0:T(8,128)(2,1)S(1)} collective-permute-done((bf16[8,16,128]{2,1,0:T(8,128)(2,1)S(1)}, bf16[8,16,128]{2,1,0:T(8,128)(2,1)S(1)}, u32[]{:S(2)}, u32[]{:S(2)}) %collective-permute-start.5) | collective-permute-done | bytes 32800 | tf_op jit(solution)/shard_map/ppermute | solution.py:446
  28.0 1.6 %pack.1 = bf16[64,40,128]{2,1,0:T(8,128)(2,1)} custom-call(bf16[8,16,128]{2,1,0:T(8,128)(2,1)S(1)} %get-tuple-element.29.r0_ref, bf16[8,16,128]{2,1,0:T(8,128)(2,1)S(1)} %collective-permute-done.3.r1_ref, bf16[8,16,128]{2,1,0:T(8,128)(2,1)S(1)} %collective-permute-done.4.r2_ref, bf16[8,16,128]{2,1,0:T(8,128)(2,1)S(1)} %collective-permute-done.5.r3_ref, ...), custom_call_target="tpu_custom_call" | custom-call | tf_op jit(solution)/shard_map/pack/pallas_call | solution.py:356
  29.6 14.0 %all-to-all-start = ((bf16[64,40,128]{2,1,0:T(8,128)(2,1)}), bf16[64,40,128]{2,1,0:T(8,128)(2,1)S(1)}, u32[]{:S(2)}, u32[]{:S(2)}) async-start(bf16[64,40,128]{2,1,0:T(8,128)(2,1)} %pack.1), calls=%async_computation | async-start | bytes 1310720 | tf_op jit(solution)/shard_map/all_to_all | solution.py:461
  43.6 0.8 %collective-permute-start.6 = (bf16[256,128]{1,0:T(8,128)(2,1)S(1)}, bf16[256,128]{1,0:T(8,128)(2,1)S(1)}, u32[]{:S(2)}, u32[]{:S(2)}) collective-permute-start(bf16[256,128]{1,0:T(8,128)(2,1)S(1)} %get-tuple-element.36.r0_ref), channel_id=1, source_target_pairs={{0,64},{64,0},{128,192},{192,128},{1,65},{65,1},{129,193},{193,129... | collective-permute-start | bytes 196616 | tf_op jit(solution)/shard_map/ppermute | solution.py:446
  44.4 1.9 %collective-permute-start.8 = (bf16[256,128]{1,0:T(8,128)(2,1)S(1)}, bf16[256,128]{1,0:T(8,128)(2,1)S(1)}, u32[]{:S(2)}, u32[]{:S(2)}) collective-permute-start(bf16[256,128]{1,0:T(8,128)(2,1)S(1)} %get-tuple-element.36.r0_ref), channel_id=1, source_target_pairs={{0,192},{64,128},{128,64},{192,0},{1,193},{65,129},{129,65},{193,1... | collective-permute-start | bytes 196616 | tf_op jit(solution)/shard_map/ppermute | solution.py:446
  46.3 2.7 %collective-permute-done.7.r2_ref = bf16[256,128]{1,0:T(8,128)(2,1)S(1)} collective-permute-done((bf16[256,128]{1,0:T(8,128)(2,1)S(1)}, bf16[256,128]{1,0:T(8,128)(2,1)S(1)}, u32[]{:S(2)}, u32[]{:S(2)}) %collective-permute-start.7) | collective-permute-done | bytes 65568 | tf_op jit(solution)/shard_map/ppermute | solution.py:446
  49.0 3.4 %collective-permute-done.8.r3_ref = bf16[256,128]{1,0:T(8,128)(2,1)S(1)} collective-permute-done((bf16[256,128]{1,0:T(8,128)(2,1)S(1)}, bf16[256,128]{1,0:T(8,128)(2,1)S(1)}, u32[]{:S(2)}, u32[]{:S(2)}) %collective-permute-start.8) | collective-permute-done | bytes 65568 | tf_op jit(solution)/shard_map/ppermute | solution.py:446
  52.4 0.7 %join.1 = bf16[1024,128]{1,0:T(8,128)(2,1)} custom-call(bf16[256,128]{1,0:T(8,128)(2,1)S(1)} %get-tuple-element.36.r0_ref, bf16[256,128]{1,0:T(8,128)(2,1)S(1)} %collective-permute-done.6.r1_ref, bf16[256,128]{1,0:T(8,128)(2,1)S(1)} %collective-permute-done.7.r2_ref, bf16[256,128]{1,0:T(8,128)(2,1)S(1)} %collective-permute-done.8.r3_ref), custom_call_target="tpu_custom_call" | custom-call | tf_op jit(solution)/shard_map/join/pallas_call | solution.py:373
  53.2 10.2 %all-to-all-done.got_ref = bf16[64,40,128]{2,1,0:T(8,128)(2,1)S(1)} async-done(((bf16[64,40,128]{2,1,0:T(8,128)(2,1)}), bf16[64,40,128]{2,1,0:T(8,128)(2,1)S(1)}, u32[]{:S(2)}, u32[]{:S(2)}) %all-to-all-start) | async-done | bytes 655392 | tf_op jit(solution)/shard_map/all_to_all | solution.py:461
  63.4 2.2 %grid.1 = (f32[2,256,128]{2,1,0:T(8,128)S(1)}, f32[2,256,128]{2,1,0:T(8,128)S(1)}) custom-call(bf16[64,40,128]{2,1,0:T(8,128)(2,1)S(1)} %all-to-all-done.got_ref), custom_call_target="tpu_custom_call" | custom-call | tf_op jit(solution)/shard_map/grid/pallas_call | solution.py:424
  65.6 3.2 %collective-permute-start.9 = (f32[2,256,128]{2,1,0:T(8,128)S(1)}, f32[2,256,128]{2,1,0:T(8,128)S(1)}, u32[]{:S(2)}, u32[]{:S(2)}) collective-permute-start(f32[2,256,128]{2,1,0:T(8,128)S(1)} %get-tuple-element.39), channel_id=1, source_target_pairs={{0,64},{64,0},{128,192},{192,128},{1,65},{65,1},{129,193},{193,129... | collective-permute-start | bytes 786440 | tf_op jit(solution)/shard_map/ppermute | solution.py:446
  68.8 1.2 %collective-permute-done.9 = f32[2,256,128]{2,1,0:T(8,128)S(1)} collective-permute-done((f32[2,256,128]{2,1,0:T(8,128)S(1)}, f32[2,256,128]{2,1,0:T(8,128)S(1)}, u32[]{:S(2)}, u32[]{:S(2)}) %collective-permute-start.9) | collective-permute-done | bytes 262176 | tf_op jit(solution)/shard_map/ppermute | solution.py:446
  70.0 0.7 %add_bitcast_fusion = f32[1,2,256,128]{3,2,1,0:T(8,128)} fusion(f32[2,256,128]{2,1,0:T(8,128)S(1)} %get-tuple-element.38, f32[2,256,128]{2,1,0:T(8,128)S(1)} %collective-permute-done.9), kind=kLoop, calls=%fused_computation | loop fusion | flops 65536 | bytes 786432 | tf_op jit(solution)/shard_map/broadcast_in_dim | solution.py:465
  (16 shorter events, 0.3 us)
Async XLA Ops:
  9.2 11.0 %collective-permute-start.1 = (bf16[3,256,128]{2,1,0:T(8,128)(2,1)S(1)}, bf16[3,256,128]{2,1,0:T(8,128)(2,1)S(1)}, u32[]{:S(2)}, u32[]{:S(2)}) collective-permute-start(bf16[3,256,128]{2,1,0:T(8,128)(2,1)S(1)} %get-tuple-element.26), channel_id=1, source_target_pairs={{0,128},{64,192},{128,0},{192,64},{1,129},{65,193},{129,1},{193,65... | collective-permute-start | bytes 589832 | tf_op jit(solution)/shard_map/ppermute | solution.py:446
  11.3 10.3 %copy-start = (bf16[1024,128]{1,0:T(8,128)(2,1)S(1)}, bf16[1024,128]{1,0:T(8,128)(2,1)}, u32[]{:S(2)}) copy-start(bf16[1024,128]{1,0:T(8,128)(2,1)} %vis_ref.1) | copy-start | bytes 786436
  11.3 10.3 %copy-start.2 = (f32[128]{0:T(128)S(1)}, f32[128]{0:T(128)}, u32[]{:S(2)}) copy-start(f32[128]{0:T(128)} %param.12) | copy-start | bytes 1540
  11.3 14.2 %copy-start.3 = (s32[32,1]{0,1:T(1,128)S(1)}, s32[32,1]{0,1:T(1,128)}, u32[]{:S(2)}) copy-start(s32[32,1]{0,1:T(1,128)} %param.15) | copy-start | bytes 388
  11.3 14.3 %copy-start.1 = (bf16[2,1024]{1,0:T(2,128)(2,1)S(1)}, bf16[2,1024]{1,0:T(2,128)(2,1)}, u32[]{:S(2)}) copy-start(bf16[2,1024]{1,0:T(2,128)(2,1)} %uv_ref.1) | copy-start | bytes 12292
  11.3 10.1 %collective-permute-start.2 = (bf16[3,256,128]{2,1,0:T(8,128)(2,1)S(1)}, bf16[3,256,128]{2,1,0:T(8,128)(2,1)S(1)}, u32[]{:S(2)}, u32[]{:S(2)}) collective-permute-start(bf16[3,256,128]{2,1,0:T(8,128)(2,1)S(1)} %get-tuple-element.27), channel_id=1, source_target_pairs={{0,192},{64,128},{128,64},{192,0},{1,193},{65,129},{129,65},{193,1... | collective-permute-start | bytes 589832 | tf_op jit(solution)/shard_map/ppermute | solution.py:446
  20.0 1.5 %collective-permute-start = (bf16[3,256,128]{2,1,0:T(8,128)(2,1)S(1)}, bf16[3,256,128]{2,1,0:T(8,128)(2,1)S(1)}, u32[]{:S(2)}, u32[]{:S(2)}) collective-permute-start(bf16[3,256,128]{2,1,0:T(8,128)(2,1)S(1)} %get-tuple-element.25), channel_id=1, source_target_pairs={{0,64},{64,0},{128,192},{192,128},{1,65},{65,1},{129,193},{193,129... | collective-permute-start | bytes 589832 | tf_op jit(solution)/shard_map/ppermute | solution.py:446
  23.3 3.8 %collective-permute-start.3 = (bf16[8,16,128]{2,1,0:T(8,128)(2,1)S(1)}, bf16[8,16,128]{2,1,0:T(8,128)(2,1)S(1)}, u32[]{:S(2)}, u32[]{:S(2)}) collective-permute-start(bf16[8,16,128]{2,1,0:T(8,128)(2,1)S(1)} %get-tuple-element.30), channel_id=1, source_target_pairs={{0,64},{64,0},{128,192},{192,128},{1,65},{65,1},{129,193},{193,129... | collective-permute-start | bytes 98312 | tf_op jit(solution)/shard_map/ppermute | solution.py:446
  23.5 3.6 %collective-permute-start.4 = (bf16[8,16,128]{2,1,0:T(8,128)(2,1)S(1)}, bf16[8,16,128]{2,1,0:T(8,128)(2,1)S(1)}, u32[]{:S(2)}, u32[]{:S(2)}) collective-permute-start(bf16[8,16,128]{2,1,0:T(8,128)(2,1)S(1)} %get-tuple-element.31), channel_id=1, source_target_pairs={{0,128},{64,192},{128,0},{192,64},{1,129},{65,193},{129,1},{193,65... | collective-permute-start | bytes 98312 | tf_op jit(solution)/shard_map/ppermute | solution.py:446
  24.0 4.0 %collective-permute-start.5 = (bf16[8,16,128]{2,1,0:T(8,128)(2,1)S(1)}, bf16[8,16,128]{2,1,0:T(8,128)(2,1)S(1)}, u32[]{:S(2)}, u32[]{:S(2)}) collective-permute-start(bf16[8,16,128]{2,1,0:T(8,128)(2,1)S(1)} %get-tuple-element.32), channel_id=1, source_target_pairs={{0,192},{64,128},{128,64},{192,0},{1,193},{65,129},{129,65},{193,1... | collective-permute-start | bytes 98312 | tf_op jit(solution)/shard_map/ppermute | solution.py:446
  29.6 33.8 %all-to-all-start = ((bf16[64,40,128]{2,1,0:T(8,128)(2,1)}), bf16[64,40,128]{2,1,0:T(8,128)(2,1)S(1)}, u32[]{:S(2)}, u32[]{:S(2)}) async-start(bf16[64,40,128]{2,1,0:T(8,128)(2,1)} %pack.1), calls=%async_computation | async-start | bytes 1310720 | tf_op jit(solution)/shard_map/all_to_all | solution.py:461
  43.6 2.7 %collective-permute-start.6 = (bf16[256,128]{1,0:T(8,128)(2,1)S(1)}, bf16[256,128]{1,0:T(8,128)(2,1)S(1)}, u32[]{:S(2)}, u32[]{:S(2)}) collective-permute-start(bf16[256,128]{1,0:T(8,128)(2,1)S(1)} %get-tuple-element.36.r0_ref), channel_id=1, source_target_pairs={{0,64},{64,0},{128,192},{192,128},{1,65},{65,1},{129,193},{193,129... | collective-permute-start | bytes 196616 | tf_op jit(solution)/shard_map/ppermute | solution.py:446
  44.4 4.7 %collective-permute-start.7 = (bf16[256,128]{1,0:T(8,128)(2,1)S(1)}, bf16[256,128]{1,0:T(8,128)(2,1)S(1)}, u32[]{:S(2)}, u32[]{:S(2)}) collective-permute-start(bf16[256,128]{1,0:T(8,128)(2,1)S(1)} %get-tuple-element.36.r0_ref), channel_id=1, source_target_pairs={{0,128},{64,192},{128,0},{192,64},{1,129},{65,193},{129,1},{193,65... | collective-permute-start | bytes 196616 | tf_op jit(solution)/shard_map/ppermute | solution.py:446
  44.4 8.1 %collective-permute-start.8 = (bf16[256,128]{1,0:T(8,128)(2,1)S(1)}, bf16[256,128]{1,0:T(8,128)(2,1)S(1)}, u32[]{:S(2)}, u32[]{:S(2)}) collective-permute-start(bf16[256,128]{1,0:T(8,128)(2,1)S(1)} %get-tuple-element.36.r0_ref), channel_id=1, source_target_pairs={{0,192},{64,128},{128,64},{192,0},{1,193},{65,129},{129,65},{193,1... | collective-permute-start | bytes 196616 | tf_op jit(solution)/shard_map/ppermute | solution.py:446
  65.6 4.3 %collective-permute-start.9 = (f32[2,256,128]{2,1,0:T(8,128)S(1)}, f32[2,256,128]{2,1,0:T(8,128)S(1)}, u32[]{:S(2)}, u32[]{:S(2)}) collective-permute-start(f32[2,256,128]{2,1,0:T(8,128)S(1)} %get-tuple-element.39), channel_id=1, source_target_pairs={{0,64},{64,0},{128,192},{192,128},{1,65},{65,1},{129,193},{193,129... | collective-permute-start | bytes 786440 | tf_op jit(solution)/shard_map/ppermute | solution.py:446

commit v8 on v6

--- a/solution.py
+++ b/solution.py
@@ -378,17 +378,18 @@
     )(*rows)
 
 
-def grid_kernel(got_ref, keep_ref, give_ref, tab_ref, acc_ref):
-    chip = own_place()[0] // 2
-    half = own_place()[1]
+def grid_kernel(flip, got_ref, out_ref, tab_ref, acc_ref):
+    me, half, _ = own_place()
+    chip = me // 2
     tiles = N_TB * SLOTS * PART // 128
     groups = N_TB // tiles
     coords = got_ref[:, SLOTS * PART :, :].astype(F32).reshape(tiles, groups, 8, COLS)
     coords = jnp.sum(coords, axis=1)
     y_pixel = (lax.broadcasted_iota(jnp.int32, (GRID, 1), 0) - GRID // 2).astype(F32)
-    order = lax.broadcasted_iota(jnp.int32, (16, 1), 0)
-    x_pixel = (16 * chip + 8 * ((order // 8) ^ half) + order % 8 - GRID // 2).astype(F32)
+    order = lax.broadcasted_iota(jnp.int32, (8, 1), 0)
+    x_pixel = (16 * chip + 8 * (half ^ flip) + order - GRID // 2).astype(F32)
     scale = 1.0 / (2.0 * GRID)
+    share = PIX // N_DIR
     step = 256
     per_step = step // 128
 
@@ -403,10 +404,10 @@
         cx, sx = cos_sin_turns(x_pixel * u)
         cy, sy = cos_sin_turns(y_pixel * v)
         n, lanes = tile // per_step, slice(tile % per_step * 128, (tile % per_step + 1) * 128)
-        for x in range(16):
+        for x in range(8):
             a, b = cx[x : x + 1], sx[x : x + 1]
             tab_ref[n, x * GRID : (x + 1) * GRID, lanes] = (a * cy - b * sy).astype(BF16)
-            tab_ref[n, 512 + x * GRID : 512 + (x + 1) * GRID, lanes] = (b * cy + a * sy).astype(BF16)
+            tab_ref[n, share + x * GRID : share + (x + 1) * GRID, lanes] = (b * cy + a * sy).astype(BF16)
         if tile % per_step == per_step - 1:
             if n == 0:
                 acc_ref[...] = product(n)
@@ -414,23 +415,23 @@
                 acc_ref[...] += product(n)
     total = acc_ref[...] * float(ROWS_DEV) ** (-0.5)
     for part in range(2):
-        keep_ref[part] = total[part * 512 : part * 512 + 256]
-        give_ref[part] = total[part * 512 + 256 : part * 512 + 512]
-
-
-def grid_rows(got):
-    return pl.pallas_call(
-        grid_kernel,
-        out_shape=(
-            jax.ShapeDtypeStruct((2, PIX // N_DIR, COLS), F32),
-            jax.ShapeDtypeStruct((2, PIX // N_DIR, COLS), F32),
-        ),
+        out_ref[part] = total[part * share : (part + 1) * share]
+
+
+def grid_rows(flip, got):
+    def kernel(*refs):
+        grid_kernel(flip, *refs)
+
+    return pl.pallas_call(
+        kernel,
+        out_shape=jax.ShapeDtypeStruct((2, PIX // N_DIR, COLS), F32),
         in_specs=[vmem()],
-        out_specs=(vmem(), vmem()),
+        out_specs=vmem(),
         scratch_shapes=[
-            pltpu.VMEM((N_TB * SLOTS * PART // 256, 1024, 256), BF16),
-            pltpu.VMEM((1024, COLS), F32),
+            pltpu.VMEM((N_TB * SLOTS * PART // 256, 512, 256), BF16),
+            pltpu.VMEM((512, COLS), F32),
         ],
+        cost_estimate=pl.CostEstimate(flops=2 * 10**9, transcendentals=0, bytes_accessed=10**6),
         compiler_params=params(24),
         name="grid",
     )(got)
@@ -460,8 +461,10 @@
     got = lax.all_to_all(send, "tb", split_axis=0, concat_axis=0, tiled=True)
     late = after(rows, send)
     residual = join([late] + [swap(late, x) for x in range(1, N_DIR)])
-    keep, give = grid_rows(after(got, residual))
-    return residual, (keep + swap(give, 1))[None]
+    got = after(got, residual)
+    moved = swap(grid_rows(1, got), 1)
+    keep = grid_rows(0, got)
+    return residual, (keep + moved)[None]
 
 
 def solution(mesh):

time: 70.9 us -> 70 us (0.987)
  waiting for transfers between devices: 20.2 us -> 19.1 us
    ppermute x10, waiting for transfers between devices: 9.74 us -> 8.58 us  [swap(): return lax.ppermute(value, 'dir', [(i, i ^ flip) for i in range(N_DIR)])]
    pallas_call x1 -> x2, Pallas kernels: 2.23 us -> 2.54 us  [grid_rows(): pl.pallas_call(kernel, out_shape=jax.ShapeDtypeStruct((2, PIX // N_DIR, C...]
  transfers between devices with their start and end apart: 11 -> 11, of which waited for: 6 -> 5; matrix products, arithmetic and copies ran while one was open for 0% -> 0% of each run, Pallas kernels for 11% -> 13%
where the time goes in v8:
time: 70 us; the launch traced here: 69.8 us
  starting transfers between devices  27 us (39%)
  Pallas kernels  22.1 us (32%)
  waiting for transfers between devices  19.1 us (27%)
  between operations  0.77 us (1%)
  other arithmetic  0.73 us (1%)
    all_to_all x1, starting transfers between devices, local(): got = lax.all_to_all(send, 'tb', split_axis=0, concat_axis=0, tiled=True)  13.9 us
    ppermute x10, starting transfers between devices, swap(): return lax.ppermute(value, 'dir', [(i, i ^ flip) for i in range(N_DIR)])  13 us
    pallas_call x2, Pallas kernels, predict(): pl.pallas_call(kernel, out_shape=tuple((jax.ShapeDtypeStruct((DIR_DEV, QR...  11.2 us
    all_to_all x1, waiting for transfers between devices, local(): got = lax.all_to_all(send, 'tb', split_axis=0, concat_axis=0, tiled=True)  10.5 us
    ppermute x10, waiting for transfers between devices, swap(): return lax.ppermute(value, 'dir', [(i, i ^ flip) for i in range(N_DIR)])  8.58 us
    pallas_call x1, Pallas kernels, prepare(): pl.pallas_call(prepare_kernel, out_shape=(jax.ShapeDtypeStruct((8, POOL),...  2.89 us
    pallas_call x2, Pallas kernels, grid_rows(): pl.pallas_call(kernel, out_shape=jax.ShapeDtypeStruct((2, PIX // N_DIR, C...  2.54 us
    pallas_call x1, Pallas kernels, peel(): pl.pallas_call(peel_kernel, out_shape=(jax.ShapeDtypeStruct((QROWS, COLS)...  1.71 us
  transfers between devices with their start and end apart: 11, of which 5 were waited for; matrix products, arithmetic and copies ran while one was open for 0% of the time, Pallas kernels for 13%

profile of v8, /device:TPU:1, one launch (start us, length us, event | category | flops | bytes accessed | tf_op | source)
XLA Modules:
  0.0 69.8 jit_solution(15333975239016009645)
XLA Ops:
  0.6 2.9 %prepare.1 = (bf16[8,3072]{1,0:T(8,128)(2,1)S(1)}, bf16[4,8,256]{2,1,0:T(8,128)(2,1)S(1)}, bf16[12,512,384]{2,1,0:T(8,128)(2,1)S(1)}) custom-call(s32[3]{0:T(128)} %order_hbm.1, s32[1,3072]{1,0:T(1,128)} %bitcast.8, f32[2,3072]{1,0:T(2,128)} %lm_hbm.1, bf16[2,1024]{1,0:T(2,128)(2,1)} %uv_ref.1, bf16[2,3072,128]{2,1,0:T(8,128)(2,1)} %spec_hbm.1), custom_call_target="tpu_custom_call" | custom-call | tf_op jit(solution)/shard_map/prepare/pallas_call | solution.py:123
  3.5 5.6 %predict.3 = (bf16[3,256,128]{2,1,0:T(8,128)(2,1)S(1)}, bf16[3,256,128]{2,1,0:T(8,128)(2,1)S(1)}) custom-call(bf16[4,8,256]{2,1,0:T(8,128)(2,1)S(1)} %get-tuple-element.20.refs_0_, bf16[8,3072]{1,0:T(8,128)(2,1)S(1)} %get-tuple-element.21.refs_1_, bf16[12,512,384]{2,1,0:T(8,128)(2,1)S(1)} %get-tuple-element.22.refs_2_), custom_call_target="tpu_custom_call" | custom-call | flops 4831838208 | bytes 5111808 | tf_op jit(solution)/shard_map/predict/pallas_call | solution.py:183
  9.1 2.1 %collective-permute-start.1 = (bf16[3,256,128]{2,1,0:T(8,128)(2,1)S(1)}, bf16[3,256,128]{2,1,0:T(8,128)(2,1)S(1)}, u32[]{:S(2)}, u32[]{:S(2)}) collective-permute-start(bf16[3,256,128]{2,1,0:T(8,128)(2,1)S(1)} %get-tuple-element.28), channel_id=1, source_target_pairs={{0,128},{64,192},{128,0},{192,64},{1,129},{65,193},{129,1},{193,65... | collective-permute-start | bytes 589832 | tf_op jit(solution)/shard_map/ppermute | solution.py:445
  11.3 3.1 %collective-permute-start.2 = (bf16[3,256,128]{2,1,0:T(8,128)(2,1)S(1)}, bf16[3,256,128]{2,1,0:T(8,128)(2,1)S(1)}, u32[]{:S(2)}, u32[]{:S(2)}) collective-permute-start(bf16[3,256,128]{2,1,0:T(8,128)(2,1)S(1)} %get-tuple-element.29), channel_id=1, source_target_pairs={{0,192},{64,128},{128,64},{192,0},{1,193},{65,129},{129,65},{193,1... | collective-permute-start | bytes 589832 | tf_op jit(solution)/shard_map/ppermute | solution.py:445
  14.4 5.6 %predict.2 = (bf16[3,256,128]{2,1,0:T(8,128)(2,1)S(1)}, bf16[3,256,128]{2,1,0:T(8,128)(2,1)S(1)}) custom-call(bf16[4,8,256]{2,1,0:T(8,128)(2,1)S(1)} %get-tuple-element.20.refs_0_, bf16[8,3072]{1,0:T(8,128)(2,1)S(1)} %get-tuple-element.21.refs_1_, bf16[12,512,384]{2,1,0:T(8,128)(2,1)S(1)} %get-tuple-element.22.refs_2_), custom_call_target="tpu_custom_call" | custom-call | flops 4831838208 | bytes 5111808 | tf_op jit(solution)/shard_map/predict/pallas_call | solution.py:183
  20.2 1.6 %label.1 = (bf16[64,40,128]{2,1,0:T(8,128)(2,1)S(1)}, s32[32]{0:T(128)S(1)}) custom-call(s32[32]{0:T(128)S(1)} %bitcast.5, s32[32,1]{1,0:T(8,128)S(1)} %copy.10.tile_ref, bf16[2,1024]{1,0:T(2,128)(2,1)S(1)} %copy-done.1), custom_call_target="tpu_custom_call" | custom-call | tf_op jit(solution)/shard_map/label/pallas_call | solution.py:328
  21.8 1.7 %peel.1 = (bf16[256,128]{1,0:T(8,128)(2,1)S(1)}, bf16[8,16,128]{2,1,0:T(8,128)(2,1)S(1)}, bf16[8,16,128]{2,1,0:T(8,128)(2,1)S(1)}, bf16[8,16,128]{2,1,0:T(8,128)(2,1)S(1)}, bf16[8,16,128]{2,1,0:T(8,128)(2,1)S(1)}) custom-call(bf16[1024,128]{1,0:T(8,128)(2,1)S(1)} %copy-done, f32[1,128]{1,0:T(1,128)S(1)} %bitcast.7, ...), custom_call_target="tpu_custom_call" | custom-call | tf_op jit(solution)/shard_map/peel/pallas_call | solution.py:272
  23.5 0.6 collective-permute-start.3
  24.1 1.7 %collective-permute-start.5 = (bf16[8,16,128]{2,1,0:T(8,128)(2,1)S(1)}, bf16[8,16,128]{2,1,0:T(8,128)(2,1)S(1)}, u32[]{:S(2)}, u32[]{:S(2)}) collective-permute-start(bf16[8,16,128]{2,1,0:T(8,128)(2,1)S(1)} %get-tuple-element.34), channel_id=1, source_target_pairs={{0,192},{64,128},{128,64},{192,0},{1,193},{65,129},{129,65},{193,1... | collective-permute-start | bytes 98312 | tf_op jit(solution)/shard_map/ppermute | solution.py:445
  25.8 1.0 %collective-permute-done.4.r2_ref = bf16[8,16,128]{2,1,0:T(8,128)(2,1)S(1)} collective-permute-done((bf16[8,16,128]{2,1,0:T(8,128)(2,1)S(1)}, bf16[8,16,128]{2,1,0:T(8,128)(2,1)S(1)}, u32[]{:S(2)}, u32[]{:S(2)}) %collective-permute-start.4) | collective-permute-done | bytes 32800 | tf_op jit(solution)/shard_map/ppermute | solution.py:445
  26.9 1.2 %collective-permute-done.5.r3_ref = bf16[8,16,128]{2,1,0:T(8,128)(2,1)S(1)} collective-permute-done((bf16[8,16,128]{2,1,0:T(8,128)(2,1)S(1)}, bf16[8,16,128]{2,1,0:T(8,128)(2,1)S(1)}, u32[]{:S(2)}, u32[]{:S(2)}) %collective-permute-start.5) | collective-permute-done | bytes 32800 | tf_op jit(solution)/shard_map/ppermute | solution.py:445
  28.1 1.5 %pack.1 = bf16[64,40,128]{2,1,0:T(8,128)(2,1)} custom-call(s32[32]{0:T(128)S(1)} %bitcast.6, s32[32]{0:T(128)S(1)} %get-tuple-element.25.slot_ref, bf16[8,16,128]{2,1,0:T(8,128)(2,1)S(1)} %get-tuple-element.31.r0_ref, bf16[8,16,128]{2,1,0:T(8,128)(2,1)S(1)} %collective-permute-done.3.r1_ref, bf16[8,16,128]{2,1,0:T(8,128)(2,1)S(1)} %collective-permute-done.4.r2_ref, ...), custom_call_target="tpu_custom_call" | custom-call | tf_op jit(solution)/shard_map/pack/pallas_call | solution.py:353
  29.6 13.9 %all-to-all-start = ((bf16[64,40,128]{2,1,0:T(8,128)(2,1)}), bf16[64,40,128]{2,1,0:T(8,128)(2,1)S(1)}, u32[]{:S(2)}, u32[]{:S(2)}) async-start(bf16[64,40,128]{2,1,0:T(8,128)(2,1)} %pack.1), calls=%async_computation | async-start | bytes 1310720 | tf_op jit(solution)/shard_map/all_to_all | solution.py:461
  43.5 0.6 collective-permute-start.8
  44.1 1.5 %collective-permute-start.7 = (bf16[256,128]{1,0:T(8,128)(2,1)S(1)}, bf16[256,128]{1,0:T(8,128)(2,1)S(1)}, u32[]{:S(2)}, u32[]{:S(2)}) collective-permute-start(bf16[256,128]{1,0:T(8,128)(2,1)S(1)} %get-tuple-element.36.r0_ref), channel_id=1, source_target_pairs={{0,128},{64,192},{128,0},{192,64},{1,129},{65,193},{129,1},{193,65... | collective-permute-start | bytes 196616 | tf_op jit(solution)/shard_map/ppermute | solution.py:445
  45.6 0.1 collective-permute-start.6
  45.7 3.7 %collective-permute-done.8.r3_ref = bf16[256,128]{1,0:T(8,128)(2,1)S(1)} collective-permute-done((bf16[256,128]{1,0:T(8,128)(2,1)S(1)}, bf16[256,128]{1,0:T(8,128)(2,1)S(1)}, u32[]{:S(2)}, u32[]{:S(2)}) %collective-permute-start.8) | collective-permute-done | bytes 65568 | tf_op jit(solution)/shard_map/ppermute | solution.py:445
  49.4 2.7 %collective-permute-done.7.r2_ref = bf16[256,128]{1,0:T(8,128)(2,1)S(1)} collective-permute-done((bf16[256,128]{1,0:T(8,128)(2,1)S(1)}, bf16[256,128]{1,0:T(8,128)(2,1)S(1)}, u32[]{:S(2)}, u32[]{:S(2)}) %collective-permute-start.7) | collective-permute-done | bytes 65568 | tf_op jit(solution)/shard_map/ppermute | solution.py:445
  52.1 0.7 %join.1 = bf16[1024,128]{1,0:T(8,128)(2,1)} custom-call(bf16[256,128]{1,0:T(8,128)(2,1)S(1)} %get-tuple-element.36.r0_ref, bf16[256,128]{1,0:T(8,128)(2,1)S(1)} %collective-permute-done.6.r1_ref, bf16[256,128]{1,0:T(8,128)(2,1)S(1)} %collective-permute-done.7.r2_ref, bf16[256,128]{1,0:T(8,128)(2,1)S(1)} %collective-permute-done.8.r3_ref), custom_call_target="tpu_custom_call" | custom-call | tf_op jit(solution)/shard_map/join/pallas_call | solution.py:371
  52.8 10.5 %all-to-all-done.refs_0_ = bf16[64,40,128]{2,1,0:T(8,128)(2,1)S(1)} async-done(((bf16[64,40,128]{2,1,0:T(8,128)(2,1)}), bf16[64,40,128]{2,1,0:T(8,128)(2,1)S(1)}, u32[]{:S(2)}, u32[]{:S(2)}) %all-to-all-start) | async-done | bytes 655392 | tf_op jit(solution)/shard_map/all_to_all | solution.py:461
  63.3 1.3 %grid.3 = f32[2,256,128]{2,1,0:T(8,128)S(1)} custom-call(bf16[64,40,128]{2,1,0:T(8,128)(2,1)S(1)} %all-to-all-done.refs_0_), custom_call_target="tpu_custom_call" | custom-call | flops 2000000000 | bytes 1000000 | tf_op jit(solution)/shard_map/grid/pallas_call | solution.py:425
  64.6 3.2 %collective-permute-start.9 = (f32[2,256,128]{2,1,0:T(8,128)S(1)}, f32[2,256,128]{2,1,0:T(8,128)S(1)}, u32[]{:S(2)}, u32[]{:S(2)}) collective-permute-start(f32[2,256,128]{2,1,0:T(8,128)S(1)} %grid.3), channel_id=1, source_target_pairs={{0,64},{64,0},{128,192},{192,128},{1,65},{65,1},{129,193},{193,129... | collective-permute-start | bytes 786440 | tf_op jit(solution)/shard_map/ppermute | solution.py:445
  67.7 1.3 %grid.2 = f32[2,256,128]{2,1,0:T(8,128)S(1)} custom-call(bf16[64,40,128]{2,1,0:T(8,128)(2,1)S(1)} %all-to-all-done.refs_0_), custom_call_target="tpu_custom_call" | custom-call | flops 2000000000 | bytes 1000000 | tf_op jit(solution)/shard_map/grid/pallas_call | solution.py:425
  69.0 0.7 %add_bitcast_fusion = f32[1,2,256,128]{3,2,1,0:T(8,128)} fusion(f32[2,256,128]{2,1,0:T(8,128)S(1)} %grid.2, f32[2,256,128]{2,1,0:T(8,128)S(1)} %collective-permute-done.9), kind=kLoop, calls=%fused_computation | loop fusion | flops 65536 | bytes 786432 | tf_op jit(solution)/shard_map/broadcast_in_dim | solution.py:467
  (17 shorter events, 0.2 us)
Async XLA Ops:
  9.1 12.6 %collective-permute-start.1 = (bf16[3,256,128]{2,1,0:T(8,128)(2,1)S(1)}, bf16[3,256,128]{2,1,0:T(8,128)(2,1)S(1)}, u32[]{:S(2)}, u32[]{:S(2)}) collective-permute-start(bf16[3,256,128]{2,1,0:T(8,128)(2,1)S(1)} %get-tuple-element.28), channel_id=1, source_target_pairs={{0,128},{64,192},{128,0},{192,64},{1,129},{65,193},{129,1},{193,65... | collective-permute-start | bytes 589832 | tf_op jit(solution)/shard_map/ppermute | solution.py:445
  11.3 8.8 %copy-start.2 = (s32[32,1]{0,1:T(1,128)S(1)}, s32[32,1]{0,1:T(1,128)}, u32[]{:S(2)}) copy-start(s32[32,1]{0,1:T(1,128)} %param.15) | copy-start | bytes 388
  11.3 8.9 %copy-start.1 = (bf16[2,1024]{1,0:T(2,128)(2,1)S(1)}, bf16[2,1024]{1,0:T(2,128)(2,1)}, u32[]{:S(2)}) copy-start(bf16[2,1024]{1,0:T(2,128)(2,1)} %uv_ref.1) | copy-start | bytes 12292
  11.3 10.5 %copy-start = (bf16[1024,128]{1,0:T(8,128)(2,1)S(1)}, bf16[1024,128]{1,0:T(8,128)(2,1)}, u32[]{:S(2)}) copy-start(bf16[1024,128]{1,0:T(8,128)(2,1)} %vis_ref) | copy-start | bytes 786436
  11.3 10.5 %copy-start.3 = (f32[128]{0:T(128)S(1)}, f32[128]{0:T(128)}, u32[]{:S(2)}) copy-start(f32[128]{0:T(128)} %param.12) | copy-start | bytes 1540
  11.3 10.5 %collective-permute-start.2 = (bf16[3,256,128]{2,1,0:T(8,128)(2,1)S(1)}, bf16[3,256,128]{2,1,0:T(8,128)(2,1)S(1)}, u32[]{:S(2)}, u32[]{:S(2)}) collective-permute-start(bf16[3,256,128]{2,1,0:T(8,128)(2,1)S(1)} %get-tuple-element.29), channel_id=1, source_target_pairs={{0,192},{64,128},{128,64},{192,0},{1,193},{65,129},{129,65},{193,1... | collective-permute-start | bytes 589832 | tf_op jit(solution)/shard_map/ppermute | solution.py:445
  20.0 1.8 %collective-permute-start = (bf16[3,256,128]{2,1,0:T(8,128)(2,1)S(1)}, bf16[3,256,128]{2,1,0:T(8,128)(2,1)S(1)}, u32[]{:S(2)}, u32[]{:S(2)}) collective-permute-start(bf16[3,256,128]{2,1,0:T(8,128)(2,1)S(1)} %get-tuple-element.27), channel_id=1, source_target_pairs={{0,64},{64,0},{128,192},{192,128},{1,65},{65,1},{129,193},{193,129... | collective-permute-start | bytes 589832 | tf_op jit(solution)/shard_map/ppermute | solution.py:445
  23.5 2.3 %collective-permute-start.3 = (bf16[8,16,128]{2,1,0:T(8,128)(2,1)S(1)}, bf16[8,16,128]{2,1,0:T(8,128)(2,1)S(1)}, u32[]{:S(2)}, u32[]{:S(2)}) collective-permute-start(bf16[8,16,128]{2,1,0:T(8,128)(2,1)S(1)} %get-tuple-element.32), channel_id=1, source_target_pairs={{0,64},{64,0},{128,192},{192,128},{1,65},{65,1},{129,193},{193,129... | collective-permute-start | bytes 98312 | tf_op jit(solution)/shard_map/ppermute | solution.py:445
  24.1 2.8 %collective-permute-start.4 = (bf16[8,16,128]{2,1,0:T(8,128)(2,1)S(1)}, bf16[8,16,128]{2,1,0:T(8,128)(2,1)S(1)}, u32[]{:S(2)}, u32[]{:S(2)}) collective-permute-start(bf16[8,16,128]{2,1,0:T(8,128)(2,1)S(1)} %get-tuple-element.33), channel_id=1, source_target_pairs={{0,128},{64,192},{128,0},{192,64},{1,129},{65,193},{129,1},{193,65... | collective-permute-start | bytes 98312 | tf_op jit(solution)/shard_map/ppermute | solution.py:445
  24.1 4.0 %collective-permute-start.5 = (bf16[8,16,128]{2,1,0:T(8,128)(2,1)S(1)}, bf16[8,16,128]{2,1,0:T(8,128)(2,1)S(1)}, u32[]{:S(2)}, u32[]{:S(2)}) collective-permute-start(bf16[8,16,128]{2,1,0:T(8,128)(2,1)S(1)} %get-tuple-element.34), channel_id=1, source_target_pairs={{0,192},{64,128},{128,64},{192,0},{1,193},{65,129},{129,65},{193,1... | collective-permute-start | bytes 98312 | tf_op jit(solution)/shard_map/ppermute | solution.py:445
  29.6 33.7 %all-to-all-start = ((bf16[64,40,128]{2,1,0:T(8,128)(2,1)}), bf16[64,40,128]{2,1,0:T(8,128)(2,1)S(1)}, u32[]{:S(2)}, u32[]{:S(2)}) async-start(bf16[64,40,128]{2,1,0:T(8,128)(2,1)} %pack.1), calls=%async_computation | async-start | bytes 1310720 | tf_op jit(solution)/shard_map/all_to_all | solution.py:461
  43.5 5.9 %collective-permute-start.8 = (bf16[256,128]{1,0:T(8,128)(2,1)S(1)}, bf16[256,128]{1,0:T(8,128)(2,1)S(1)}, u32[]{:S(2)}, u32[]{:S(2)}) collective-permute-start(bf16[256,128]{1,0:T(8,128)(2,1)S(1)} %get-tuple-element.36.r0_ref), channel_id=1, source_target_pairs={{0,192},{64,128},{128,64},{192,0},{1,193},{65,129},{129,65},{193,1... | collective-permute-start | bytes 196616 | tf_op jit(solution)/shard_map/ppermute | solution.py:445
  44.1 8.0 %collective-permute-start.7 = (bf16[256,128]{1,0:T(8,128)(2,1)S(1)}, bf16[256,128]{1,0:T(8,128)(2,1)S(1)}, u32[]{:S(2)}, u32[]{:S(2)}) collective-permute-start(bf16[256,128]{1,0:T(8,128)(2,1)S(1)} %get-tuple-element.36.r0_ref), channel_id=1, source_target_pairs={{0,128},{64,192},{128,0},{192,64},{1,129},{65,193},{129,1},{193,65... | collective-permute-start | bytes 196616 | tf_op jit(solution)/shard_map/ppermute | solution.py:445
  45.6 6.5 %collective-permute-start.6 = (bf16[256,128]{1,0:T(8,128)(2,1)S(1)}, bf16[256,128]{1,0:T(8,128)(2,1)S(1)}, u32[]{:S(2)}, u32[]{:S(2)}) collective-permute-start(bf16[256,128]{1,0:T(8,128)(2,1)S(1)} %get-tuple-element.36.r0_ref), channel_id=1, source_target_pairs={{0,64},{64,0},{128,192},{192,128},{1,65},{65,1},{129,193},{193,129... | collective-permute-start | bytes 196616 | tf_op jit(solution)/shard_map/ppermute | solution.py:445
  64.6 4.5 %collective-permute-start.9 = (f32[2,256,128]{2,1,0:T(8,128)S(1)}, f32[2,256,128]{2,1,0:T(8,128)S(1)}, u32[]{:S(2)}, u32[]{:S(2)}) collective-permute-start(f32[2,256,128]{2,1,0:T(8,128)S(1)} %grid.3), channel_id=1, source_target_pairs={{0,64},{64,0},{128,192},{192,128},{1,65},{65,1},{129,193},{193,129... | collective-permute-start | bytes 786440 | tf_op jit(solution)/shard_map/ppermute | solution.py:445

commit v9 on v8

--- a/solution.py
+++ b/solution.py
@@ -82,7 +82,24 @@
     copies = [pltpu.make_async_copy(src, dst, sems.at[n]) for n, (src, dst) in enumerate(pairs)]
     for copy in copies:
         copy.start()
-    for copy in copies[:4]:
+    column = lax.broadcasted_iota(jnp.int32, (32, POOL), 1) // 128
+    pick = (column == lax.broadcasted_iota(jnp.int32, (32, POOL), 0)).astype(F32).astype(BF16)
+    for copy in copies[:2]:
+        copy.wait()
+    assign = assign_ref[...]
+    low = assign & 127
+    high = assign >> 7
+    pos = jnp.zeros((128, 32), F32)
+    for d in range(DIR_DEV):
+        place = jnp.where(order_ref[1] == d, 1.0, jnp.where(order_ref[2] == d, 2.0, 0.0))
+        lanes = slice(d * NCOMP, (d + 1) * NCOMP)
+        low_hot = (lax.broadcasted_iota(jnp.int32, (128, NCOMP), 0) == low[:, lanes]).astype(F32).astype(BF16)
+        high_hot = (lax.broadcasted_iota(jnp.int32, (32, NCOMP), 0) == high[:, lanes]).astype(F32).astype(BF16)
+        pos = pos + place * lax.dot_general(
+            low_hot, high_hot, (((1,), (1,)), ((), ())), preferred_element_type=F32
+        )
+    pos_ref[...] = jnp.dot(pos.astype(BF16), pick, preferred_element_type=F32)
+    for copy in copies[2:4]:
         copy.wait()
     lh, lmid, ll = three_parts(lm_ref[...])
     zero = jnp.zeros((2, POOL), BF16)
@@ -93,19 +110,6 @@
         u = uv_ref[0:1, q * QROWS : (q + 1) * QROWS]
         v = uv_ref[1:2, q * QROWS : (q + 1) * QROWS]
         uv8_ref[q] = jnp.concatenate([u, u, u, v, v, v, jnp.zeros((2, QROWS), BF16)], axis=0)
-    assign = assign_ref[...]
-    low = assign & 127
-    high = assign >> 7
-    segment = lax.broadcasted_iota(jnp.int32, (1, POOL), 1) // NCOMP
-    place = jnp.zeros((1, POOL), F32)
-    for p in range(DIR_DEV):
-        place = jnp.where(segment == order_ref[p], float(p), place)
-    low_hot = (lax.broadcasted_iota(jnp.int32, (128, POOL), 0) == low).astype(F32).astype(BF16)
-    high_hot = jnp.where(lax.broadcasted_iota(jnp.int32, (32, POOL), 0) == high, place, 0.0).astype(BF16)
-    pos = lax.dot_general(low_hot, high_hot, (((1,), (1,)), ((), ())), preferred_element_type=F32)
-    column = lax.broadcasted_iota(jnp.int32, (32, POOL), 1) // 128
-    pick = (column == lax.broadcasted_iota(jnp.int32, (32, POOL), 0)).astype(F32).astype(BF16)
-    pos_ref[...] = jnp.dot(pos.astype(BF16), pick, preferred_element_type=F32)
     for column in range(POOL // 128):
         if column % (POOL // 128 // PIECES) == 0:
             copies[4 + column // (POOL // 128 // PIECES)].wait()

time: 70 us -> 69.8 us (level)
  no operation moved by 1% of the time
where the time goes in v9:
time: 69.8 us; the launch traced here: 69.6 us
  starting transfers between devices  27 us (39%)
  Pallas kernels  21.9 us (31%)
  waiting for transfers between devices  19.1 us (27%)
  between operations  0.77 us (1%)
  other arithmetic  0.73 us (1%)
    all_to_all x1, starting transfers between devices, local(): got = lax.all_to_all(send, 'tb', split_axis=0, concat_axis=0, tiled=True)  13.9 us
    ppermute x10, starting transfers between devices, swap(): return lax.ppermute(value, 'dir', [(i, i ^ flip) for i in range(N_DIR)])  13 us
    pallas_call x2, Pallas kernels, predict(): pl.pallas_call(kernel, out_shape=tuple((jax.ShapeDtypeStruct((DIR_DEV, QR...  11.2 us
    all_to_all x1, waiting for transfers between devices, local(): got = lax.all_to_all(send, 'tb', split_axis=0, concat_axis=0, tiled=True)  10.5 us
    ppermute x10, waiting for transfers between devices, swap(): return lax.ppermute(value, 'dir', [(i, i ^ flip) for i in range(N_DIR)])  8.6 us
    pallas_call x1, Pallas kernels, prepare(): pl.pallas_call(prepare_kernel, out_shape=(jax.ShapeDtypeStruct((8, POOL),...  2.67 us
    pallas_call x2, Pallas kernels, grid_rows(): pl.pallas_call(kernel, out_shape=jax.ShapeDtypeStruct((2, PIX // N_DIR, C...  2.54 us
    pallas_call x1, Pallas kernels, peel(): pl.pallas_call(peel_kernel, out_shape=(jax.ShapeDtypeStruct((QROWS, COLS)...  1.71 us
  transfers between devices with their start and end apart: 11, of which 5 were waited for; matrix products, arithmetic and copies ran while one was open for 0% of the time, Pallas kernels for 13%

profile of v9, /device:TPU:1, one launch (start us, length us, event | category | flops | bytes accessed | tf_op | source)
XLA Modules:
  0.0 69.6 jit_solution(17443632030772846684)
XLA Ops:
  0.6 2.7 %prepare.1 = (bf16[8,3072]{1,0:T(8,128)(2,1)S(1)}, bf16[4,8,256]{2,1,0:T(8,128)(2,1)S(1)}, bf16[12,512,384]{2,1,0:T(8,128)(2,1)S(1)}) custom-call(s32[3]{0:T(128)} %order_hbm.1, s32[1,3072]{1,0:T(1,128)} %bitcast.8, f32[2,3072]{1,0:T(2,128)} %lm_hbm.1, bf16[2,1024]{1,0:T(2,128)(2,1)} %uv_ref.1, bf16[2,3072,128]{2,1,0:T(8,128)(2,1)} %spec_hbm.1), custom_call_target="tpu_custom_call" | custom-call | tf_op jit(solution)/shard_map/prepare/pallas_call | solution.py:127
  3.3 5.6 %predict.3 = (bf16[3,256,128]{2,1,0:T(8,128)(2,1)S(1)}, bf16[3,256,128]{2,1,0:T(8,128)(2,1)S(1)}) custom-call(bf16[4,8,256]{2,1,0:T(8,128)(2,1)S(1)} %get-tuple-element.20.refs_0_, bf16[8,3072]{1,0:T(8,128)(2,1)S(1)} %get-tuple-element.21.refs_1_, bf16[12,512,384]{2,1,0:T(8,128)(2,1)S(1)} %get-tuple-element.22.refs_2_), custom_call_target="tpu_custom_call" | custom-call | flops 4831838208 | bytes 5111808 | tf_op jit(solution)/shard_map/predict/pallas_call | solution.py:187
  8.9 2.1 %collective-permute-start.1 = (bf16[3,256,128]{2,1,0:T(8,128)(2,1)S(1)}, bf16[3,256,128]{2,1,0:T(8,128)(2,1)S(1)}, u32[]{:S(2)}, u32[]{:S(2)}) collective-permute-start(bf16[3,256,128]{2,1,0:T(8,128)(2,1)S(1)} %get-tuple-element.28), channel_id=1, source_target_pairs={{0,128},{64,192},{128,0},{192,64},{1,129},{65,193},{129,1},{193,65... | collective-permute-start | bytes 589832 | tf_op jit(solution)/shard_map/ppermute | solution.py:449
  11.1 3.1 %collective-permute-start.2 = (bf16[3,256,128]{2,1,0:T(8,128)(2,1)S(1)}, bf16[3,256,128]{2,1,0:T(8,128)(2,1)S(1)}, u32[]{:S(2)}, u32[]{:S(2)}) collective-permute-start(bf16[3,256,128]{2,1,0:T(8,128)(2,1)S(1)} %get-tuple-element.29), channel_id=1, source_target_pairs={{0,192},{64,128},{128,64},{192,0},{1,193},{65,129},{129,65},{193,1... | collective-permute-start | bytes 589832 | tf_op jit(solution)/shard_map/ppermute | solution.py:449
  14.2 5.6 %predict.2 = (bf16[3,256,128]{2,1,0:T(8,128)(2,1)S(1)}, bf16[3,256,128]{2,1,0:T(8,128)(2,1)S(1)}) custom-call(bf16[4,8,256]{2,1,0:T(8,128)(2,1)S(1)} %get-tuple-element.20.refs_0_, bf16[8,3072]{1,0:T(8,128)(2,1)S(1)} %get-tuple-element.21.refs_1_, bf16[12,512,384]{2,1,0:T(8,128)(2,1)S(1)} %get-tuple-element.22.refs_2_), custom_call_target="tpu_custom_call" | custom-call | flops 4831838208 | bytes 5111808 | tf_op jit(solution)/shard_map/predict/pallas_call | solution.py:187
  19.9 1.6 %label.1 = (bf16[64,40,128]{2,1,0:T(8,128)(2,1)S(1)}, s32[32]{0:T(128)S(1)}) custom-call(s32[32]{0:T(128)S(1)} %bitcast.5, s32[32,1]{1,0:T(8,128)S(1)} %copy.10.tile_ref, bf16[2,1024]{1,0:T(2,128)(2,1)S(1)} %copy-done.1), custom_call_target="tpu_custom_call" | custom-call | tf_op jit(solution)/shard_map/label/pallas_call | solution.py:332
  21.6 1.7 %peel.1 = (bf16[256,128]{1,0:T(8,128)(2,1)S(1)}, bf16[8,16,128]{2,1,0:T(8,128)(2,1)S(1)}, bf16[8,16,128]{2,1,0:T(8,128)(2,1)S(1)}, bf16[8,16,128]{2,1,0:T(8,128)(2,1)S(1)}, bf16[8,16,128]{2,1,0:T(8,128)(2,1)S(1)}) custom-call(bf16[1024,128]{1,0:T(8,128)(2,1)S(1)} %copy-done, f32[1,128]{1,0:T(1,128)S(1)} %bitcast.7, ...), custom_call_target="tpu_custom_call" | custom-call | tf_op jit(solution)/shard_map/peel/pallas_call | solution.py:276
  23.3 0.6 collective-permute-start.3
  23.9 1.7 %collective-permute-start.5 = (bf16[8,16,128]{2,1,0:T(8,128)(2,1)S(1)}, bf16[8,16,128]{2,1,0:T(8,128)(2,1)S(1)}, u32[]{:S(2)}, u32[]{:S(2)}) collective-permute-start(bf16[8,16,128]{2,1,0:T(8,128)(2,1)S(1)} %get-tuple-element.34), channel_id=1, source_target_pairs={{0,192},{64,128},{128,64},{192,0},{1,193},{65,129},{129,65},{193,1... | collective-permute-start | bytes 98312 | tf_op jit(solution)/shard_map/ppermute | solution.py:449
  25.6 1.0 %collective-permute-done.4.r2_ref = bf16[8,16,128]{2,1,0:T(8,128)(2,1)S(1)} collective-permute-done((bf16[8,16,128]{2,1,0:T(8,128)(2,1)S(1)}, bf16[8,16,128]{2,1,0:T(8,128)(2,1)S(1)}, u32[]{:S(2)}, u32[]{:S(2)}) %collective-permute-start.4) | collective-permute-done | bytes 32800 | tf_op jit(solution)/shard_map/ppermute | solution.py:449
  26.6 1.2 %collective-permute-done.5.r3_ref = bf16[8,16,128]{2,1,0:T(8,128)(2,1)S(1)} collective-permute-done((bf16[8,16,128]{2,1,0:T(8,128)(2,1)S(1)}, bf16[8,16,128]{2,1,0:T(8,128)(2,1)S(1)}, u32[]{:S(2)}, u32[]{:S(2)}) %collective-permute-start.5) | collective-permute-done | bytes 32800 | tf_op jit(solution)/shard_map/ppermute | solution.py:449
  27.8 1.5 %pack.1 = bf16[64,40,128]{2,1,0:T(8,128)(2,1)} custom-call(s32[32]{0:T(128)S(1)} %bitcast.6, s32[32]{0:T(128)S(1)} %get-tuple-element.25.slot_ref, bf16[8,16,128]{2,1,0:T(8,128)(2,1)S(1)} %get-tuple-element.31.r0_ref, bf16[8,16,128]{2,1,0:T(8,128)(2,1)S(1)} %collective-permute-done.3.r1_ref, bf16[8,16,128]{2,1,0:T(8,128)(2,1)S(1)} %collective-permute-done.4.r2_ref, ...), custom_call_target="tpu_custom_call" | custom-call | tf_op jit(solution)/shard_map/pack/pallas_call | solution.py:357
  29.3 13.9 %all-to-all-start = ((bf16[64,40,128]{2,1,0:T(8,128)(2,1)}), bf16[64,40,128]{2,1,0:T(8,128)(2,1)S(1)}, u32[]{:S(2)}, u32[]{:S(2)}) async-start(bf16[64,40,128]{2,1,0:T(8,128)(2,1)} %pack.1), calls=%async_computation | async-start | bytes 1310720 | tf_op jit(solution)/shard_map/all_to_all | solution.py:465
  43.3 0.6 collective-permute-start.8
  43.9 1.5 %collective-permute-start.7 = (bf16[256,128]{1,0:T(8,128)(2,1)S(1)}, bf16[256,128]{1,0:T(8,128)(2,1)S(1)}, u32[]{:S(2)}, u32[]{:S(2)}) collective-permute-start(bf16[256,128]{1,0:T(8,128)(2,1)S(1)} %get-tuple-element.36.r0_ref), channel_id=1, source_target_pairs={{0,128},{64,192},{128,0},{192,64},{1,129},{65,193},{129,1},{193,65... | collective-permute-start | bytes 196616 | tf_op jit(solution)/shard_map/ppermute | solution.py:449
  45.4 0.1 collective-permute-start.6
  45.5 3.7 %collective-permute-done.8.r3_ref = bf16[256,128]{1,0:T(8,128)(2,1)S(1)} collective-permute-done((bf16[256,128]{1,0:T(8,128)(2,1)S(1)}, bf16[256,128]{1,0:T(8,128)(2,1)S(1)}, u32[]{:S(2)}, u32[]{:S(2)}) %collective-permute-start.8) | collective-permute-done | bytes 65568 | tf_op jit(solution)/shard_map/ppermute | solution.py:449
  49.2 2.7 %collective-permute-done.7.r2_ref = bf16[256,128]{1,0:T(8,128)(2,1)S(1)} collective-permute-done((bf16[256,128]{1,0:T(8,128)(2,1)S(1)}, bf16[256,128]{1,0:T(8,128)(2,1)S(1)}, u32[]{:S(2)}, u32[]{:S(2)}) %collective-permute-start.7) | collective-permute-done | bytes 65568 | tf_op jit(solution)/shard_map/ppermute | solution.py:449
  51.8 0.7 %join.1 = bf16[1024,128]{1,0:T(8,128)(2,1)} custom-call(bf16[256,128]{1,0:T(8,128)(2,1)S(1)} %get-tuple-element.36.r0_ref, bf16[256,128]{1,0:T(8,128)(2,1)S(1)} %collective-permute-done.6.r1_ref, bf16[256,128]{1,0:T(8,128)(2,1)S(1)} %collective-permute-done.7.r2_ref, bf16[256,128]{1,0:T(8,128)(2,1)S(1)} %collective-permute-done.8.r3_ref), custom_call_target="tpu_custom_call" | custom-call | tf_op jit(solution)/shard_map/join/pallas_call | solution.py:375
  52.6 10.5 %all-to-all-done.refs_0_ = bf16[64,40,128]{2,1,0:T(8,128)(2,1)S(1)} async-done(((bf16[64,40,128]{2,1,0:T(8,128)(2,1)}), bf16[64,40,128]{2,1,0:T(8,128)(2,1)S(1)}, u32[]{:S(2)}, u32[]{:S(2)}) %all-to-all-start) | async-done | bytes 655392 | tf_op jit(solution)/shard_map/all_to_all | solution.py:465
  63.1 1.3 %grid.3 = f32[2,256,128]{2,1,0:T(8,128)S(1)} custom-call(bf16[64,40,128]{2,1,0:T(8,128)(2,1)S(1)} %all-to-all-done.refs_0_), custom_call_target="tpu_custom_call" | custom-call | flops 2000000000 | bytes 1000000 | tf_op jit(solution)/shard_map/grid/pallas_call | solution.py:429
  64.4 3.2 %collective-permute-start.9 = (f32[2,256,128]{2,1,0:T(8,128)S(1)}, f32[2,256,128]{2,1,0:T(8,128)S(1)}, u32[]{:S(2)}, u32[]{:S(2)}) collective-permute-start(f32[2,256,128]{2,1,0:T(8,128)S(1)} %grid.3), channel_id=1, source_target_pairs={{0,64},{64,0},{128,192},{192,128},{1,65},{65,1},{129,193},{193,129... | collective-permute-start | bytes 786440 | tf_op jit(solution)/shard_map/ppermute | solution.py:449
  67.5 1.3 %grid.2 = f32[2,256,128]{2,1,0:T(8,128)S(1)} custom-call(bf16[64,40,128]{2,1,0:T(8,128)(2,1)S(1)} %all-to-all-done.refs_0_), custom_call_target="tpu_custom_call" | custom-call | flops 2000000000 | bytes 1000000 | tf_op jit(solution)/shard_map/grid/pallas_call | solution.py:429
  68.8 0.7 %add_bitcast_fusion = f32[1,2,256,128]{3,2,1,0:T(8,128)} fusion(f32[2,256,128]{2,1,0:T(8,128)S(1)} %grid.2, f32[2,256,128]{2,1,0:T(8,128)S(1)} %collective-permute-done.9), kind=kLoop, calls=%fused_computation | loop fusion | flops 65536 | bytes 786432 | tf_op jit(solution)/shard_map/broadcast_in_dim | solution.py:471
  (17 shorter events, 0.2 us)
Async XLA Ops:
  8.9 12.6 %collective-permute-start.1 = (bf16[3,256,128]{2,1,0:T(8,128)(2,1)S(1)}, bf16[3,256,128]{2,1,0:T(8,128)(2,1)S(1)}, u32[]{:S(2)}, u32[]{:S(2)}) collective-permute-start(bf16[3,256,128]{2,1,0:T(8,128)(2,1)S(1)} %get-tuple-element.28), channel_id=1, source_target_pairs={{0,128},{64,192},{128,0},{192,64},{1,129},{65,193},{129,1},{193,65... | collective-permute-start | bytes 589832 | tf_op jit(solution)/shard_map/ppermute | solution.py:449
  11.0 8.8 %copy-start.2 = (s32[32,1]{0,1:T(1,128)S(1)}, s32[32,1]{0,1:T(1,128)}, u32[]{:S(2)}) copy-start(s32[32,1]{0,1:T(1,128)} %param.15) | copy-start | bytes 388
  11.0 8.9 %copy-start.1 = (bf16[2,1024]{1,0:T(2,128)(2,1)S(1)}, bf16[2,1024]{1,0:T(2,128)(2,1)}, u32[]{:S(2)}) copy-start(bf16[2,1024]{1,0:T(2,128)(2,1)} %uv_ref.1) | copy-start | bytes 12292
  11.0 10.5 %copy-start = (bf16[1024,128]{1,0:T(8,128)(2,1)S(1)}, bf16[1024,128]{1,0:T(8,128)(2,1)}, u32[]{:S(2)}) copy-start(bf16[1024,128]{1,0:T(8,128)(2,1)} %vis_ref) | copy-start | bytes 786436
  11.0 10.5 %copy-start.3 = (f32[128]{0:T(128)S(1)}, f32[128]{0:T(128)}, u32[]{:S(2)}) copy-start(f32[128]{0:T(128)} %param.12) | copy-start | bytes 1540
  11.1 10.5 %collective-permute-start.2 = (bf16[3,256,128]{2,1,0:T(8,128)(2,1)S(1)}, bf16[3,256,128]{2,1,0:T(8,128)(2,1)S(1)}, u32[]{:S(2)}, u32[]{:S(2)}) collective-permute-start(bf16[3,256,128]{2,1,0:T(8,128)(2,1)S(1)} %get-tuple-element.29), channel_id=1, source_target_pairs={{0,192},{64,128},{128,64},{192,0},{1,193},{65,129},{129,65},{193,1... | collective-permute-start | bytes 589832 | tf_op jit(solution)/shard_map/ppermute | solution.py:449
  19.7 1.8 %collective-permute-start = (bf16[3,256,128]{2,1,0:T(8,128)(2,1)S(1)}, bf16[3,256,128]{2,1,0:T(8,128)(2,1)S(1)}, u32[]{:S(2)}, u32[]{:S(2)}) collective-permute-start(bf16[3,256,128]{2,1,0:T(8,128)(2,1)S(1)} %get-tuple-element.27), channel_id=1, source_target_pairs={{0,64},{64,0},{128,192},{192,128},{1,65},{65,1},{129,193},{193,129... | collective-permute-start | bytes 589832 | tf_op jit(solution)/shard_map/ppermute | solution.py:449
  23.3 2.3 %collective-permute-start.3 = (bf16[8,16,128]{2,1,0:T(8,128)(2,1)S(1)}, bf16[8,16,128]{2,1,0:T(8,128)(2,1)S(1)}, u32[]{:S(2)}, u32[]{:S(2)}) collective-permute-start(bf16[8,16,128]{2,1,0:T(8,128)(2,1)S(1)} %get-tuple-element.32), channel_id=1, source_target_pairs={{0,64},{64,0},{128,192},{192,128},{1,65},{65,1},{129,193},{193,129... | collective-permute-start | bytes 98312 | tf_op jit(solution)/shard_map/ppermute | solution.py:449
  23.9 2.8 %collective-permute-start.4 = (bf16[8,16,128]{2,1,0:T(8,128)(2,1)S(1)}, bf16[8,16,128]{2,1,0:T(8,128)(2,1)S(1)}, u32[]{:S(2)}, u32[]{:S(2)}) collective-permute-start(bf16[8,16,128]{2,1,0:T(8,128)(2,1)S(1)} %get-tuple-element.33), channel_id=1, source_target_pairs={{0,128},{64,192},{128,0},{192,64},{1,129},{65,193},{129,1},{193,65... | collective-permute-start | bytes 98312 | tf_op jit(solution)/shard_map/ppermute | solution.py:449
  23.9 4.0 %collective-permute-start.5 = (bf16[8,16,128]{2,1,0:T(8,128)(2,1)S(1)}, bf16[8,16,128]{2,1,0:T(8,128)(2,1)S(1)}, u32[]{:S(2)}, u32[]{:S(2)}) collective-permute-start(bf16[8,16,128]{2,1,0:T(8,128)(2,1)S(1)} %get-tuple-element.34), channel_id=1, source_target_pairs={{0,192},{64,128},{128,64},{192,0},{1,193},{65,129},{129,65},{193,1... | collective-permute-start | bytes 98312 | tf_op jit(solution)/shard_map/ppermute | solution.py:449
  29.3 33.8 %all-to-all-start = ((bf16[64,40,128]{2,1,0:T(8,128)(2,1)}), bf16[64,40,128]{2,1,0:T(8,128)(2,1)S(1)}, u32[]{:S(2)}, u32[]{:S(2)}) async-start(bf16[64,40,128]{2,1,0:T(8,128)(2,1)} %pack.1), calls=%async_computation | async-start | bytes 1310720 | tf_op jit(solution)/shard_map/all_to_all | solution.py:465
  43.3 5.9 %collective-permute-start.8 = (bf16[256,128]{1,0:T(8,128)(2,1)S(1)}, bf16[256,128]{1,0:T(8,128)(2,1)S(1)}, u32[]{:S(2)}, u32[]{:S(2)}) collective-permute-start(bf16[256,128]{1,0:T(8,128)(2,1)S(1)} %get-tuple-element.36.r0_ref), channel_id=1, source_target_pairs={{0,192},{64,128},{128,64},{192,0},{1,193},{65,129},{129,65},{193,1... | collective-permute-start | bytes 196616 | tf_op jit(solution)/shard_map/ppermute | solution.py:449
  43.9 8.0 %collective-permute-start.7 = (bf16[256,128]{1,0:T(8,128)(2,1)S(1)}, bf16[256,128]{1,0:T(8,128)(2,1)S(1)}, u32[]{:S(2)}, u32[]{:S(2)}) collective-permute-start(bf16[256,128]{1,0:T(8,128)(2,1)S(1)} %get-tuple-element.36.r0_ref), channel_id=1, source_target_pairs={{0,128},{64,192},{128,0},{192,64},{1,129},{65,193},{129,1},{193,65... | collective-permute-start | bytes 196616 | tf_op jit(solution)/shard_map/ppermute | solution.py:449
  45.4 6.5 %collective-permute-start.6 = (bf16[256,128]{1,0:T(8,128)(2,1)S(1)}, bf16[256,128]{1,0:T(8,128)(2,1)S(1)}, u32[]{:S(2)}, u32[]{:S(2)}) collective-permute-start(bf16[256,128]{1,0:T(8,128)(2,1)S(1)} %get-tuple-element.36.r0_ref), channel_id=1, source_target_pairs={{0,64},{64,0},{128,192},{192,128},{1,65},{65,1},{129,193},{193,129... | collective-permute-start | bytes 196616 | tf_op jit(solution)/shard_map/ppermute | solution.py:449
  64.4 4.5 %collective-permute-start.9 = (f32[2,256,128]{2,1,0:T(8,128)S(1)}, f32[2,256,128]{2,1,0:T(8,128)S(1)}, u32[]{:S(2)}, u32[]{:S(2)}) collective-permute-start(f32[2,256,128]{2,1,0:T(8,128)S(1)} %grid.3), channel_id=1, source_target_pairs={{0,64},{64,0},{128,192},{192,128},{1,65},{65,1},{129,193},{193,129... | collective-permute-start | bytes 786440 | tf_op jit(solution)/shard_map/ppermute | solution.py:449
